TPU v7x, 32 devices: a whole 2x2x4 slice. The times are simulated.
32 devices in a mesh: gx: 4 (over z), gy: 8 (over y, x, core).
Axes of the slice: x: 2, y: 2, z: 4, core: 2. Of those that a mesh axis runs over, the one named last changes fastest.
Arguments:
- media: bfloat16 [16384, 1536], P(('gx', 'gy')), may hold values from -6 to 6
- latents: bfloat16 [2048, 1536], P(('gx', 'gy')), may hold values from -6 to 6
- frame_counts: int32 [8, 4], replicated, may hold values from 1 to 8, 16 in all within a row
- time_index: int32 [128], P(('gx', 'gy')), may hold values from 0 to 7
- valid: int32 [16384], P(('gx', 'gy')), may hold values from 0 to 1
- time_table: bfloat16 [8, 1536], P(None, ('gx', 'gy')), may hold values from -3 to 3
- media_gain: bfloat16 [1536], P(('gx', 'gy')), may hold values from 0.5 to 1.5
- latent_gain: bfloat16 [1536], P(('gx', 'gy')), may hold values from 0.5 to 1.5
- ffn_gain: bfloat16 [1536], P(('gx', 'gy')), may hold values from 0.5 to 1.5
- w_query: bfloat16 [1536, 1536], P(('gx', 'gy')), may hold values from -0.3125 to 0.3125
- w_key: bfloat16 [1536, 1536], P(('gx', 'gy')), may hold values from -0.15625 to 0.15625
- w_value: bfloat16 [1536, 1536], P(('gx', 'gy')), may hold values from -0.15625 to 0.15625
- w_out: bfloat16 [1536, 1536], P(('gx', 'gy')), may hold values from -0.625 to 0.625
- w_up: bfloat16 [1536, 6144], P(('gx', 'gy')), may hold values from -0.15625 to 0.15625
- w_down: bfloat16 [6144, 1536], P(('gx', 'gy')), may hold values from -0.078125 to 0.078125
- cotangent: bfloat16 [2048, 1536], P(('gx', 'gy')), may hold values from -6 to 6
Outputs:
- new_latents: bfloat16 [2048, 1536], P(('gx', 'gy'))
- media_grad: float32 [16384, 1536], P(('gx', 'gy'))
- latents_grad: float32 [2048, 1536], P(('gx', 'gy'))
- time_table_grad: float32 [8, 1536], P(None, ('gx', 'gy'))
- media_gain_grad: float32 [1536], P(('gx', 'gy'))
- latent_gain_grad: float32 [1536], P(('gx', 'gy'))
- feedforward_gain_gradient: float32 [1536], P(('gx', 'gy'))
- w_query_grad: float32 [1536, 1536], P(('gx', 'gy'))
- w_key_grad: float32 [1536, 1536], P(('gx', 'gy'))
- w_value_grad: float32 [1536, 1536], P(('gx', 'gy'))
- w_out_grad: float32 [1536, 1536], P(('gx', 'gy'))
- w_up_grad: float32 [1536, 6144], P(('gx', 'gy'))
- w_down_grad: float32 [6144, 1536], P(('gx', 'gy'))
Inputs may be any that keep to these rules, and one draw needn't show every extreme that they name: `frame_counts`: entry (g, j) counts the frames of item j times the number of rows plus g, which lie in order of j; each row sums to 4 times its number of entries and holds one entry of exactly 8.
All inputs are finite; a program needn't handle non-finite values.
Results may differ from a plain program's by a relative error of at most 0.015.
Values may be sent and summed in bfloat16 or wider, within the bound.
A program may use at most 448 MiB of HBM per device.

v0:
```python
from functools import partial

import jax
import jax.numpy as jnp
from jax import lax
from jax.sharding import PartitionSpec as P

H = 16


ENTROPY_WEIGHT = 4.0
NORM_STABILIZER = 1e-05


def layer_norm(row_block, gain_row):
    row_mean = jnp.mean(row_block, axis=-1, keepdims=True)
    centred = row_block - row_mean
    variance = jnp.mean(centred * centred, axis=-1, keepdims=True)
    return centred * lax.rsqrt(variance + NORM_STABILIZER) * gain_row


def product(left_side, right_side):
    return jnp.dot(left_side, right_side, preferred_element_type=jnp.float32)


def inner_first(left_side, right_side):
    return lax.dot_general(
        left_side, right_side, (((0,), (0,)), ((), ())), preferred_element_type=jnp.float32
    )


def inner_last(left_side, right_side):
    return lax.dot_general(
        left_side, right_side, (((1,), (1,)), ((), ())), preferred_element_type=jnp.float32
    )


def collect(onehot_rows, value_rows):
    return lax.dot_general(
        onehot_rows,
        value_rows,
        (((0,), (0,)), ((), ())),
        precision=lax.Precision.HIGHEST,
        preferred_element_type=jnp.float32,
    )


def per_device(
    media,
    latents,
    frame_counts,
    time_index,
    valid,
    time_table,
    media_gain,
    latent_gain,
    ffn_gain,
    w_query,
    w_key,
    w_value,
    w_out,
    w_up,
    w_down,
    cotangent,
):
    frames = time_index.shape[0]
    patches = valid.shape[0] // frames
    latent_rows = latents.shape[0]
    model_width = latents.shape[1]
    head_size = model_width // H
    score_scale = head_size ** (-0.5)
    across = lax.axis_size("gx")
    column = lax.axis_index("gx")
    row_index = lax.axis_index("gy")
    frame_ends = jnp.cumsum(frame_counts[row_index])
    position = column * frames + jnp.arange(frames, dtype=jnp.int32)
    item_index = jnp.sum((frame_ends[None, :] <= position[:, None]).astype(jnp.int32), axis=1)
    item_onehot = (item_index[:, None] == jnp.arange(across, dtype=jnp.int32)[None, :]).astype(
        jnp.float32
    )
    (
        full_query,
        full_key,
        full_value,
        full_out,
        full_up,
        full_down,
        full_media_gain,
        full_latent_gain,
        full_ffn_gain,
        full_time,
    ) = (
        lax.all_gather(w_query, ("gx", "gy"), axis=0, tiled=True),
        lax.all_gather(w_key, ("gx", "gy"), axis=0, tiled=True),
        lax.all_gather(w_value, ("gx", "gy"), axis=0, tiled=True),
        lax.all_gather(w_out, ("gx", "gy"), axis=0, tiled=True),
        lax.all_gather(w_up, ("gx", "gy"), axis=0, tiled=True),
        lax.all_gather(w_down, ("gx", "gy"), axis=0, tiled=True),
        lax.all_gather(media_gain, ("gx", "gy"), axis=0, tiled=True),
        lax.all_gather(latent_gain, ("gx", "gy"), axis=0, tiled=True),
        lax.all_gather(ffn_gain, ("gx", "gy"), axis=0, tiled=True),
        lax.all_gather(time_table, ("gx", "gy"), axis=1, tiled=True),
    )
    time_onehot = (
        time_index[:, None] == jnp.arange(full_time.shape[0], dtype=jnp.int32)[None, :]
    ).astype(jnp.float32)
    time_rows = product(time_onehot.astype(jnp.bfloat16), full_time)
    media_in = (
        media.astype(jnp.float32).reshape(frames, patches, model_width) + time_rows[:, None, :]
    ).reshape(-1, model_width)
    media_normed = layer_norm(media_in, full_media_gain.astype(jnp.float32)).astype(jnp.bfloat16)
    key_heads = (
        product(media_normed, full_key).astype(jnp.bfloat16).reshape(frames, patches, H, head_size)
    )
    value_heads = (
        product(media_normed, full_value)
        .astype(jnp.bfloat16)
        .reshape(frames, patches, H, head_size)
    )
    latent_in = latents.astype(jnp.float32)
    latent_normed = layer_norm(latent_in, full_latent_gain.astype(jnp.float32)).astype(jnp.bfloat16)
    own_query = product(latent_normed, full_query).astype(jnp.bfloat16)
    own_key = product(latent_normed, full_key).astype(jnp.bfloat16)
    own_value = product(latent_normed, full_value).astype(jnp.bfloat16)
    valid_total = lax.psum(jnp.sum(valid.astype(jnp.float32)), ("gx", "gy"))
    coefficient = ENTROPY_WEIGHT * (valid.shape[0] * lax.axis_size(("gx", "gy"))) / valid_total
    query_table = lax.all_gather(own_query, "gx", axis=0, tiled=True)
    picked = query_table.reshape(-1, latent_rows, H, head_size)[item_index]
    media_score = (
        jnp.einsum("flhd,fphd->flhp", picked, key_heads, preferred_element_type=jnp.float32)
        * score_scale
    )
    valid_mask = valid.reshape(frames, 1, 1, patches) > 0
    media_expo = jnp.where(valid_mask, jnp.exp(media_score), 0.0)
    expo_low = media_expo.astype(jnp.bfloat16)
    media_total = jnp.sum(media_expo, axis=-1)
    media_moment = jnp.sum(media_expo * media_score, axis=-1)
    media_weighted = jnp.einsum(
        "flhp,fphd->flhd", expo_low, value_heads, preferred_element_type=jnp.float32
    )
    dense_weighted = collect(item_onehot, media_weighted.reshape(frames, -1)).reshape(
        -1, model_width
    )
    dense_total = collect(item_onehot, media_total.reshape(frames, -1)).reshape(-1, H)
    dense_moment = collect(item_onehot, media_moment.reshape(frames, -1)).reshape(-1, H)
    got_weighted, got_total, got_moment = (
        lax.psum_scatter(dense_weighted, "gx", scatter_dimension=0, tiled=True),
        lax.psum_scatter(dense_total, "gx", scatter_dimension=0, tiled=True),
        lax.psum_scatter(dense_moment, "gx", scatter_dimension=0, tiled=True),
    )
    query_head_count = own_query.reshape(latent_rows, H, head_size)
    latent_key_rows = own_key.reshape(latent_rows, H, head_size)
    latent_value_rows = own_value.reshape(latent_rows, H, head_size)
    latent_score = (
        jnp.einsum(
            "uer,zer->uez", query_head_count, latent_key_rows, preferred_element_type=jnp.float32
        )
        * score_scale
    )
    latent_expo = jnp.exp(latent_score)
    latent_reduced_precision = latent_expo.astype(jnp.bfloat16)
    weighted = got_weighted.reshape(latent_rows, H, head_size) + jnp.einsum(
        "nwr,rwb->nwb",
        latent_reduced_precision,
        latent_value_rows,
        preferred_element_type=jnp.float32,
    )
    totals = got_total + jnp.sum(latent_expo, axis=-1)
    moment = got_moment + jnp.sum(latent_expo * latent_score, axis=-1)
    attention = weighted / totals[..., None]
    attn_low = attention.reshape(latent_rows, model_width).astype(jnp.bfloat16)
    middle = latent_in + product(attn_low, full_out)
    ffn_normed = layer_norm(middle, full_ffn_gain.astype(jnp.float32)).astype(jnp.bfloat16)
    up_rows = product(ffn_normed, full_up)
    hidden = jax.nn.gelu(up_rows, approximate=False).astype(jnp.bfloat16)
    new_latents = (middle + product(hidden, full_down)).astype(jnp.bfloat16)
    (
        back_query,
        back_key,
        back_value,
        back_out,
        back_up,
        back_down,
        back_media_gain,
        back_latent_gain,
        back_ffn_gain,
    ) = (
        lax.all_gather(w_query, ("gx", "gy"), axis=0, tiled=True),
        lax.all_gather(w_key, ("gx", "gy"), axis=0, tiled=True),
        lax.all_gather(w_value, ("gx", "gy"), axis=0, tiled=True),
        lax.all_gather(w_out, ("gx", "gy"), axis=0, tiled=True),
        lax.all_gather(w_up, ("gx", "gy"), axis=0, tiled=True),
        lax.all_gather(w_down, ("gx", "gy"), axis=0, tiled=True),
        lax.all_gather(media_gain, ("gx", "gy"), axis=0, tiled=True),
        lax.all_gather(latent_gain, ("gx", "gy"), axis=0, tiled=True),
        lax.all_gather(ffn_gain, ("gx", "gy"), axis=0, tiled=True),
    )
    owned_latent, owned_attn, owned_ffn, owned_hidden = (
        lax.all_to_all(latent_normed, ("gx", "gy"), split_axis=1, concat_axis=0, tiled=True),
        lax.all_to_all(attn_low, ("gx", "gy"), split_axis=1, concat_axis=0, tiled=True),
        lax.all_to_all(ffn_normed, ("gx", "gy"), split_axis=1, concat_axis=0, tiled=True),
        lax.all_to_all(hidden, ("gx", "gy"), split_axis=1, concat_axis=0, tiled=True),
    )
    hidden_grad = inner_last(cotangent, back_down)
    gelu_pull = jax.vjp(partial(jax.nn.gelu, approximate=False), up_rows)[1]
    up_grad = gelu_pull(hidden_grad)[0].astype(jnp.bfloat16)
    ffn_normed_grad = inner_last(up_grad, back_up)
    ffn_pull = jax.vjp(layer_norm, middle, back_ffn_gain.astype(jnp.float32))[1]
    middle_part, grad_ffn_gain = ffn_pull(ffn_normed_grad)
    middle_grad = cotangent.astype(jnp.float32) + middle_part
    middle_low = middle_grad.astype(jnp.bfloat16)
    attn_grad = inner_last(middle_low, back_out).reshape(latent_rows, H, head_size)
    weighted_sum_gradient = (attn_grad / totals[..., None]).astype(jnp.bfloat16)
    slope_term = -coefficient / totals
    shift_term = (
        -jnp.sum(attn_grad * attention, axis=-1) / totals
        + coefficient * (1.0 / totals + moment / (totals * totals))
        + slope_term
    )
    latent_mix = jnp.einsum(
        "uer,zer->uez", weighted_sum_gradient, latent_value_rows, preferred_element_type=jnp.float32
    )
    latent_sgrad = latent_expo * (
        latent_mix + shift_term[..., None] + slope_term[..., None] * latent_score
    )
    latent_residual_gradient = (latent_sgrad * score_scale).astype(jnp.bfloat16)
    query_part = jnp.einsum(
        "nwr,rwb->nwb",
        latent_residual_gradient,
        latent_key_rows,
        preferred_element_type=jnp.float32,
    )
    own_key_grad = (
        jnp.einsum(
            "zry,zrj->yrj",
            latent_residual_gradient,
            query_head_count,
            preferred_element_type=jnp.float32,
        )
        .astype(jnp.bfloat16)
        .reshape(latent_rows, model_width)
    )
    own_value_grad = (
        jnp.einsum(
            "zry,zrj->yrj",
            latent_reduced_precision,
            weighted_sum_gradient,
            preferred_element_type=jnp.float32,
        )
        .astype(jnp.bfloat16)
        .reshape(latent_rows, model_width)
    )
    grad_table = lax.all_gather(
        weighted_sum_gradient.reshape(latent_rows, model_width), "gx", axis=0, tiled=True
    )
    shift_table, slope_table = (
        lax.all_gather(shift_term, "gx", axis=0, tiled=True),
        lax.all_gather(slope_term, "gx", axis=0, tiled=True),
    )
    picked_grad = grad_table.reshape(-1, latent_rows, H, head_size)[item_index]
    picked_shift = shift_table.reshape(-1, latent_rows, H)[item_index]
    picked_slope = slope_table.reshape(-1, latent_rows, H)[item_index]
    media_mix = jnp.einsum(
        "flhd,fphd->flhp", picked_grad, value_heads, preferred_element_type=jnp.float32
    )
    media_sgrad = media_expo * (
        media_mix + picked_shift[..., None] + picked_slope[..., None] * media_score
    )
    media_rgrad = (media_sgrad * score_scale).astype(jnp.bfloat16)
    query_terms = jnp.einsum(
        "flhp,fphd->flhd", media_rgrad, key_heads, preferred_element_type=jnp.float32
    )
    dense_query = collect(item_onehot, query_terms.reshape(frames, -1)).reshape(-1, model_width)
    got_query = lax.psum_scatter(
        dense_query.astype(jnp.bfloat16), "gx", scatter_dimension=0, tiled=True
    ).astype(jnp.float32)
    media_key_grad = (
        jnp.einsum("flhp,flhd->fphd", media_rgrad, picked, preferred_element_type=jnp.float32)
        .astype(jnp.bfloat16)
        .reshape(-1, model_width)
    )
    media_value_grad = (
        jnp.einsum("flhp,flhd->fphd", expo_low, picked_grad, preferred_element_type=jnp.float32)
        .astype(jnp.bfloat16)
        .reshape(-1, model_width)
    )
    grad_key = inner_first(media_normed, media_key_grad) + inner_first(latent_normed, own_key_grad)
    grad_value = inner_first(media_normed, media_value_grad) + inner_first(
        latent_normed, own_value_grad
    )
    media_normed_grad = inner_last(media_key_grad, back_key) + inner_last(
        media_value_grad, back_value
    )
    media_pull = jax.vjp(layer_norm, media_in, back_media_gain.astype(jnp.float32))[1]
    media_grad, grad_media_gain = media_pull(media_normed_grad)
    frame_sums = jnp.sum(media_grad.reshape(frames, patches, model_width), axis=1)
    grad_time = collect(time_onehot, frame_sums)
    query_grad = (
        (got_query.reshape(latent_rows, H, head_size) + query_part)
        .astype(jnp.bfloat16)
        .reshape(latent_rows, model_width)
    )
    latent_normed_grad = (
        inner_last(query_grad, back_query)
        + inner_last(own_key_grad, back_key)
        + inner_last(own_value_grad, back_value)
    )
    latent_pull = jax.vjp(layer_norm, latent_in, back_latent_gain.astype(jnp.float32))[1]
    latent_part, grad_latent_gain = latent_pull(latent_normed_grad)
    latents_grad = middle_grad + latent_part
    piece_query = lax.all_gather(query_grad, ("gx", "gy"), axis=0, tiled=True)
    piece_middle = lax.all_gather(middle_low, ("gx", "gy"), axis=0, tiled=True)
    piece_up = lax.all_gather(up_grad, ("gx", "gy"), axis=0, tiled=True)
    piece_cot = lax.all_gather(cotangent, ("gx", "gy"), axis=0, tiled=True)
    shard_query = inner_first(owned_latent, piece_query)
    shard_out = inner_first(owned_attn, piece_middle)
    shard_up = inner_first(owned_ffn, piece_up)
    shard_down = inner_first(owned_hidden, piece_cot)
    shard_grads = (
        lax.psum_scatter(grad_key, ("gx", "gy"), scatter_dimension=0, tiled=True),
        lax.psum_scatter(grad_value, ("gx", "gy"), scatter_dimension=0, tiled=True),
        lax.psum_scatter(grad_media_gain, ("gx", "gy"), scatter_dimension=0, tiled=True),
        lax.psum_scatter(grad_latent_gain, ("gx", "gy"), scatter_dimension=0, tiled=True),
        lax.psum_scatter(grad_ffn_gain, ("gx", "gy"), scatter_dimension=0, tiled=True),
        lax.psum_scatter(grad_time, ("gx", "gy"), scatter_dimension=1, tiled=True),
    )
    return (
        new_latents,
        media_grad,
        latents_grad,
        shard_grads[5],
        shard_grads[2],
        shard_grads[3],
        shard_grads[4],
        shard_query,
        shard_grads[0],
        shard_grads[1],
        shard_out,
        shard_up,
        shard_down,
    )


def solution(mesh):
    in_specs = (
        P(("gx", "gy"), None),
        P(("gx", "gy"), None),
        P(),
        P(("gx", "gy")),
        P(("gx", "gy")),
        P(None, ("gx", "gy")),
        P(("gx", "gy")),
        P(("gx", "gy")),
        P(("gx", "gy")),
        P(("gx", "gy"), None),
        P(("gx", "gy"), None),
        P(("gx", "gy"), None),
        P(("gx", "gy"), None),
        P(("gx", "gy"), None),
        P(("gx", "gy"), None),
        P(("gx", "gy"), None),
    )
    out_specs = (
        P(("gx", "gy"), None),
        P(("gx", "gy"), None),
        P(("gx", "gy"), None),
        P(None, ("gx", "gy")),
        P(("gx", "gy")),
        P(("gx", "gy")),
        P(("gx", "gy")),
        P(("gx", "gy"), None),
        P(("gx", "gy"), None),
        P(("gx", "gy"), None),
        P(("gx", "gy"), None),
        P(("gx", "gy"), None),
        P(("gx", "gy"), None),
    )
    return jax.shard_map(
        per_device, mesh=mesh, in_specs=in_specs, out_specs=out_specs, check_vma=False
    )
```

profile of v0, /device:TPU:0, one launch (start us, length us, event | category | flops | bytes accessed | tf_op | source)
XLA Modules:
  0.0 1510.0 jit_solution(1071463498415896200)
XLA Ops:
  12.0 42.5 %all-reduce.7 = (bf16[1536]{0:T(1024)(128)(2,1)S(1)}, bf16[1536]{0:T(1024)(128)(2,1)S(1)}, bf16[1536]{0:T(1024)(128)(2,1)S(1)}) all-reduce(bf16[1536]{0:T(1024)(128)(2,1)S(1)} %dynamic-update-slice, bf16[1536]{0:T(1024)(128)(2,1)S(1)} %dynamic-update-slice.1, ...), channel_id=1, replica_groups=mesh['gx'=4,'gy'=8] {'gx','gy'}, use_global_device_ids=true, to_apply=%add | all-reduce | flops 4608 | bytes 18432
  54.9 40.9 %all-gather = bf16[32,48,8]{1,2,0:T(8,128)(2,1)S(1)} all-gather(bf16[1,48,8]{1,2,0:T(8,128)(2,1)} %bitcast.226), channel_id=1, replica_groups=mesh['gx'=4,'gy'=8] {'gx','gy'}, dimensions={0}, use_global_device_ids=true | all-gather | bytes 25344 | tf_op jit(solution)/shard_map/all_gather | solution.py:102
  101.9 3.3 convolution_convert_fusion.5
  105.2 22.3 %all_gather.69 = bf16[256,1536]{1,0:T(8,128)(2,1)S(1)} all-gather(bf16[64,1536]{1,0:T(8,128)(2,1)S(1)} %convolution_convert_fusion.5), channel_id=1, replica_groups=mesh['gx'=4,'gy'=8] {'gx'}, dimensions={0}, use_global_device_ids=true | all-gather | bytes 983040 | tf_op jit(solution)/shard_map/all_gather | solution.py:127
  129.3 15.9 %all-gather.16.cloned.1.call-done = bf16[1536,1536]{1,0:T(8,128)(2,1)} async-done(((bf16[48,1536]{1,0:T(8,128)(2,1)}), bf16[1536,1536]{1,0:T(8,128)(2,1)}) %all-gather.16.cloned.1.call-update) | async-done | bytes 4718608 | tf_op jit(solution)/shard_map/all_gather | solution.py:94
  145.2 6.6 convolution_convert_fusion.1
  151.8 4.3 reshape.353
  156.1 4.5 copy.174
  162.6 3.6 multiply_reduce_fusion.3
  168.1 42.6 %all-gather.14.cloned.1.call-done = bf16[1536,1536]{1,0:T(8,128)(2,1)} async-done(((bf16[48,1536]{1,0:T(8,128)(2,1)}), bf16[1536,1536]{1,0:T(8,128)(2,1)}) %all-gather.14.cloned.1.call-update) | async-done | bytes 4718608 | tf_op jit(solution)/shard_map/all_gather | solution.py:95
  210.6 6.6 convolution_convert_fusion.2
  217.2 4.4 reshape.352
  221.6 4.5 copy.176
  226.3 3.3 convolution_bitcast_fusion.2
  232.5 4.3 reshape.275
  237.6 4.2 fusion.68
  241.8 3.7 reshape.276
  248.4 42.4 %psum.7 = f32[]{:T(128)} all-reduce(f32[]{:T(128)} %convert_reduce_fusion.1), channel_id=1, replica_groups=mesh['gx'=4,'gy'=8] {'gx','gy'}, use_global_device_ids=true, to_apply=%region_16.17 | all-reduce | flops 1 | bytes 8 | tf_op jit(solution)/shard_map/psum | solution.py:125
  292.4 3.3 convolution_convert_fusion.3
  296.6 4.0 convolution_convert_fusion.4
  316.1 42.1 %all-gather.20.cloned.1.call-done = bf16[1536,1536]{1,0:T(8,128)(2,1)} async-done(((bf16[48,1536]{1,0:T(8,128)(2,1)}), bf16[1536,1536]{1,0:T(8,128)(2,1)}) %all-gather.20.cloned.1.call-update) | async-done | bytes 4718608 | tf_op jit(solution)/shard_map/all_gather | solution.py:96
  358.2 3.5 fusion.91
  362.7 121.9 %all-gather.22.cloned.1.call-done = bf16[1536,6144]{1,0:T(8,128)(2,1)} async-done(((bf16[48,6144]{1,0:T(8,128)(2,1)}), bf16[1536,6144]{1,0:T(8,128)(2,1)}) %all-gather.22.cloned.1.call-update) | async-done | bytes 18874384 | tf_op jit(solution)/shard_map/all_gather | solution.py:97
  484.6 11.1 fusion.92
  495.7 114.6 %all-gather.24.cloned.1.call-done = bf16[6144,1536]{1,0:T(8,128)(2,1)} async-done(((bf16[192,1536]{1,0:T(8,128)(2,1)}), bf16[6144,1536]{1,0:T(8,128)(2,1)}) %all-gather.24.cloned.1.call-update) | async-done | bytes 18874384 | tf_op jit(solution)/shard_map/all_gather | solution.py:98
  610.4 13.1 add_convert_fusion
  623.5 13.3 multiply_reduce_fusion.5
  640.6 4.8 divide_convert_fusion.1
  645.3 18.7 %all_gather.74 = bf16[256,1536]{1,0:T(8,128)(2,1)} all-gather(bf16[64,1536]{1,0:T(8,128)(2,1)S(1)} %get-tuple-element.48), channel_id=1, replica_groups=mesh['gx'=4,'gy'=8] {'gx'}, dimensions={0}, use_global_device_ids=true | all-gather | bytes 983040 | tf_op jit(solution)/shard_map/all_gather | solution.py:253
  664.0 2.7 reshape.283
  666.8 2.9 gather_fusion.1
  678.2 13.1 all-gather.2
  692.6 13.1 all-gather.1
  706.4 3.8 fusion.7
  714.1 4.2 reshape.291
  718.3 4.1 convolution_convert_fusion
  728.3 5.9 fusion.16
  734.2 3.8 multiply_reduce_fusion
  752.4 4.1 fusion.11
  756.5 5.1 convolution_add_fusion
  763.2 4.6 fusion.14
  767.8 4.9 convolution_add_fusion.1
  773.9 3.9 all-to-all-start
  779.0 7.7 all-to-all-done
  786.7 2.7 all-to-all-start.1
  792.1 6.2 all-to-all-done.1
  798.3 2.9 all-to-all-start.2
  806.3 5.0 all-to-all-done.2
  815.9 10.4 fusion.3
  826.3 24.9 %reduce-scatter.26.cloned.1.call-done = f32[48,8]{1,0:T(8,128)} async-done(((f32[1536,8]{1,0:T(8,128)}), f32[48,8]{1,0:T(8,128)}) %reduce-scatter.26.cloned.1.call-update) | async-done | bytes 1552
  852.6 69.9 %all-gather.32.cloned.1.call-done = bf16[2048,1536]{1,0:T(8,128)(2,1)} async-done(((bf16[64,1536]{1,0:T(8,128)(2,1)}), bf16[2048,1536]{1,0:T(8,128)(2,1)}) %all-gather.32.cloned.1.call-update) | async-done | bytes 6291472 | tf_op jit(solution)/shard_map/all_gather | solution.py:314
  922.6 5.3 fusion.97
  927.8 3.9 fusion.93
  931.7 4.0 convolution_add_fusion.4
  935.8 4.1 fusion.55
  940.2 40.6 %all-reduce.6 = (f32[1536]{0:T(1024)S(1)}, f32[1536]{0:T(1024)S(1)}, f32[1536]{0:T(1024)S(1)}) all-reduce(f32[1536]{0:T(1024)S(1)} %get-tuple-element.13, f32[1536]{0:T(1024)S(1)} %get-tuple-element.19, f32[1536]{0:T(1024)S(1)} %get-tuple-element.17), channel_id=7, replica_groups=mesh['gx'=4,'gy'=8] {'gx','gy'}, use_global_device_ids=true, to_apply=%region_28.29.clone | all-reduce | flops 4608 | bytes 36864
  983.6 10.8 all-gather.28.cloned.1.call-done
  994.4 4.6 fusion.95
  999.0 66.1 %all-gather.26.cloned.1.call-done = bf16[2048,1536]{1,0:T(8,128)(2,1)} async-done(((bf16[64,1536]{1,0:T(8,128)(2,1)}), bf16[2048,1536]{1,0:T(8,128)(2,1)}) %all-gather.26.cloned.1.call-update) | async-done | bytes 6291472 | tf_op jit(solution)/shard_map/all_gather | solution.py:311
  1065.2 4.6 fusion.94
  1069.8 151.2 %all-gather.30.cloned.1.call-done = bf16[2048,6144]{1,0:T(8,128)(2,1)} async-done(((bf16[64,6144]{1,0:T(8,128)(2,1)}), bf16[2048,6144]{1,0:T(8,128)(2,1)}) %all-gather.30.cloned.1.call-update) | async-done | bytes 25165840 | tf_op jit(solution)/shard_map/all_gather | solution.py:313
  1221.1 11.5 fusion.96
  1232.5 128.6 %reduce-scatter.20.cloned.1.call-done = f32[48,1536]{1,0:T(8,128)} async-done(((f32[1536,1536]{1,0:T(8,128)}), f32[48,1536]{1,0:T(8,128)}) %reduce-scatter.20.cloned.1.call-update) | async-done | bytes 294928 | tf_op jit(solution)/shard_map/reduce_scatter | solution.py:321
  1361.1 142.1 %reduce-scatter.18.cloned.1.call-done = f32[48,1536]{1,0:T(8,128)} async-done(((f32[1536,1536]{1,0:T(8,128)}), f32[48,1536]{1,0:T(8,128)}) %reduce-scatter.18.cloned.1.call-update) | async-done | bytes 294928 | tf_op jit(solution)/shard_map/reduce_scatter | solution.py:320
  (247 shorter events, 100.6 us)
Async XLA Ops:
  7.2 47.3 %copy-start = (s32[8,4]{0,1:T(4,128)S(1)}, s32[8,4]{0,1:T(4,128)}, u32[]{:S(2)}) copy-start(s32[8,4]{0,1:T(4,128)} %param.18) | copy-start | bytes 388
  7.2 91.4 %copy-start.2 = (bf16[512,1536]{1,0:T(8,128)(2,1)S(1)}, bf16[512,1536]{1,0:T(8,128)(2,1)}, u32[]{:S(2)}) copy-start(bf16[512,1536]{1,0:T(8,128)(2,1)} %param.16) | copy-start | bytes 4718596
  7.2 94.7 %all-gather.18.cloned.1.call-start = ((), (), s32[]{:S(2)}) async-start(), calls=%async_computation.13 | async-start | bytes 4866048 | tf_op jit(solution)/shard_map/all_gather | solution.py:93
  7.9 137.3 %all-gather.16.cloned.1.call-start = ((), (), s32[]{:S(2)}) async-start(), calls=%async_computation.12 | async-start | bytes 4866048 | tf_op jit(solution)/shard_map/all_gather | solution.py:94
  8.7 201.9 %all-gather.14.cloned.1.call-start = ((), (), s32[]{:S(2)}) async-start(), calls=%async_computation.11 | async-start | bytes 4866048 | tf_op jit(solution)/shard_map/all_gather | solution.py:95
  9.4 295.1 %reduce-scatter.22.cloned.1.call-start = ((), (), s32[]{:S(2)}) async-start(), calls=%async_computation.25 | async-start | bytes 163840
  99.2 2.0 copy-start.3
  99.3 2.4 copy-start.27
  101.2 136.3 %copy-start.34 = (s32[4]{0:T(128)}, s32[4]{0:T(128)S(1)}, u32[]{:S(2)}) copy-start(s32[4]{0:T(128)S(1)} %convert_reduce_fusion.2) | copy-start | bytes 52
  101.3 565.5 %copy-start.26 = (s32[1024]{0:T(1024)}, s32[1024]{0:T(1024)S(1)}, u32[]{:S(2)}) copy-start(s32[1024]{0:T(1024)S(1)} %pad_clamp_fusion) | copy-start | bytes 12292
  101.7 3.5 copy-start.36
  101.7 3.5 copy-start.29
  101.7 568.0 %copy-start.31 = (pred[4,128]{1,0:T(4,128)(4,1)}, pred[4,128]{1,0:T(4,128)(4,1)S(1)}, u32[]{:S(2)}) copy-start(pred[4,128]{1,0:T(4,128)(4,1)S(1)} %compare_bitcast_fusion) | copy-start | bytes 1540
  167.5 141.6 %reduce-scatter.24.cloned.1.call-start = ((), (), s32[]{:S(2)}) async-start(), calls=%async_computation.26 | async-start | bytes 163840
  237.5 72.4 %reduce-scatter.14.cloned.1.call-start = ((), (), s32[]{:S(2)}) async-start(), calls=%async_computation.14 | async-start | bytes 1966080 | tf_op jit(solution)/shard_map/reduce_scatter | solution.py:147
  245.5 112.7 %all-gather.20.cloned.1.call-start = ((), (), s32[]{:S(2)}) async-start(), calls=%async_computation.15 | async-start | bytes 4866048 | tf_op jit(solution)/shard_map/all_gather | solution.py:96
  246.2 238.4 %all-gather.22.cloned.1.call-start = ((), (), s32[]{:S(2)}) async-start(), calls=%async_computation.16 | async-start | bytes 19464192 | tf_op jit(solution)/shard_map/all_gather | solution.py:97
  247.0 363.4 %all-gather.24.cloned.1.call-start = ((), (), s32[]{:S(2)}) async-start(), calls=%async_computation.17 | async-start | bytes 19464192 | tf_op jit(solution)/shard_map/all_gather | solution.py:98
  247.7 499.2 %reduce-scatter.16.cloned.1.call-start = ((), (), s32[]{:S(2)}) async-start(), calls=%async_computation.18 | async-start | bytes 983040 | tf_op jit(solution)/shard_map/reduce_scatter | solution.py:274
  296.6 5.9 copy-start.17
  304.5 7.4 copy-start.24
  314.3 0.7 copy-start.20
  638.1 0.7 copy-start.8
  638.1 7.2 copy-start.32
  706.4 3.8 copy-start.4
  710.2 1.3 copy-start.7
  714.1 4.2 copy-start.35
  725.1 126.1 %reduce-scatter.26.cloned.1.call-start = ((), (), s32[]{:S(2)}) async-start(), calls=%async_computation.27 | async-start | bytes 811008
  727.0 7.1 slice-start
  728.2 5.9 copy-start.16
  728.2 5.9 slice-start.1
  728.2 5.9 copy-start.5
  739.1 2.1 copy-start.38
  741.2 3.2 copy-start.10
  741.2 3.2 copy-start.25
  741.2 3.2 copy-start.28
  741.2 3.2 copy-start.39
  743.0 179.6 %all-gather.32.cloned.1.call-start = ((), (), s32[]{:S(2)}) async-start(), calls=%async_computation.24 | async-start | bytes 6488064 | tf_op jit(solution)/shard_map/all_gather | solution.py:314
  743.5 250.9 %all-gather.28.cloned.1.call-start = ((), (), s32[]{:S(2)}) async-start(), calls=%async_computation.22 | async-start | bytes 6488064 | tf_op jit(solution)/shard_map/all_gather | solution.py:312
  744.3 320.9 %all-gather.26.cloned.1.call-start = ((), (), s32[]{:S(2)}) async-start(), calls=%async_computation.19 | async-start | bytes 6488064 | tf_op jit(solution)/shard_map/all_gather | solution.py:311
  744.4 3.7 copy-start.19
  749.5 471.5 %all-gather.30.cloned.1.call-start = ((), (), s32[]{:S(2)}) async-start(), calls=%async_computation.23 | async-start | bytes 25952256 | tf_op jit(solution)/shard_map/all_gather | solution.py:313
  750.1 2.2 copy-start.6
  750.1 611.0 %reduce-scatter.20.cloned.1.call-start = ((), (), s32[]{:S(2)}) async-start(), calls=%async_computation.21 | async-start | bytes 9732096 | tf_op jit(solution)/shard_map/reduce_scatter | solution.py:321
  752.4 4.2 copy-start.12
  761.6 1.0 copy-start.18
  761.6 741.6 %reduce-scatter.18.cloned.1.call-start = ((), (), s32[]{:S(2)}) async-start(), calls=%async_computation.20 | async-start | bytes 9732096 | tf_op jit(solution)/shard_map/reduce_scatter | solution.py:320
  772.7 5.1 copy-start.21
  773.9 12.8 all-to-all-start
  779.0 11.9 copy-start.11
  786.7 11.6 all-to-all-start.1
  798.3 12.9 all-to-all-start.2
  811.3 111.3 %all-to-all-start.3 = ((bf16[64,32,192]{2,0,1:T(8,128)(2,1)}), bf16[64,32,192]{2,0,1:T(8,128)(2,1)S(1)}, u32[]{:S(2)}, u32[]{:S(2)}) async-start(bf16[64,32,192]{2,0,1:T(8,128)(2,1)} %copy.213), calls=%async_computation.7 | async-start | bytes 2097152 | tf_op jit(solution)/shard_map/all_to_all | solution.py:202
  922.6 5.3 copy-start.15
  931.7 4.0 copy-start.13
  935.7 4.1 copy-start.37
  935.7 4.1 copy-start.30
  935.7 46.8 %copy-start.9 = (f32[64,1536]{1,0:T(8,128)S(1)}, f32[64,1536]{1,0:T(8,128)}, u32[]{:S(2)}) copy-start(f32[64,1536]{1,0:T(8,128)} %copy-done.8) | copy-start | bytes 1179652
  935.7 46.8 %copy-start.14 = (bf16[64,1536]{1,0:T(8,128)(2,1)S(1)}, bf16[64,1536]{1,0:T(8,128)(2,1)}, u32[]{:S(2)}) copy-start(bf16[64,1536]{1,0:T(8,128)(2,1)} %param.31) | copy-start | bytes 589828
  935.8 46.8 %copy-start.33 = (f32[64]{0:T(128)S(1)}, f32[64]{0:T(128)}, u32[]{:S(2)}) copy-start(f32[64]{0:T(128)} %copy-done.32) | copy-start | bytes 772
  939.8 54.6 %copy-start.23 = (bf16[2048,48]{0,1:T(8,128)(2,1)S(1)}, bf16[2048,48]{0,1:T(8,128)(2,1)}, u32[]{:S(2)}) copy-start(bf16[2048,48]{0,1:T(8,128)(2,1)} %all_to_all.60) | copy-start | bytes 589828
  983.6 81.6 %copy-start.22 = (bf16[2048,48]{0,1:T(8,128)(2,1)S(1)}, bf16[2048,48]{0,1:T(8,128)(2,1)}, u32[]{:S(2)}) copy-start(bf16[2048,48]{0,1:T(8,128)(2,1)} %all_to_all.57) | copy-start | bytes 589828
  1221.1 282.1 %copy-start.1 = (s32[8,4]{0,1:T(4,128)S(1)}, s32[8,4]{0,1:T(4,128)}, u32[]{:S(2)}) copy-start(s32[8,4]{0,1:T(4,128)} %param.18) | copy-start | bytes 388
Sparse Core Ops, SparseCore 0:
  10.9 66.6 all-gather.17
  80.5 64.6 all-gather.15
  148.1 62.4 all-gather.13
  213.3 17.9 reduce-scatter.21
  237.6 17.9 reduce-scatter.23
  257.8 34.2 reduce-scatter.13
  295.1 63.0 all-gather.19
  361.1 123.4 all-gather.21
  487.5 122.8 all-gather.23
  725.2 21.6 reduce-scatter.15
  752.6 98.5 reduce-scatter.25
  853.9 68.5 all-gather.31
  925.4 68.9 all-gather.27
  997.1 68.0 all-gather.25
  1067.9 153.1 all-gather.29
  1227.4 133.6 reduce-scatter.19
  1368.4 134.7 reduce-scatter.17
where the time goes:
time: 1520 us; the launch traced here: 1510 us
  waiting for transfers between devices  958 us (63%)
  blocking collectives  234 us (15%)
  matrix products  181 us (12%)
  local copies, waits for them, and re-layouts  89.1 us (6%)
  other arithmetic  19.1 us (1%)
  between operations  15.9 us (1%)
    all_gather x1, waiting for transfers between devices, per_device(): piece_up = lax.all_gather(up_grad, ('gx', 'gy'), axis=0, tiled=True)  151 us
    reduce_scatter x1, waiting for transfers between devices, per_device(): lax.psum_scatter(grad_key, ('gx', 'gy'), scatter_dimension=0, tiled=True)  142 us
    reduce_scatter x1, waiting for transfers between devices, per_device(): lax.psum_scatter(grad_value, ('gx', 'gy'), scatter_dimension=0, tiled=True)  129 us
    all_gather x1, waiting for transfers between devices, per_device(): lax.all_gather(w_up, ('gx', 'gy'), axis=0, tiled=True)  122 us
    all_gather x1, waiting for transfers between devices, per_device(): lax.all_gather(w_down, ('gx', 'gy'), axis=0, tiled=True)  115 us
    unnamed x2, blocking collectives  83.1 us
    all_gather x1, waiting for transfers between devices, per_device(): piece_cot = lax.all_gather(cotangent, ('gx', 'gy'), axis=0, tiled=True)  69.9 us
    all_gather x1, waiting for transfers between devices, per_device(): piece_query = lax.all_gather(query_grad, ('gx', 'gy'), axis=0, tiled=True)  66.1 us
  transfers between devices with their start and end apart: 21, of which 16 were waited for; matrix products, arithmetic and copies ran while one was open for 14% of the time, Pallas kernels for 0%

commit v1 on v0

--- a/solution.py
+++ b/solution.py
@@ -3,6 +3,8 @@
 import jax
 import jax.numpy as jnp
 from jax import lax
+from jax.experimental import pallas as pl
+from jax.experimental.pallas import tpu as pltpu
 from jax.sharding import PartitionSpec as P
 
 H = 16
@@ -10,6 +12,406 @@
 
 ENTROPY_WEIGHT = 4.0
 NORM_STABILIZER = 1e-05
+AXES = ("gx", "gy")
+LINES = 4
+PLANE = 4
+HBM = pl.ANY
+BF16 = jnp.bfloat16
+F32 = jnp.float32
+
+
+def here():
+    z = lax.axis_index("gx")
+    g = lax.axis_index("gy")
+    return z, g, g // 2, g % 2
+
+
+def sibling(g):
+    return g + 1 - 2 * (g % 2)
+
+
+def along_x(g):
+    return g + 2 - 4 * ((g // 2) % 2)
+
+
+def along_y(g):
+    return (g + 4) % 8
+
+
+def turn(z, k):
+    return (z + k) % LINES
+
+
+def greet(devices):
+    barrier = pltpu.get_barrier_semaphore()
+    for device in devices:
+        pl.semaphore_signal(
+            barrier, inc=1, device_id=device, device_id_type=pl.DeviceIdType.MESH
+        )
+    pl.semaphore_wait(barrier, len(devices))
+
+
+def line_of(z, g):
+    return [(turn(z, k), g) for k in (1, 2, 3)]
+
+
+class Wires:
+    def __init__(self, send_sems, recv_sems):
+        self.send_sems, self.recv_sems, self.used, self.sent = send_sems, recv_sems, 0, []
+
+    def send(self, source, target, device):
+        n = self.used
+        self.used += 1
+        copy = pltpu.make_async_remote_copy(
+            src_ref=source,
+            dst_ref=target,
+            send_sem=self.send_sems.at[n],
+            recv_sem=self.recv_sems.at[n],
+            device_id=device,
+            device_id_type=pl.DeviceIdType.MESH,
+        )
+        copy.start()
+        self.sent.append(copy)
+        return copy
+
+    def drain(self):
+        for copy in self.sent:
+            copy.wait_send()
+
+
+class Spread:
+    def __init__(self, wires, shard, slot, half, whole):
+        self.wires, self.shard, self.slot, self.half, self.whole = wires, shard, slot, half, whole
+        self.z, self.g, _, _ = here()
+        self.zs = [turn(self.z, LINES - k) if k else self.z for k in range(LINES)]
+        self.line, self.x, self.y, self.dx, self.dy, self.sib = {}, {}, {}, {}, {}, []
+
+    def side(self, gy):
+        return (self.z, gy)
+
+    def to_sibling(self, source, where):
+        if self.whole:
+            self.sib.append(self.wires.send(source, where, self.side(sibling(self.g))))
+
+    def first(self):
+        own = self.slot(self.z, self.g)
+        for k in (1, 3, 2):
+            self.line[k] = self.wires.send(self.shard, own, (turn(self.z, k), self.g))
+        self.x[0] = self.wires.send(self.shard, own, self.side(along_x(self.g)))
+        self.y[0] = self.wires.send(self.shard, own, self.side(along_y(self.g)))
+        self.to_sibling(self.shard, own)
+
+    def column(self, k):
+        self.line[k].wait_recv()
+        held = self.slot(self.zs[k], self.g)
+        self.x[k] = self.wires.send(held, held, self.side(along_x(self.g)))
+        self.y[k] = self.wires.send(held, held, self.side(along_y(self.g)))
+        self.to_sibling(held, held)
+
+    def corner(self, k):
+        self.x[k].wait_recv()
+        held = self.slot(self.zs[k], along_x(self.g))
+        part = self.half(held, 0)
+        self.dy[k] = self.wires.send(part, part, self.side(along_y(self.g)))
+        self.to_sibling(held, held)
+        self.y[k].wait_recv()
+        held = self.slot(self.zs[k], along_y(self.g))
+        part = self.half(held, 1)
+        self.dx[k] = self.wires.send(part, part, self.side(along_x(self.g)))
+        self.to_sibling(held, held)
+
+    def last(self, k):
+        self.dy[k].wait_recv()
+        self.dx[k].wait_recv()
+        held = self.slot(self.zs[k], along_y(along_x(self.g)))
+        self.to_sibling(held, held)
+
+    def finish(self):
+        for copy in self.sib:
+            copy.wait_recv()
+
+
+def spread_all(flows):
+    for flow in flows:
+        flow.first()
+    for flow in flows:
+        flow.corner(0)
+    for k in (1, 3, 2):
+        for flow in flows:
+            flow.column(k)
+    for k in (1, 3, 2):
+        for flow in flows:
+            flow.corner(k)
+    for k in (0, 1, 3, 2):
+        for flow in flows:
+            flow.last(k)
+    for flow in flows:
+        flow.finish()
+
+
+def spread_sems(flows, whole):
+    return flows * (3 + 8 + 8 + (16 if whole else 0))
+
+
+def columns_half(ref, which):
+    width = ref.shape[-1] // 2
+    return ref.at[..., pl.ds(which * width, width)]
+
+
+def gather_kernel(count, small, whole, *refs):
+    shards, outs = refs[:count], refs[count : 2 * count]
+    send_sems, recv_sems, local_sems = refs[2 * count :]
+    z, g, chip, core = here()
+    others = line_of(z, g) + [(z, along_x(g)), (z, along_y(g))]
+    if whole:
+        others.append((z, sibling(g)))
+    greet(others)
+    wires = Wires(send_sems, recv_sems)
+
+    def slot_of(out):
+        if whole:
+            return lambda zz, gg: out.at[zz * 8 + gg]
+        return lambda zz, gg: out.at[zz * 4 + gg // 2]
+
+    def rows_half(ref, which):
+        rows = ref.shape[0] // 2
+        return ref.at[pl.ds(which * rows, rows)]
+
+    flows = [
+        Spread(wires, shards[n], slot_of(outs[n]), rows_half if n in small else columns_half, whole)
+        for n in range(count)
+    ]
+    kept = []
+    for n in range(count):
+        copy = pltpu.make_async_copy(shards[n], slot_of(outs[n])(z, g), local_sems.at[n])
+        copy.start()
+        kept.append(copy)
+    spread_all(flows)
+    for copy in kept:
+        copy.wait()
+    wires.drain()
+
+
+def gather(shards, whole, ident, small=()):
+    count = len(shards)
+    slots = 32 if whole else 16
+    sems = spread_sems(count, whole)
+    return pl.pallas_call(
+        partial(gather_kernel, count, small, whole),
+        out_shape=[jax.ShapeDtypeStruct((slots,) + s.shape, s.dtype) for s in shards],
+        in_specs=[pl.BlockSpec(memory_space=HBM)] * count,
+        out_specs=[pl.BlockSpec(memory_space=HBM)] * count,
+        scratch_shapes=[
+            pltpu.SemaphoreType.DMA((sems,)),
+            pltpu.SemaphoreType.DMA((sems,)),
+            pltpu.SemaphoreType.DMA((count,)),
+        ],
+        compiler_params=pltpu.CompilerParams(collective_id=ident, has_side_effects=True),
+        name="gather_%d" % ident,
+    )(*shards)
+
+
+def line_kernel(count, spread, *refs):
+    sources, outs = refs[:count], refs[count : 2 * count]
+    send_sems, recv_sems = refs[2 * count :]
+    z, g, _, _ = here()
+    greet(line_of(z, g))
+    wires = Wires(send_sems, recv_sems)
+    copies = []
+    for k in (2, 1, 3):
+        for source, out in zip(sources, outs):
+            there = turn(z, k)
+            piece = source if spread else source.at[there]
+            copies.append(wires.send(piece, out.at[z], (there, g)))
+    for source, out in zip(sources, outs):
+        out[z] = source[...] if spread else source[z]
+    for copy in copies:
+        copy.wait_recv()
+    wires.drain()
+
+
+def along_line(arrays, spread, ident):
+    count = len(arrays)
+    shapes = [((LINES,) + a.shape) if spread else a.shape for a in arrays]
+    return pl.pallas_call(
+        partial(line_kernel, count, spread),
+        out_shape=[jax.ShapeDtypeStruct(s, a.dtype) for s, a in zip(shapes, arrays)],
+        in_specs=[pl.BlockSpec(memory_space=pltpu.VMEM)] * count,
+        out_specs=[pl.BlockSpec(memory_space=pltpu.VMEM)] * count,
+        scratch_shapes=[
+            pltpu.SemaphoreType.DMA((3 * count,)),
+            pltpu.SemaphoreType.DMA((3 * count,)),
+        ],
+        compiler_params=pltpu.CompilerParams(collective_id=ident, has_side_effects=True),
+        name="line_%d" % ident,
+    )(*arrays)
+
+
+def add_slots(target, source, count):
+    @pl.loop(0, count)
+    def _(n):
+        target[n] = (target[n].astype(F32) + source[n].astype(F32)).astype(target.dtype)
+
+
+class Fold:
+    def __init__(self, wires, parts, keep, whole, scratch, out, local_sem):
+        self.wires, self.parts, self.whole, self.out = wires, parts, whole, out
+        self.held, self.from_sib, self.cx, self.cy, self.fx, self.fy, self.fz = scratch
+        self.z, self.g, self.chip, self.core = here()
+        self.load = pltpu.make_async_copy(keep, self.held, local_sem)
+        self.width = self.held.shape[-1] // 2
+
+    def chip_of(self, gy):
+        return gy // 2
+
+    def half(self, ref, which):
+        return ref.at[:, :, pl.ds(which * self.width, self.width)]
+
+    def start(self, to_sibling):
+        self.load.start()
+        if self.whole:
+            self.sib = self.wires.send(to_sibling, self.from_sib, (self.z, sibling(self.g)))
+
+    def corner(self):
+        self.load.wait()
+        if self.whole:
+            self.sib.wait_recv()
+
+            @pl.loop(0, LINES)
+            def _(n):
+                for q in range(PLANE):
+                    self.held[n, q] = (
+                        self.held[n, q].astype(F32) + self.from_sib[n, q].astype(F32)
+                    ).astype(BF16)
+
+        far = self.held.at[:, self.chip_of(along_y(along_x(self.g)))]
+        self.to_y = self.wires.send(self.half(far, 0), self.cy, (self.z, along_y(self.g)))
+        self.to_x = self.wires.send(self.half(far, 1), self.cx, (self.z, along_x(self.g)))
+
+    def sides(self):
+        width = self.width
+        self.to_y.wait_recv()
+        near = self.chip_of(along_x(self.g))
+
+        @pl.loop(0, LINES)
+        def _(n):
+            self.held[n, near, :, :width] = (
+                self.held[n, near, :, :width].astype(F32) + self.cy[n].astype(F32)
+            ).astype(BF16)
+
+        self.along_x = self.wires.send(self.held.at[:, near], self.fx, (self.z, along_x(self.g)))
+        self.to_x.wait_recv()
+        beside = self.chip_of(along_y(self.g))
+
+        @pl.loop(0, LINES)
+        def _(n):
+            self.held[n, beside, :, width:] = (
+                self.held[n, beside, :, width:].astype(F32) + self.cx[n].astype(F32)
+            ).astype(BF16)
+
+        self.along_y = self.wires.send(self.held.at[:, beside], self.fy, (self.z, along_y(self.g)))
+
+    def line(self):
+        self.along_x.wait_recv()
+        self.along_y.wait_recv()
+        self.zs = []
+        for k in (2, 1, 3):
+            there = turn(self.z, k)
+            self.fx[there] = (
+                self.held[there, self.chip].astype(F32)
+                + self.fx[there].astype(F32)
+                + self.fy[there].astype(F32)
+            ).astype(BF16)
+            self.zs.append(
+                self.wires.send(self.fx.at[there], self.fz.at[k - 1], (there, self.g))
+            )
+        z = self.z
+        self.out[...] = (
+            self.held[z, self.chip].astype(F32) + self.fx[z].astype(F32) + self.fy[z].astype(F32)
+        )
+
+    def finish(self):
+        for copy in self.zs:
+            copy.wait_recv()
+        self.out[...] += (
+            self.fz[0].astype(F32) + self.fz[1].astype(F32) + self.fz[2].astype(F32)
+        )
+
+
+def fold_scratch(rows, cols, whole):
+    half = cols // 2
+    return [
+        pltpu.VMEM((LINES, PLANE, rows, cols), BF16),
+        pltpu.VMEM((LINES, PLANE, rows, cols) if whole else (1, 1, 16, 128), BF16),
+        pltpu.VMEM((LINES, rows, half), BF16),
+        pltpu.VMEM((LINES, rows, half), BF16),
+        pltpu.VMEM((LINES, rows, cols), BF16),
+        pltpu.VMEM((LINES, rows, cols), BF16),
+        pltpu.VMEM((LINES - 1, rows, cols), BF16),
+    ]
+
+
+def fold_sems(count, whole):
+    return count * ((1 if whole else 0) + 4 + 3)
+
+
+def fold_all(flows):
+    stages = ("corner", "sides", "line", "finish")
+    for tick in range(len(flows) + len(stages) - 1):
+        for n in range(len(stages)):
+            flow = tick - n
+            if 0 <= flow < len(flows):
+                getattr(flows[flow], stages[n])()
+
+
+def scatter_kernel(count, whole, *refs):
+    parts, outs = refs[:count], refs[count : 2 * count]
+    rest = list(refs[2 * count :])
+    send_sems, recv_sems, local_sems = rest[:3]
+    scratch = rest[3:]
+    z, g, chip, core = here()
+    others = line_of(z, g) + [(z, along_x(g)), (z, along_y(g))]
+    if whole:
+        others.append((z, sibling(g)))
+    greet(others)
+    wires = Wires(send_sems, recv_sems)
+    flows = []
+    for n in range(count):
+        ours = parts[n].at[:, :, core] if whole else parts[n]
+        flows.append(
+            Fold(
+                wires, parts[n], ours, whole, scratch[7 * n : 7 * n + 7], outs[n], local_sems.at[n]
+            )
+        )
+    for n, flow in enumerate(flows):
+        flow.start(parts[n].at[:, :, 1 - core] if whole else None)
+    fold_all(flows)
+    wires.drain()
+
+
+def scatter(parts, whole, ident):
+    count = len(parts)
+    rows, cols = parts[0].shape[-2:]
+    scratch = []
+    for _ in parts:
+        scratch += fold_scratch(rows, cols, whole)
+    sems = fold_sems(count, whole)
+    return pl.pallas_call(
+        partial(scatter_kernel, count, whole),
+        out_shape=[jax.ShapeDtypeStruct((rows, cols), F32)] * count,
+        in_specs=[pl.BlockSpec(memory_space=HBM)] * count,
+        out_specs=[pl.BlockSpec(memory_space=pltpu.VMEM)] * count,
+        scratch_shapes=[
+            pltpu.SemaphoreType.DMA((sems,)),
+            pltpu.SemaphoreType.DMA((sems,)),
+            pltpu.SemaphoreType.DMA((count,)),
+        ]
+        + scratch,
+        compiler_params=pltpu.CompilerParams(
+            collective_id=ident, has_side_effects=True, vmem_limit_bytes=60 * 2**20
+        ),
+        name="scatter_%d" % ident,
+    )(*parts)
 
 
 def layer_norm(row_block, gain_row):
@@ -45,7 +447,7 @@
     )
 
 
-def per_device(
+def plain_device(
     media,
     latents,
     frame_counts,
@@ -341,6 +743,757 @@
     )
 
 
+GROUP = 4
+
+
+def feed_kernel(
+    up_ref, down_ref, cot_ref, up_out, down_out, cot_out, send_sems, recv_sems, local_sems
+):
+    z, g, chip, core = here()
+    here_chip = 4 * z + chip
+    me = 2 * here_chip + core
+    width = up_out.shape[-1]
+    mates = []
+    for j in range(1, 16):
+        there = (here_chip + j) % 16
+        mates.append((there // 4, 2 * (there % 4) + core))
+    near = (z, sibling(g))
+    greet(mates + [near])
+    wires = Wires(send_sems, recv_sems)
+
+    def piece(there):
+        return up_ref.at[:, pl.ds(pl.multiple_of(there * width, 128), width)]
+
+    kept = [
+        pltpu.make_async_copy(piece(here_chip), up_out.at[me], local_sems.at[0]),
+        pltpu.make_async_copy(down_ref, down_out.at[core], local_sems.at[1]),
+        pltpu.make_async_copy(cot_ref, cot_out.at[here_chip], local_sems.at[2]),
+    ]
+    for copy in kept:
+        copy.start()
+    flow = Spread(
+        wires, cot_ref, lambda zz, gg: cot_out.at[zz * 4 + gg // 2], columns_half, False
+    )
+    flow.first()
+    down = wires.send(down_ref, down_out.at[core], near)
+    given = [wires.send(piece(here_chip), up_out.at[me], near)]
+    moved = []
+    for j in range(1, 16):
+        moved.append(wires.send(piece((here_chip + j) % 16), up_out.at[me], mates[j - 1]))
+    flow.corner(0)
+    for k in (1, 3, 2):
+        flow.column(k)
+    for k in (1, 3, 2):
+        flow.corner(k)
+    for j in range(1, 16):
+        moved[j - 1].wait_recv()
+        origin = 2 * ((here_chip + 16 - j) % 16) + core
+        given.append(wires.send(up_out.at[origin], up_out.at[origin], near))
+    for k in (0, 1, 3, 2):
+        flow.last(k)
+    down.wait_recv()
+    for copy in given:
+        copy.wait_recv()
+    for copy in kept:
+        copy.wait()
+    wires.drain()
+
+
+def feed(w_up, w_down, cotangent):
+    rows, width = w_up.shape
+    sems = spread_sems(1, False) + 1 + 16 + 15
+    return pl.pallas_call(
+        feed_kernel,
+        out_shape=[
+            jax.ShapeDtypeStruct((32, rows, width // 16), BF16),
+            jax.ShapeDtypeStruct((2,) + w_down.shape, BF16),
+            jax.ShapeDtypeStruct((16,) + cotangent.shape, BF16),
+        ],
+        in_specs=[pl.BlockSpec(memory_space=HBM)] * 3,
+        out_specs=[pl.BlockSpec(memory_space=HBM)] * 3,
+        scratch_shapes=[
+            pltpu.SemaphoreType.DMA((sems,)),
+            pltpu.SemaphoreType.DMA((sems,)),
+            pltpu.SemaphoreType.DMA((3,)),
+        ],
+        compiler_params=pltpu.CompilerParams(collective_id=1, has_side_effects=True),
+        name="feed",
+    )(w_up, w_down, cotangent)
+
+
+def give_back_kernel(
+    up_ref,
+    down_ref,
+    up_out,
+    down_out,
+    up_held,
+    up_near,
+    down_near,
+    send_sems,
+    recv_sems,
+    local_sems,
+):
+    z, g, chip, core = here()
+    here_chip = 4 * z + chip
+    mates = []
+    for j in range(1, 16):
+        there = (here_chip + j) % 16
+        mates.append((there // 4, 2 * (there % 4) + core))
+    near = (z, sibling(g))
+    greet(mates + [near])
+    wires = Wires(send_sems, recv_sems)
+    load_up = pltpu.make_async_copy(up_ref.at[:, core], up_held, local_sems.at[0])
+    load_down = pltpu.make_async_copy(down_ref.at[core], down_out, local_sems.at[1])
+    load_up.start()
+    load_down.start()
+    up = wires.send(up_ref.at[:, 1 - core], up_near, near)
+    down = wires.send(down_ref.at[1 - core], down_near, near)
+    load_up.wait()
+    up.wait_recv()
+    add_slots(up_held, up_near, 16)
+    moved = []
+    for j in range(1, 16):
+        there = (here_chip + j) % 16
+        moved.append(wires.send(up_held.at[there], up_out.at[here_chip], mates[j - 1]))
+    up_out[here_chip] = up_held[here_chip]
+    load_down.wait()
+    down.wait_recv()
+    rows = down_out.shape[0] // 8
+
+    @pl.loop(0, 8)
+    def _(n):
+        block = pl.ds(pl.multiple_of(n * rows, 8), rows)
+        down_out[block] = down_out[block] + down_near[block]
+
+    for copy in moved:
+        copy.wait_recv()
+    wires.drain()
+
+
+def give_back(up_part, down_part):
+    rows, width = up_part.shape[-2:]
+    down_shape = down_part.shape[1:]
+    return pl.pallas_call(
+        give_back_kernel,
+        out_shape=[
+            jax.ShapeDtypeStruct((16, rows, width), BF16),
+            jax.ShapeDtypeStruct(down_shape, F32),
+        ],
+        in_specs=[pl.BlockSpec(memory_space=HBM)] * 2,
+        out_specs=[pl.BlockSpec(memory_space=pltpu.VMEM)] * 2,
+        scratch_shapes=[
+            pltpu.VMEM((16, rows, width), BF16),
+            pltpu.VMEM((16, rows, width), BF16),
+            pltpu.VMEM(down_shape, F32),
+            pltpu.SemaphoreType.DMA((17,)),
+            pltpu.SemaphoreType.DMA((17,)),
+            pltpu.SemaphoreType.DMA((2,)),
+        ],
+        compiler_params=pltpu.CompilerParams(collective_id=2, has_side_effects=True),
+        name="give_back",
+    )(up_part, down_part)
+
+
+def total_kernel(mine, out, sums, got, send_sems, recv_sems):
+    z, g, _, _ = here()
+    sides = [(z, sibling(g)), (z, along_x(g)), (z, along_y(g))]
+    line = line_of(z, g)
+    greet(sides + line)
+    wires = Wires(send_sems, recv_sems)
+    source = mine
+    for n, side in enumerate(sides):
+        copy = wires.send(source, got.at[n], side)
+        copy.wait_recv()
+        sums[n] = source[...] + got[n]
+        source = sums.at[n]
+    copies = [wires.send(source, got.at[3 + k], line[k]) for k in range(3)]
+    for copy in copies:
+        copy.wait_recv()
+    out[...] = source[...] + got[3] + got[4] + got[5]
+    wires.drain()
+
+
+def total(array):
+    return pl.pallas_call(
+        total_kernel,
+        out_shape=jax.ShapeDtypeStruct(array.shape, F32),
+        in_specs=[pl.BlockSpec(memory_space=pltpu.VMEM)],
+        out_specs=pl.BlockSpec(memory_space=pltpu.VMEM),
+        scratch_shapes=[
+            pltpu.VMEM((3,) + array.shape, F32),
+            pltpu.VMEM((6,) + array.shape, F32),
+            pltpu.SemaphoreType.DMA((6,)),
+            pltpu.SemaphoreType.DMA((6,)),
+        ],
+        compiler_params=pltpu.CompilerParams(collective_id=3, has_side_effects=True),
+        name="total",
+    )(array)
+
+
+def head_masks(rows, width, head_size):
+    lane = lax.broadcasted_iota(jnp.int32, (rows, width), 1)
+    return [(lane >= h * head_size) & (lane < (h + 1) * head_size) for h in range(GROUP)]
+
+
+def stacked(block, masks):
+    zero = jnp.zeros_like(block)
+    return jnp.concatenate([jnp.where(mask, block, zero) for mask in masks], axis=0)
+
+
+def unstacked(block, masks):
+    rows = block.shape[0] // GROUP
+    total = jnp.where(masks[0], block[:rows], 0.0)
+    for h in range(1, GROUP):
+        total = jnp.where(masks[h], block[h * rows : (h + 1) * rows], total)
+    return total
+
+
+def dot_last(a, b):
+    return lax.dot_general(a, b, (((1,), (1,)), ((), ())), preferred_element_type=F32)
+
+
+def dot_first(a, b):
+    return lax.dot_general(a, b, (((0,), (0,)), ((), ())), preferred_element_type=F32)
+
+
+def spread_heads(columns, first, masks):
+    out = jnp.where(masks[0], columns[:, first : first + 1], 0.0)
+    for h in range(1, GROUP):
+        out = jnp.where(masks[h], columns[:, first + h : first + h + 1], out)
+    return out
+
+
+def attend(queries, keys, values, valid, scale, masks):
+    rows = queries.shape[0]
+    score = dot_last(stacked(queries, masks), keys) * scale
+    expo = jnp.exp(score)
+    if valid is not None:
+        expo = jnp.where(valid > 0, expo, 0.0)
+    totals = jnp.sum(expo, axis=1, keepdims=True)
+    moments = jnp.sum(expo * score, axis=1, keepdims=True)
+    weighted = jnp.dot(expo.astype(BF16), values, preferred_element_type=F32)
+    heads = [(totals[h * rows : (h + 1) * rows], moments[h * rows : (h + 1) * rows]) for h in range(GROUP)]
+    return unstacked(weighted, masks), heads
+
+
+def put_heads(heads, group, lane):
+    out = jnp.zeros(lane.shape, F32)
+    for h, (total, moment) in enumerate(heads):
+        out = jnp.where(lane == group * GROUP + h, total, out)
+        out = jnp.where(lane == H + group * GROUP + h, moment, out)
+    return out
+
+
+def forward_kernel(
+    scale,
+    item_ref,
+    table_ref,
+    key_ref,
+    value_ref,
+    valid_ref,
+    own_query_ref,
+    own_key_ref,
+    own_value_ref,
+    weighted_ref,
+    stats_ref,
+    own_weighted_ref,
+    own_stats_ref,
+    sums,
+):
+    items, rows, width = table_ref.shape
+    frames = valid_ref.shape[0]
+    patches = valid_ref.shape[2]
+    groups = H // GROUP
+    span = width // groups
+    masks = head_masks(rows, span, span // GROUP)
+    lane = lax.broadcasted_iota(jnp.int32, (rows, 128), 1)
+    sums[...] = jnp.zeros_like(sums)
+    stats_ref[...] = jnp.zeros_like(stats_ref)
+    stats = jnp.zeros((rows, 128), F32)
+    for group in range(groups):
+        cols = pl.ds(group * span, span)
+        weighted, heads = attend(
+            own_query_ref[:, cols], own_key_ref[:, cols], own_value_ref[:, cols], None, scale, masks
+        )
+        own_weighted_ref[:, cols] = weighted
+        stats = stats + put_heads(heads, group, lane)
+    own_stats_ref[...] = stats
+
+    @pl.loop(0, frames)
+    def _(frame):
+        item = item_ref[frame]
+        block = pl.ds(pl.multiple_of(frame * patches, patches), patches)
+        valid = valid_ref[frame]
+        stats = jnp.zeros((rows, 128), F32)
+        for group in range(groups):
+            cols = pl.ds(group * span, span)
+            weighted, heads = attend(
+                table_ref[item, :, cols],
+                key_ref[block, cols],
+                value_ref[block, cols],
+                valid,
+                scale,
+                masks,
+            )
+            sums[item, :, cols] += weighted
+            stats = stats + put_heads(heads, group, lane)
+        stats_ref[item] += stats
+
+    weighted_ref[...] = sums[...].astype(BF16)
+
+
+def forward(item_index, table, keys, values, valid, own, scale):
+    items, rows, width = table.shape
+    vmem = pl.BlockSpec(memory_space=pltpu.VMEM)
+    return pl.pallas_call(
+        partial(forward_kernel, scale),
+        out_shape=[
+            jax.ShapeDtypeStruct((items, rows, width), BF16),
+            jax.ShapeDtypeStruct((items, rows, 128), F32),
+            jax.ShapeDtypeStruct((rows, width), F32),
+            jax.ShapeDtypeStruct((rows, 128), F32),
+        ],
+        in_specs=[pl.BlockSpec(memory_space=pltpu.SMEM)] + [vmem] * 7,
+        out_specs=[vmem] * 4,
+        scratch_shapes=[pltpu.VMEM((items, rows, width), F32)],
+        name="attention_forward",
+    )(item_index, table, keys, values, valid, *own)
+
+
+def repel(queries, grads, keys, values, valid, shift, slope, scale, masks):
+    query_stack = stacked(queries, masks)
+    grad_stack = stacked(grads, masks)
+    score = dot_last(query_stack, keys) * scale
+    expo = jnp.exp(score)
+    if valid is not None:
+        expo = jnp.where(valid > 0, expo, 0.0)
+    mix = dot_last(grad_stack, values)
+    raw = (expo * (mix + shift + slope * score) * scale).astype(BF16)
+    query_grad = unstacked(jnp.dot(raw, keys, preferred_element_type=F32), masks)
+    key_grad = dot_first(raw, query_stack).astype(BF16)
+    value_grad = dot_first(expo.astype(BF16), grad_stack).astype(BF16)
+    return query_grad, key_grad, value_grad
+
+
+def stacked_columns(terms, first):
+    return jnp.concatenate([terms[:, first + h : first + h + 1] for h in range(GROUP)], axis=0)
+
+
+def backward_kernel(
+    scale,
+    item_ref,
+    table_ref,
+    grad_ref,
+    terms_ref,
+    key_ref,
+    value_ref,
+    valid_ref,
+    own_query_ref,
+    own_grad_ref,
+    own_terms_ref,
+    own_key_ref,
+    own_value_ref,
+    query_grad_ref,
+    key_grad_ref,
+    value_grad_ref,
+    own_query_grad_ref,
+    own_key_grad_ref,
+    own_value_grad_ref,
+    sums,
+):
+    items, rows, width = table_ref.shape
+    frames = valid_ref.shape[0]
+    patches = valid_ref.shape[2]
+    groups = H // GROUP
+    span = width // groups
+    masks = head_masks(rows, span, span // GROUP)
+    sums[...] = jnp.zeros_like(sums)
+    own_terms = own_terms_ref[...]
+    for group in range(groups):
+        cols = pl.ds(group * span, span)
+        own_query_grad_ref[:, cols], own_key_grad_ref[:, cols], own_value_grad_ref[:, cols] = repel(
+            own_query_ref[:, cols],
+            own_grad_ref[:, cols],
+            own_key_ref[:, cols],
+            own_value_ref[:, cols],
+            None,
+            stacked_columns(own_terms, group * GROUP),
+            stacked_columns(own_terms, H + group * GROUP),
+            scale,
+            masks,
+        )
+
+    @pl.loop(0, frames)
+    def _(frame):
+        item = item_ref[frame]
+        block = pl.ds(pl.multiple_of(frame * patches, patches), patches)
+        valid = valid_ref[frame]
+        terms = terms_ref[item]
+        for group in range(groups):
+            cols = pl.ds(group * span, span)
+            query_grad, key_grad_ref[block, cols], value_grad_ref[block, cols] = repel(
+                table_ref[item, :, cols],
+                grad_ref[item, :, cols],
+                key_ref[block, cols],
+                value_ref[block, cols],
+                valid,
+                stacked_columns(terms, group * GROUP),
+                stacked_columns(terms, H + group * GROUP),
+                scale,
+                masks,
+            )
+            sums[item, :, cols] += query_grad
+
+    query_grad_ref[...] = sums[...].astype(BF16)
+
+
+def backward(item_index, table, grads, terms, keys, values, valid, own, scale):
+    items, rows, width = table.shape
+    vmem = pl.BlockSpec(memory_space=pltpu.VMEM)
+    return pl.pallas_call(
+        partial(backward_kernel, scale),
+        out_shape=[
+            jax.ShapeDtypeStruct((items, rows, width), BF16),
+            jax.ShapeDtypeStruct(keys.shape, BF16),
+            jax.ShapeDtypeStruct(keys.shape, BF16),
+            jax.ShapeDtypeStruct((rows, width), F32),
+            jax.ShapeDtypeStruct((rows, width), BF16),
+            jax.ShapeDtypeStruct((rows, width), BF16),
+        ],
+        in_specs=[pl.BlockSpec(memory_space=pltpu.SMEM)] + [vmem] * 11,
+        out_specs=[vmem] * 6,
+        scratch_shapes=[pltpu.VMEM((items, rows, width), F32)],
+        name="attention_backward",
+    )(item_index, table, grads, terms, keys, values, valid, *own)
+
+
+def settle_kernel(
+    weighted_ref,
+    stats_ref,
+    own_weighted_ref,
+    own_stats_ref,
+    out_ref,
+    latents_ref,
+    gain_ref,
+    attention_ref,
+    attn_ref,
+    sums_ref,
+    middle_ref,
+    normed_ref,
+):
+    rows, width = latents_ref.shape
+    span = width // (H // GROUP)
+    masks = head_masks(rows, span, span // GROUP)
+    stats = own_stats_ref[...]
+    for n in range(stats_ref.shape[0]):
+        stats = stats + stats_ref[n]
+    sums_ref[...] = stats
+    for group in range(H // GROUP):
+        cols = pl.ds(group * span, span)
+        weighted = own_weighted_ref[:, cols]
+        for n in range(weighted_ref.shape[0]):
+            weighted = weighted + weighted_ref[n, :, cols].astype(F32)
+        attention = weighted / spread_heads(stats, group * GROUP, masks)
+        attention_ref[:, cols] = attention
+        attn_ref[:, cols] = attention.astype(BF16)
+    middle = latents_ref[...].astype(F32) + jnp.dot(
+        attn_ref[...], out_ref[...], preferred_element_type=F32
+    )
+    middle_ref[...] = middle
+    normed_ref[...] = layer_norm(middle, gain_ref[...]).astype(BF16)
+
+
+def settle(weighted, stats, own_weighted, own_stats, w_out, latents, gain):
+    vmem = pl.BlockSpec(memory_space=pltpu.VMEM)
+    shape = latents.shape
+    return pl.pallas_call(
+        settle_kernel,
+        out_shape=[
+            jax.ShapeDtypeStruct(shape, F32),
+            jax.ShapeDtypeStruct(shape, BF16),
+            jax.ShapeDtypeStruct(own_stats.shape, F32),
+            jax.ShapeDtypeStruct(shape, F32),
+            jax.ShapeDtypeStruct(shape, BF16),
+        ],
+        in_specs=[vmem] * 7,
+        out_specs=[vmem] * 5,
+        name="settle",
+    )(weighted, stats, own_weighted, own_stats, w_out, latents, gain)
+
+
+def norm_pull(rows, gain, grad):
+    mean = jnp.mean(rows, axis=-1, keepdims=True)
+    centred = rows - mean
+    inverse = lax.rsqrt(jnp.mean(centred * centred, axis=-1, keepdims=True) + NORM_STABILIZER)
+    xhat = centred * inverse
+    t = grad * gain
+    pulled = (
+        t
+        - jnp.mean(t, axis=-1, keepdims=True)
+        - xhat * jnp.mean(t * xhat, axis=-1, keepdims=True)
+    ) * inverse
+    return pulled, grad * xhat
+
+
+def unsettle_kernel(
+    normed_grad_ref,
+    middle_ref,
+    gain_ref,
+    cot_ref,
+    out_ref,
+    attention_ref,
+    stats_ref,
+    coef_ref,
+    middle_grad_ref,
+    low_ref,
+    gain_grad_ref,
+    weighted_grad_ref,
+    terms_ref,
+    attn_grad,
+):
+    rows, width = middle_ref.shape
+    span = width // (H // GROUP)
+    masks = head_masks(rows, span, span // GROUP)
+    pulled, summand = norm_pull(middle_ref[...], gain_ref[...], normed_grad_ref[...])
+    gain_grad_ref[...] = jnp.sum(summand, axis=0, keepdims=True)
+    middle_grad = cot_ref[...].astype(F32) + pulled
+    middle_grad_ref[...] = middle_grad
+    low_ref[...] = middle_grad.astype(BF16)
+    attn_grad[...] = dot_last(low_ref[...], out_ref[...])
+    stats = stats_ref[...]
+    coef = coef_ref[0, 0]
+    lane = lax.broadcasted_iota(jnp.int32, (rows, 128), 1)
+    terms = jnp.zeros((rows, 128), F32)
+    for group in range(H // GROUP):
+        cols = pl.ds(group * span, span)
+        grad = attn_grad[:, cols]
+        first = group * GROUP
+        weighted_grad_ref[:, cols] = (grad / spread_heads(stats, first, masks)).astype(BF16)
+        along = grad * attention_ref[:, cols]
+        for h in range(GROUP):
+            inner = jnp.sum(jnp.where(masks[h], along, 0.0), axis=1, keepdims=True)
+            total = stats[:, first + h : first + h + 1]
+            moment = stats[:, H + first + h : H + first + h + 1]
+            slope = -coef / total
+            shift = -inner / total + coef * (1.0 / total + moment / (total * total)) + slope
+            terms = jnp.where(lane == first + h, shift, terms)
+            terms = jnp.where(lane == H + first + h, slope, terms)
+    terms_ref[...] = terms
+
+
+def unsettle(normed_grad, middle, gain, cotangent, w_out, attention, stats, coef):
+    vmem = pl.BlockSpec(memory_space=pltpu.VMEM)
+    shape = middle.shape
+    return pl.pallas_call(
+        unsettle_kernel,
+        out_shape=[
+            jax.ShapeDtypeStruct(shape, F32),
+            jax.ShapeDtypeStruct(shape, BF16),
+            jax.ShapeDtypeStruct((1, shape[1]), F32),
+            jax.ShapeDtypeStruct(shape, BF16),
+            jax.ShapeDtypeStruct(stats.shape, F32),
+        ],
+        in_specs=[vmem] * 7 + [pl.BlockSpec(memory_space=pltpu.SMEM)],
+        out_specs=[vmem] * 5,
+        scratch_shapes=[pltpu.VMEM(shape, F32)],
+        name="unsettle",
+    )(normed_grad, middle, gain, cotangent, w_out, attention, stats, coef)
+
+
+def per_device(
+    media,
+    latents,
+    frame_counts,
+    time_index,
+    valid,
+    time_table,
+    media_gain,
+    latent_gain,
+    ffn_gain,
+    w_query,
+    w_key,
+    w_value,
+    w_out,
+    w_up,
+    w_down,
+    cotangent,
+):
+    frames = time_index.shape[0]
+    patches = valid.shape[0] // frames
+    latent_rows, width = latents.shape
+    shard = media_gain.shape[0]
+    scale = (width // H) ** (-0.5)
+    column = lax.axis_index("gx")
+    row_index = lax.axis_index("gy")
+    frame_ends = jnp.cumsum(frame_counts[row_index])
+    position = column * frames + jnp.arange(frames, dtype=jnp.int32)
+    item_index = jnp.sum((frame_ends[None, :] <= position[:, None]).astype(jnp.int32), axis=1)
+    item_index = jnp.clip(item_index, 0, LINES - 1).astype(jnp.int32)
+
+    count = jnp.sum(valid.astype(F32))
+    small = jnp.concatenate(
+        [
+            time_table.astype(F32),
+            media_gain.astype(F32)[None],
+            latent_gain.astype(F32)[None],
+            ffn_gain.astype(F32)[None],
+            jnp.full((1, shard), count, F32),
+            jnp.zeros((4, shard), F32),
+        ],
+        axis=0,
+    )
+    small = jnp.pad(small, ((0, 0), (0, 128 - shard)))
+    smalls, full_key, full_value, full_query, full_out = gather(
+        [small, w_key, w_value, w_query, w_out], True, 0, small=(0,)
+    )
+    full_key, full_value, full_query, full_out = (
+        w.reshape(width, width) for w in (full_key, full_value, full_query, full_out)
+    )
+    tables = jnp.swapaxes(smalls[:, :11, :shard], 0, 1).reshape(11, width)
+    full_time = tables[:8].astype(BF16)
+    full_media_gain, full_latent_gain, full_ffn_gain = tables[8:9], tables[9:10], tables[10:11]
+    valid_total = jnp.sum(smalls[:, 11, 0])
+    coefficient = ENTROPY_WEIGHT * (valid.shape[0] * lax.axis_size(AXES)) / valid_total
+    up_cols, down_rows, cot_rows = feed(w_up, w_down, cotangent)
+    up_cols = up_cols.reshape(width, -1)
+    down_rows = down_rows.reshape(-1, width)
+    cot_rows = cot_rows.reshape(-1, width)
+
+    time_onehot = (
+        time_index[:, None] == jnp.arange(full_time.shape[0], dtype=jnp.int32)[None, :]
+    ).astype(F32)
+    time_rows = product(time_onehot.astype(BF16), full_time)
+    media_in = (
+        media.astype(F32).reshape(frames, patches, width) + time_rows[:, None, :]
+    ).reshape(-1, width)
+    media_normed = layer_norm(media_in, full_media_gain).astype(BF16)
+    media_key = product(media_normed, full_key).astype(BF16)
+    media_value = product(media_normed, full_value).astype(BF16)
+    latent_in = latents.astype(F32)
+    latent_normed = layer_norm(latent_in, full_latent_gain).astype(BF16)
+    own_query = product(latent_normed, full_query).astype(BF16)
+    own_key = product(latent_normed, full_key).astype(BF16)
+    own_value = product(latent_normed, full_value).astype(BF16)
+    valid_rows = valid.reshape(frames, 1, patches)
+    (table,) = along_line([own_query], True, 4)
+    weighted, stats, own_weighted, own_stats = forward(
+        item_index,
+        table,
+        media_key,
+        media_value,
+        valid_rows,
+        (own_query, own_key, own_value),
+        scale,
+    )
+    got_weighted, got_stats = along_line([weighted, stats], False, 5)
+    attention, attn_low, sums, middle, ffn_normed = settle(
+        got_weighted, got_stats, own_weighted, own_stats, full_out, latents, full_ffn_gain
+    )
+    (ffn_rows,) = gather([ffn_normed], False, 6)
+    ffn_rows = ffn_rows.reshape(-1, width)
+    up_rows = product(ffn_rows, up_cols)
+    hidden = jax.nn.gelu(up_rows, approximate=False).astype(BF16)
+    hidden_grad = inner_last(cot_rows, down_rows)
+    gelu_pull = jax.vjp(partial(jax.nn.gelu, approximate=False), up_rows)[1]
+    up_grad = gelu_pull(hidden_grad)[0].astype(BF16)
+    normed_part = inner_last(up_grad, up_cols).astype(BF16)
+    down_part = product(hidden, down_rows).astype(BF16)
+    shape = (LINES, PLANE, latent_rows, width)
+    ffn_normed_grad, down_sum = scatter(
+        [normed_part.reshape(shape), down_part.reshape(shape)], False, 7
+    )
+    new_latents = (middle + down_sum).astype(BF16)
+    up_grad_part = inner_first(ffn_rows, up_grad).astype(BF16)
+    down_grad_part = inner_first(hidden, cot_rows)
+    shard_up, shard_down = give_back(
+        up_grad_part.reshape(16, 2, shard, -1), down_grad_part.reshape(2, -1, width)
+    )
+    shard_up = jnp.swapaxes(shard_up, 0, 1).reshape(shard, -1).astype(F32)
+    middle_grad, middle_low, grad_ffn_gain, weighted_grad, terms = unsettle(
+        ffn_normed_grad,
+        middle,
+        full_ffn_gain,
+        cotangent,
+        full_out,
+        attention,
+        sums,
+        coefficient.reshape(1, 1),
+    )
+    grad_table, terms_table = along_line([weighted_grad, terms], True, 8)
+    query_terms, media_key_grad, media_value_grad, query_part, own_key_grad, own_value_grad = backward(
+        item_index,
+        table,
+        grad_table,
+        terms_table,
+        media_key,
+        media_value,
+        valid_rows,
+        (own_query, weighted_grad, terms, own_key, own_value),
+        scale,
+    )
+    (got_query,) = along_line([query_terms], False, 9)
+    query_grad = (jnp.sum(got_query.astype(F32), axis=0) + query_part).astype(BF16)
+    media_normed_grad = inner_last(media_key_grad, full_key) + inner_last(
+        media_value_grad, full_value
+    )
+    media_grad, media_summand = norm_pull(media_in, full_media_gain, media_normed_grad)
+    grad_media_gain = jnp.sum(media_summand, axis=0, keepdims=True)
+    frame_sums = jnp.sum(media_grad.reshape(frames, patches, width), axis=1)
+    grad_time = collect(time_onehot, frame_sums)
+    latent_normed_grad = (
+        inner_last(query_grad, full_query)
+        + inner_last(own_key_grad, full_key)
+        + inner_last(own_value_grad, full_value)
+    )
+    latent_part, latent_summand = norm_pull(latent_in, full_latent_gain, latent_normed_grad)
+    grad_latent_gain = jnp.sum(latent_summand, axis=0, keepdims=True)
+    latents_grad = middle_grad + latent_part
+    key_part = inner_first(media_normed, media_key_grad) + inner_first(latent_normed, own_key_grad)
+    value_part = inner_first(media_normed, media_value_grad) + inner_first(
+        latent_normed, own_value_grad
+    )
+    out_part = inner_first(attn_low, middle_low)
+    query_weight_part = inner_first(latent_normed, query_grad)
+    slots = (LINES, PLANE, 2, shard, width)
+    shard_out, shard_value, shard_key, shard_query = scatter(
+        [
+            part.astype(BF16).reshape(slots)
+            for part in (out_part, value_part, key_part, query_weight_part)
+        ],
+        True,
+        10,
+    )
+    smalls_grad = total(
+        jnp.concatenate(
+            [
+                grad_time,
+                grad_media_gain,
+                grad_latent_gain,
+                grad_ffn_gain,
+                jnp.zeros((5, width), F32),
+            ],
+            axis=0,
+        )
+    )
+    place = (column * 8 + row_index) * shard
+    mine = lax.dynamic_slice(smalls_grad, (0, place), (16, shard))
+    return (
+        new_latents,
+        media_grad,
+        latents_grad,
+        mine[:8],
+        mine[8],
+        mine[9],
+        mine[10],
+        shard_query,
+        shard_key,
+        shard_value,
+        shard_out,
+        shard_up,
+        shard_down,
+    )
+
+
 def solution(mesh):
     in_specs = (
         P(("gx", "gy"), None),
@@ -376,5 +1529,6 @@
         P(("gx", "gy"), None),
     )
     return jax.shard_map(
-        per_device, mesh=mesh, in_specs=in_specs, out_specs=out_specs, check_vma=False
-    )
+        per_device if dict(mesh.shape) == {"gx": 4, "gy": 8} else plain_device,
+        mesh=mesh, in_specs=in_specs, out_specs=out_specs, check_vma=False
+    )

time: 1520 us -> 648 us (0.43)
  waiting for transfers between devices: 958 us -> 0 us
  Pallas kernels: 0 us -> 519 us
  blocking collectives: 234 us -> 0 us
  matrix products: 181 us -> 81.6 us
  local copies, waits for them, and re-layouts: 89.1 us -> 20 us
    all_gather x10 -> x0, waiting for transfers between devices: 635 us -> none  [the longest x1 151 us: per_device(): piece_up = lax.all_gather(up_grad, ('gx', 'gy'), axis=0, tiled=True)]
    pallas_call x0 -> x15, Pallas kernels: none -> 519 us  [the longest x2 175 us: scatter(): pl.pallas_call(partial(scatter_kernel, count, whole), out_shape=[jax.Shap...]
    reduce_scatter x4 -> x0, waiting for transfers between devices: 273 us -> none  [the longest x1 142 us: per_device(): lax.psum_scatter(grad_key, ('gx', 'gy'), scatter_dimension=0, tiled=True)]
    all_gather x5 -> x0, blocking collectives: 108 us -> none  [the longest x1 40.9 us: per_device(): lax.all_gather(time_table, ('gx', 'gy'), axis=1, tiled=True)]
    unnamed x2 -> x0, blocking collectives: 83.1 us -> none
    reshape x22 -> x0, local copies, waits for them, and re-layouts: 46.5 us -> none  [the longest x2 8.84 us: per_device(): value_heads = product(media_normed, full_value).astype(jnp.bfloat16).resh...]
    psum x1 -> x0, blocking collectives: 42.4 us -> none  [per_device(): valid_total = lax.psum(jnp.sum(valid.astype(jnp.float32)), ('gx', 'gy'))]
    unnamed x20 -> x0, waiting for transfers between devices: 30.9 us -> none
  transfers between devices with their start and end apart: 21 -> 0, of which waited for: 16 -> 0; matrix products, arithmetic and copies ran while one was open for 14% -> 0% of each run, Pallas kernels for 0% -> 0%
where the time goes in v1:
time: 648 us; the launch traced here: 641 us
  Pallas kernels  519 us (80%)
  matrix products  81.6 us (13%)
  local copies, waits for them, and re-layouts  20 us (3%)
  other arithmetic  17.7 us (3%)
    pallas_call x2, Pallas kernels, scatter(): pl.pallas_call(partial(scatter_kernel, count, whole), out_shape=[jax.Shap...  175 us
    pallas_call x2, Pallas kernels, gather(): pl.pallas_call(partial(gather_kernel, count, small, whole), out_shape=[ja...  128 us
    pallas_call x4, Pallas kernels, along_line(): pl.pallas_call(partial(line_kernel, count, spread), out_shape=[jax.ShapeD...  101 us
    pallas_call x1, Pallas kernels, feed(): pl.pallas_call(feed_kernel, out_shape=[jax.ShapeDtypeStruct((32, rows, wi...  45.3 us
    dot_general x8, matrix products, product(): return jnp.dot(left_side, right_side, preferred_element_type=jnp.float32)  28.4 us
    dot_general x7, matrix products, inner_last(): lax.dot_general(left_side, right_side, (((1,), (1,)), ((), ())), preferre...  26.6 us
    dot_general x8, matrix products, inner_first(): lax.dot_general(left_side, right_side, (((0,), (0,)), ((), ())), preferre...  26.3 us
    pallas_call x1, Pallas kernels, total(): pl.pallas_call(total_kernel, out_shape=jax.ShapeDtypeStruct(array.shape,...  23.3 us

profile of v1, /device:TPU:0, one launch (start us, length us, event | category | flops | bytes accessed | tf_op | source)
XLA Modules:
  0.0 640.9 jit_solution(9338047930409960135)
XLA Ops:
  0.7 1.3 convert_reduce_fusion.2
  2.0 0.6 broadcast_in_dim.56
  3.7 0.7 bitcast_convert_fusion.2
  4.4 1.1 convert_reduce_fusion.1
  5.5 1.2 fusion.41
  6.6 0.8 bitcast_convert_fusion
  7.4 0.7 concatenate.6
  8.8 45.3 %feed.1 = (bf16[32,48,384]{2,1,0:T(8,128)(2,1)}, bf16[2,192,1536]{2,1,0:T(8,128)(2,1)}, bf16[16,64,1536]{2,1,0:T(8,128)(2,1)}) custom-call(bf16[48,6144]{1,0:T(8,128)(2,1)} %up_ref.1, bf16[192,1536]{1,0:T(8,128)(2,1)} %down_ref.1, bf16[64,1536]{1,0:T(8,128)(2,1)} %cot_ref.3), custom_call_target="tpu_custom_call" | custom-call | tf_op jit(solution)/shard_map/feed/pallas_call | solution.py:805
  54.1 92.2 %gather_0.1 = (f32[32,16,128]{2,1,0:T(8,128)}, bf16[32,48,1536]{2,1,0:T(8,128)(2,1)}, bf16[32,48,1536]{2,1,0:T(8,128)(2,1)}, bf16[32,48,1536]{2,1,0:T(8,128)(2,1)}, bf16[32,48,1536]{2,1,0:T(8,128)(2,1)}) custom-call(f32[16,128]{1,0:T(8,128)} %pad.4.refs_0_, bf16[48,1536]{1,0:T(8,128)(2,1)} %refs_1_.1, bf16[48,1536]{1,0:T(8,128)(2,1)} %refs_2_.1, ...), custom_call_target="tpu_custom_call" | custom-call | tf_op jit(solution)/shard_map/gather_0/pallas_call | solution.py:199
  146.4 1.5 slice_reduce_fusion.3
  148.6 1.0 slice_bitcast_fusion
  150.1 0.7 slice.42.gain_ref
  151.2 0.6 multiply_reduce_fusion.2
  151.9 4.1 convolution_convert_fusion.9.refs_0_.own_query_ref
  156.1 1.7 convolution_convert_fusion.7.own_value_ref
  157.8 0.7 copy-done.6
  158.5 1.7 convolution_convert_fusion.8.own_key_ref
  160.2 31.8 %line_4.1.table_ref = bf16[4,64,1536]{2,1,0:T(8,128)(2,1)} custom-call(bf16[64,1536]{1,0:T(8,128)(2,1)} %convolution_convert_fusion.9.refs_0_.own_query_ref), custom_call_target="tpu_custom_call" | custom-call | tf_op jit(solution)/shard_map/line_4/pallas_call | solution.py:236
  192.6 6.7 %convolution_convert_fusion.4.value_ref = bf16[512,1536]{1,0:T(8,128)(2,1)} fusion(bf16[512,1536]{1,0:T(8,128)(2,1)S(1)} %multiply_convert_fusion, bf16[1536,1536]{1,0:T(8,128)(2,1)} %bitcast.162), kind=kOutput, calls=%fused_computation.19 | convolution fusion | flops 2416705536 | bytes 7864320 | tf_op jit(solution)/shard_map/dot_general | solution.py:425
  199.3 3.8 convolution_convert_fusion.5.key_ref
  203.1 8.3 %attention_forward.1 = (bf16[4,64,1536]{2,1,0:T(8,128)(2,1)}, f32[4,64,128]{2,1,0:T(8,128)}, f32[64,1536]{1,0:T(8,128)}, f32[64,128]{1,0:T(8,128)}) custom-call(s32[4]{0:T(128)} %broadcast_clamp_fusion.item_ref, bf16[4,64,1536]{2,1,0:T(8,128)(2,1)} %line_4.1.table_ref, bf16[512,1536]{1,0:T(8,128)(2,1)} %convolution_convert_fusion.5.key_ref, ...), custom_call_target="tpu_custom_call" | custom-call | tf_op jit(solution)/shard_map/attention_forward/pallas_call | solution.py:1048
  211.4 24.7 %line_5.1 = (bf16[4,64,1536]{2,1,0:T(8,128)(2,1)}, f32[4,64,128]{2,1,0:T(8,128)}) custom-call(bf16[4,64,1536]{2,1,0:T(8,128)(2,1)} %get-tuple-element.57.refs_0_, f32[4,64,128]{2,1,0:T(8,128)} %get-tuple-element.58.refs_1_), custom_call_target="tpu_custom_call" | custom-call | tf_op jit(solution)/shard_map/line_5/pallas_call | solution.py:236
  236.1 4.8 settle.1
  240.9 35.4 %gather_6.1 = bf16[16,64,1536]{2,1,0:T(8,128)(2,1)} custom-call(bf16[64,1536]{1,0:T(8,128)(2,1)} %get-tuple-element.65.refs_0_), custom_call_target="tpu_custom_call" | custom-call | tf_op jit(solution)/shard_map/gather_6/pallas_call | solution.py:199
  276.4 6.7 %fusion.8 = (bf16[384,1024]{1,0:T(8,128)(2,1)S(1)}, f32[1024,384]{0,1:T(8,128)S(1)}) fusion(bf16[1024,1536]{1,0:T(8,128)(2,1)} %bitcast.183, bf16[1536,384]{1,0:T(8,128)(2,1)} %bitcast.195), kind=kOutput, calls=%fused_computation.33 | convolution fusion | flops 1233518592 | bytes 6684672 | tf_op jit(solution)/shard_map/dot_general | solution.py:425
  283.1 2.8 fusion.58.down_ref
  285.9 5.6 add_convert_fusion
  291.5 2.9 convolution_convert_fusion.6
  294.4 3.6 convolution_convert_fusion.2
  297.9 15.9 %give_back.1 = (bf16[16,48,384]{2,1,0:T(8,128)(2,1)}, f32[192,1536]{1,0:T(8,128)}) custom-call(bf16[16,2,48,384]{3,2,1,0:T(8,128)(2,1)} %bitcast.188, f32[2,192,1536]{2,1,0:T(8,128)} %fusion.58.down_ref), custom_call_target="tpu_custom_call" | custom-call | tf_op jit(solution)/shard_map/give_back/pallas_call | solution.py:876
  313.9 1.1 convert_bitcast_fusion
  315.0 1.1 copy.40
  316.9 3.5 convolution_convert_fusion.3
  320.4 76.9 %scatter_7.1 = (f32[64,1536]{1,0:T(8,128)}, f32[64,1536]{1,0:T(8,128)}) custom-call(bf16[4,4,64,1536]{3,2,1,0:T(8,128)(2,1)} %bitcast.185, bf16[4,4,64,1536]{3,2,1,0:T(8,128)(2,1)} %bitcast.170), custom_call_target="tpu_custom_call" | custom-call | tf_op jit(solution)/shard_map/scatter_7/pallas_call | solution.py:399
  397.4 5.6 unsettle.1
  403.0 1.7 add_convert_fusion.2
  404.7 23.1 %line_8.1 = (bf16[4,64,1536]{2,1,0:T(8,128)(2,1)}, f32[4,64,128]{2,1,0:T(8,128)}) custom-call(bf16[64,1536]{1,0:T(8,128)(2,1)} %get-tuple-element.73.refs_0_.own_grad_ref, f32[64,128]{1,0:T(8,128)} %get-tuple-element.74.refs_1_.own_terms_ref), custom_call_target="tpu_custom_call" | custom-call | tf_op jit(solution)/shard_map/line_8/pallas_call | solution.py:236
  427.8 12.6 %attention_backward.1 = (bf16[4,64,1536]{2,1,0:T(8,128)(2,1)}, bf16[512,1536]{1,0:T(8,128)(2,1)}, bf16[512,1536]{1,0:T(8,128)(2,1)}, f32[64,1536]{1,0:T(8,128)},...) custom-call(s32[4]{0:T(128)} %broadcast_clamp_fusion.item_ref, bf16[4,64,1536]{2,1,0:T(8,128)(2,1)} %line_4.1.table_ref, ...), custom_call_target="tpu_custom_call" | custom-call | tf_op jit(solution)/shard_map/attention_backward/pallas_call | solution.py:1153
  440.5 21.3 %line_9.1 = bf16[4,64,1536]{2,1,0:T(8,128)(2,1)} custom-call(bf16[4,64,1536]{2,1,0:T(8,128)(2,1)} %get-tuple-element.80.refs_0_), custom_call_target="tpu_custom_call" | custom-call | tf_op jit(solution)/shard_map/line_9/pallas_call | solution.py:236
  461.7 1.3 convert_reduce_fusion
  463.0 1.0 add_convert_fusion.1
  464.1 4.0 fusion.55
  468.1 4.0 convolution_add_fusion.4
  472.2 4.6 fusion.54
  476.9 1.7 fusion.40
  478.6 3.2 multiply_reduce_fusion
  483.1 0.9 fusion.39
  484.0 2.6 bitcast_reduce_fusion
  486.9 2.0 concatenate.7.mine
  488.9 23.3 %total.1 = f32[16,1536]{1,0:T(8,128)} custom-call(f32[16,1536]{1,0:T(8,128)} %concatenate.7.mine), custom_call_target="tpu_custom_call" | custom-call | tf_op jit(solution)/shard_map/total/pallas_call | solution.py:917
  512.3 1.4 dynamic-slice_bitcast_fusion
  513.7 1.4 constant_dynamic-slice_fusion
  515.0 4.4 convolution_convert_fusion
  519.4 3.6 convolution_convert_fusion.1
  523.0 2.7 fusion.56
  525.7 3.7 fusion
  529.5 2.6 fusion.57
  532.1 3.6 fusion.1
  535.8 98.0 %scatter_10.1 = (f32[48,1536]{1,0:T(8,128)}, f32[48,1536]{1,0:T(8,128)}, f32[48,1536]{1,0:T(8,128)}, f32[48,1536]{1,0:T(8,128)}) custom-call(bf16[4,4,2,48,1536]{4,3,2,1,0:T(8,128)(2,1)} %bitcast.169, bf16[4,4,2,48,1536]{4,3,2,1,0:T(8,128)(2,1)} %bitcast.179, bf16[4,4,2,48,1536]{4,3,2,1,0:T(8,128)(2,1)} %bitcast.180, bf16[4,4,2,48,1536]{4,3,2,1,0:T(8,128)(2,1)} %bitcast.168), custom_call_target="tpu_custom_call" | custom-call | tf_op jit(solution)/shard_map/scatter_10/pallas_call | solution.py:399
  633.8 1.8 copy.46
  635.6 1.7 copy.47
  637.3 1.7 copy.48
  639.0 0.7 copy.49
  639.7 1.0 copy.50
  (119 shorter events, 5.8 us)
Async XLA Ops:
  0.6 2.0 copy-start
  5.4 152.3 %copy-start.23 = (f32[64]{0:T(128)}, f32[64]{0:T(128)S(1)}, u32[]{:S(2)}) copy-start(f32[64]{0:T(128)S(1)} %broadcast_multiply_fusion.5) | copy-start | bytes 772
  5.4 144.4 %copy-start.33 = (s32[4]{0:T(128)S(1)}, s32[4]{0:T(128)}, u32[]{:S(2)}) copy-start(s32[4]{0:T(128)} %param.19) | copy-start | bytes 52
  6.6 144.1 %copy-start.3 = (bf16[512,1536]{1,0:T(8,128)(2,1)S(1)}, bf16[512,1536]{1,0:T(8,128)(2,1)}, u32[]{:S(2)}) copy-start(bf16[512,1536]{1,0:T(8,128)(2,1)} %param.16) | copy-start | bytes 4718596
  6.6 151.1 %copy-start.28 = (f32[64]{0:T(128)}, f32[64]{0:T(128)S(1)}, u32[]{:S(2)}) copy-start(f32[64]{0:T(128)S(1)} %add_rsqrt_fusion.1) | copy-start | bytes 772
  150.1 41.9 %copy-start.18 = (f32[4,1536]{1,0:T(4,128)}, f32[4,1536]{1,0:T(4,128)S(1)}, u32[]{:S(2)}) copy-start(f32[4,1536]{1,0:T(4,128)S(1)} %fusion.43) | copy-start | bytes 73732
  150.8 1.2 copy-start.4
  151.1 40.8 %copy-start.26 = (f32[512]{0:T(512)}, f32[512]{0:T(512)S(1)}, u32[]{:S(2)}) copy-start(f32[512]{0:T(512)S(1)} %broadcast_multiply_fusion.2) | copy-start | bytes 6148
  151.8 40.2 %copy-start.31 = (f32[512]{0:T(512)}, f32[512]{0:T(512)S(1)}, u32[]{:S(2)}) copy-start(f32[512]{0:T(512)S(1)} %add_rsqrt_fusion) | copy-start | bytes 6148
  151.9 4.2 copy-start.2
  156.1 2.4 copy-start.6
  192.0 7.3 %slice-start.2 = ((s8[4718592]{0:T(1024)(128)(4,1)}), s8[4194304]{0:T(1024)(128)(4,1)S(1)}, s32[]{:S(2)}) async-start(s8[4718592]{0:T(1024)(128)(4,1)} %bitcast.174), calls=%async_computation.2 | async-start | bytes 8388608
  192.6 6.7 %slice-start.3 = ((s8[4718592]{0:T(1024)(128)(4,1)}), s8[524288]{0:T(1024)(128)(4,1)S(1)}, s32[]{:S(2)}) async-start(s8[4718592]{0:T(1024)(128)(4,1)} %bitcast.174), calls=%async_computation.3 | async-start | bytes 1048576
  276.4 6.8 %copy-start.35 = (bf16[16,64,1536]{2,1,0:T(8,128)(2,1)S(1)}, bf16[16,64,1536]{2,1,0:T(8,128)(2,1)}, u32[]{:S(2)}) copy-start(bf16[16,64,1536]{2,1,0:T(8,128)(2,1)} %get-tuple-element.67) | copy-start | bytes 9437188
  283.1 2.8 copy-start.11
  285.9 5.6 copy-start.7
  291.5 2.9 copy-start.39
  315.0 1.7 copy-start.38
  315.0 1.9 copy-start.40
  397.4 5.6 copy-start.8
  464.1 4.0 copy-start.13
  464.1 8.1 %copy-start.36 = (bf16[512,1536]{1,0:T(8,128)(2,1)S(1)}, bf16[512,1536]{1,0:T(8,128)(2,1)}, u32[]{:S(2)}) copy-start(bf16[512,1536]{1,0:T(8,128)(2,1)} %get-tuple-element.77) | copy-start | bytes 4718596
  468.1 8.7 %slice-start = ((s8[4718592]{0:T(1024)(128)(4,1)}), s8[4194304]{0:T(1024)(128)(4,1)S(1)}, s32[]{:S(2)}) async-start(s8[4718592]{0:T(1024)(128)(4,1)} %bitcast.164), calls=%async_computation | async-start | bytes 8388608
  472.1 4.7 slice-start.1
  472.1 4.7 copy-start.5
  472.2 4.7 copy-start.15
  472.2 4.7 copy-start.24
  472.2 4.7 copy-start.29
  476.9 1.7 copy-start.9
  476.9 1.7 copy-start.19
  476.9 1.7 copy-start.27
  476.9 1.7 copy-start.32
  478.6 4.5 copy-start.20
  484.0 2.6 copy-start.34
  515.0 4.4 copy-start.17
  515.0 4.4 copy-start.22
  519.4 3.6 copy-start.10
  523.0 2.7 copy-start.16
  523.0 2.7 copy-start.25
  523.0 2.7 copy-start.30
  525.7 3.7 copy-start.37
  529.5 2.7 copy-start.14
  633.8 5.2 copy-start.21
  633.8 5.9 copy-start.12
  637.3 3.4 copy-start.1

commit v2 on v1

--- a/solution.py
+++ b/solution.py
@@ -59,72 +59,134 @@
     def __init__(self, send_sems, recv_sems):
         self.send_sems, self.recv_sems, self.used, self.sent = send_sems, recv_sems, 0, []
 
-    def send(self, source, target, device):
-        n = self.used
-        self.used += 1
-        copy = pltpu.make_async_remote_copy(
+    def reserve(self, count):
+        first = self.used
+        self.used += count
+        return first
+
+    def copy(self, source, target, device, send, recv):
+        return pltpu.make_async_remote_copy(
             src_ref=source,
             dst_ref=target,
-            send_sem=self.send_sems.at[n],
-            recv_sem=self.recv_sems.at[n],
+            send_sem=self.send_sems.at[send],
+            recv_sem=self.recv_sems.at[recv],
             device_id=device,
             device_id_type=pl.DeviceIdType.MESH,
         )
+
+    def send(self, source, target, device):
+        n = self.reserve(1)
+        copy = self.copy(source, target, device, n, n)
         copy.start()
-        self.sent.append(copy)
+        self.sent.append((None, copy))
         return copy
 
+    def send_if(self, condition, source, target, device, send, recv):
+        copy = self.copy(source, target, device, send, recv)
+        self.sent.append((condition, copy))
+
+        @pl.when(condition)
+        def _():
+            copy.start()
+
+        return copy
+
     def drain(self):
-        for copy in self.sent:
-            copy.wait_send()
+        for condition, copy in self.sent:
+            if condition is None:
+                copy.wait_send()
+            else:
+                pl.when(condition)(copy.wait_send)
+
+
+class Line:
+    def __init__(self, wires, shard, slot):
+        self.wires, self.shard, self.slot = wires, shard, slot
+        self.z, self.g, _, _ = here()
+        self.base = wires.reserve(4)
+        low, high = (3 - self.z) // 3, self.z // 3
+        self.order = (1 + 2 * low, 3 - low - high, 2 - low + high)
+
+    def first(self):
+        z, g = self.z, self.g
+        own = self.slot(z)
+        base = self.base
+        self.wires.send_if(z < 3, self.shard, own, (turn(z, 1), g), base + 1, base + 1)
+        self.wires.send_if(z > 0, self.shard, own, (turn(z, 3), g), base + 3, base + 3)
+        self.across = self.wires.copy(self.shard, own, (turn(z, 2), g), base + 2, base + 2)
+        self.across.start()
+        self.wires.sent.append((None, self.across))
+
+    def take(self, step):
+        z, g = self.z, self.g
+        k = self.order[step]
+        origin = turn(z, LINES - k)
+        held = self.slot(origin)
+        self.wires.copy(held, held, (z, g), 0, self.base + k).wait_recv()
+        if step == 2:
+            self.relay(z == 2, 3, 3)
+        if step == 2:
+            self.relay(z == 1, 0, 1)
+        return origin
+
+    def relay(self, condition, there, k):
+        held = self.slot(turn(self.z, 2))
+        self.wires.send_if(
+            condition, held, held, (there, self.g), self.base, self.base + k
+        )
 
 
 class Spread:
     def __init__(self, wires, shard, slot, half, whole):
         self.wires, self.shard, self.slot, self.half, self.whole = wires, shard, slot, half, whole
         self.z, self.g, _, _ = here()
-        self.zs = [turn(self.z, LINES - k) if k else self.z for k in range(LINES)]
-        self.line, self.x, self.y, self.dx, self.dy, self.sib = {}, {}, {}, {}, {}, []
+        self.line = Line(wires, shard, lambda z: slot(z, self.g))
+        self.zs, self.x, self.y, self.dx, self.dy, self.sib = [self.z], [], [], {}, {}, []
 
     def side(self, gy):
         return (self.z, gy)
 
-    def to_sibling(self, source, where):
+    def to_sibling(self, held):
         if self.whole:
-            self.sib.append(self.wires.send(source, where, self.side(sibling(self.g))))
+            self.sib.append(self.wires.send(held, held, self.side(sibling(self.g))))
 
     def first(self):
         own = self.slot(self.z, self.g)
-        for k in (1, 3, 2):
-            self.line[k] = self.wires.send(self.shard, own, (turn(self.z, k), self.g))
-        self.x[0] = self.wires.send(self.shard, own, self.side(along_x(self.g)))
-        self.y[0] = self.wires.send(self.shard, own, self.side(along_y(self.g)))
-        self.to_sibling(self.shard, own)
-
-    def column(self, k):
-        self.line[k].wait_recv()
-        held = self.slot(self.zs[k], self.g)
-        self.x[k] = self.wires.send(held, held, self.side(along_x(self.g)))
-        self.y[k] = self.wires.send(held, held, self.side(along_y(self.g)))
-        self.to_sibling(held, held)
-
-    def corner(self, k):
-        self.x[k].wait_recv()
-        held = self.slot(self.zs[k], along_x(self.g))
+        self.line.first()
+        self.x.append(self.wires.send(self.shard, own, self.side(along_x(self.g))))
+        self.y.append(self.wires.send(self.shard, own, self.side(along_y(self.g))))
+        if self.whole:
+            self.sib.append(self.wires.send(self.shard, own, self.side(sibling(self.g))))
+
+    def column(self, step):
+        self.zs.append(self.line.take(step))
+        held = self.slot(self.zs[-1], self.g)
+        self.x.append(self.wires.send(held, held, self.side(along_x(self.g))))
+        self.y.append(self.wires.send(held, held, self.side(along_y(self.g))))
+        self.to_sibling(held)
+
+    def corner(self, n):
+        self.corner_x(n)
+        self.corner_y(n)
+
+    def corner_x(self, n):
+        self.x[n].wait_recv()
+        held = self.slot(self.zs[n], along_x(self.g))
         part = self.half(held, 0)
-        self.dy[k] = self.wires.send(part, part, self.side(along_y(self.g)))
-        self.to_sibling(held, held)
-        self.y[k].wait_recv()
-        held = self.slot(self.zs[k], along_y(self.g))
+        self.dy[n] = self.wires.send(part, part, self.side(along_y(self.g)))
+        self.to_sibling(held)
+
+    def corner_y(self, n):
+        self.y[n].wait_recv()
+        held = self.slot(self.zs[n], along_y(self.g))
         part = self.half(held, 1)
-        self.dx[k] = self.wires.send(part, part, self.side(along_x(self.g)))
-        self.to_sibling(held, held)
-
-    def last(self, k):
-        self.dy[k].wait_recv()
-        self.dx[k].wait_recv()
-        held = self.slot(self.zs[k], along_y(along_x(self.g)))
-        self.to_sibling(held, held)
+        self.dx[n] = self.wires.send(part, part, self.side(along_x(self.g)))
+        self.to_sibling(held)
+
+    def last(self, n):
+        self.dy[n].wait_recv()
+        self.dx[n].wait_recv()
+        self.to_sibling(self.slot(self.zs[n], along_y(along_x(self.g))))
 
     def finish(self):
         for copy in self.sib:
@@ -136,21 +198,23 @@
         flow.first()
     for flow in flows:
         flow.corner(0)
-    for k in (1, 3, 2):
+    for step in range(3):
         for flow in flows:
-            flow.column(k)
-    for k in (1, 3, 2):
+            flow.column(step)
         for flow in flows:
-            flow.corner(k)
-    for k in (0, 1, 3, 2):
+            flow.corner(step + 1)
+    for n in range(4):
         for flow in flows:
-            flow.last(k)
+            flow.last(n)
     for flow in flows:
         flow.finish()
 
 
-def spread_sems(flows, whole):
-    return flows * (3 + 8 + 8 + (16 if whole else 0))
+LINE_SEMS = 4
+
+
+def spread_sems(whole):
+    return LINE_SEMS + 8 + 8 + (16 if whole else 0)
 
 
 def columns_half(ref, which):
@@ -158,93 +222,73 @@
     return ref.at[..., pl.ds(which * width, width)]
 
 
-def gather_kernel(count, small, whole, *refs):
-    shards, outs = refs[:count], refs[count : 2 * count]
-    send_sems, recv_sems, local_sems = refs[2 * count :]
+def rows_half(ref, which):
+    rows = ref.shape[0] // 2
+    return ref.at[pl.ds(which * rows, rows)]
+
+
+def sides_of(z, g, whole):
+    near = [(z, along_x(g)), (z, along_y(g))]
+    return near + [(z, sibling(g))] if whole else near
+
+
+def params(ident):
+    return pltpu.CompilerParams(
+        collective_id=ident, has_side_effects=True, vmem_limit_bytes=60 * 2**20
+    )
+
+
+def sems(count):
+    return pltpu.SemaphoreType.DMA((count,))
+
+
+VMEM = pl.BlockSpec(memory_space=pltpu.VMEM)
+LEFT = pl.BlockSpec(memory_space=HBM)
+
+
+def gather_kernel(shard, out, send_sems, recv_sems, local_sem):
     z, g, chip, core = here()
-    others = line_of(z, g) + [(z, along_x(g)), (z, along_y(g))]
-    if whole:
-        others.append((z, sibling(g)))
-    greet(others)
+    greet(line_of(z, g) + sides_of(z, g, False))
     wires = Wires(send_sems, recv_sems)
-
-    def slot_of(out):
-        if whole:
-            return lambda zz, gg: out.at[zz * 8 + gg]
-        return lambda zz, gg: out.at[zz * 4 + gg // 2]
-
-    def rows_half(ref, which):
-        rows = ref.shape[0] // 2
-        return ref.at[pl.ds(which * rows, rows)]
-
-    flows = [
-        Spread(wires, shards[n], slot_of(outs[n]), rows_half if n in small else columns_half, whole)
-        for n in range(count)
-    ]
-    kept = []
-    for n in range(count):
-        copy = pltpu.make_async_copy(shards[n], slot_of(outs[n])(z, g), local_sems.at[n])
-        copy.start()
-        kept.append(copy)
-    spread_all(flows)
-    for copy in kept:
-        copy.wait()
+    copy = pltpu.make_async_copy(shard, out.at[4 * z + chip], local_sem)
+    copy.start()
+    spread_all([Spread(wires, shard, lambda zz, gg: out.at[zz * 4 + gg // 2], columns_half, False)])
+    copy.wait()
     wires.drain()
 
 
-def gather(shards, whole, ident, small=()):
-    count = len(shards)
-    slots = 32 if whole else 16
-    sems = spread_sems(count, whole)
+def gather(shard, ident):
     return pl.pallas_call(
-        partial(gather_kernel, count, small, whole),
-        out_shape=[jax.ShapeDtypeStruct((slots,) + s.shape, s.dtype) for s in shards],
-        in_specs=[pl.BlockSpec(memory_space=HBM)] * count,
-        out_specs=[pl.BlockSpec(memory_space=HBM)] * count,
-        scratch_shapes=[
-            pltpu.SemaphoreType.DMA((sems,)),
-            pltpu.SemaphoreType.DMA((sems,)),
-            pltpu.SemaphoreType.DMA((count,)),
-        ],
-        compiler_params=pltpu.CompilerParams(collective_id=ident, has_side_effects=True),
-        name="gather_%d" % ident,
-    )(*shards)
-
-
-def line_kernel(count, spread, *refs):
-    sources, outs = refs[:count], refs[count : 2 * count]
-    send_sems, recv_sems = refs[2 * count :]
-    z, g, _, _ = here()
-    greet(line_of(z, g))
-    wires = Wires(send_sems, recv_sems)
-    copies = []
-    for k in (2, 1, 3):
-        for source, out in zip(sources, outs):
+        gather_kernel,
+        out_shape=jax.ShapeDtypeStruct((16,) + shard.shape, shard.dtype),
+        in_specs=[LEFT],
+        out_specs=LEFT,
+        scratch_shapes=[sems(spread_sems(False)), sems(spread_sems(False)), pltpu.SemaphoreType.DMA],
+        compiler_params=params(ident),
+        name="gather",
+    )(shard)
+
+
+class Exchange:
+    def __init__(self, wires, pairs):
+        self.wires, self.pairs = wires, pairs
+        self.z, self.g, _, _ = here()
+
+    def first(self):
+        z = self.z
+        self.copies = []
+        for k in (2, 1, 3):
             there = turn(z, k)
-            piece = source if spread else source.at[there]
-            copies.append(wires.send(piece, out.at[z], (there, g)))
-    for source, out in zip(sources, outs):
-        out[z] = source[...] if spread else source[z]
-    for copy in copies:
-        copy.wait_recv()
-    wires.drain()
-
-
-def along_line(arrays, spread, ident):
-    count = len(arrays)
-    shapes = [((LINES,) + a.shape) if spread else a.shape for a in arrays]
-    return pl.pallas_call(
-        partial(line_kernel, count, spread),
-        out_shape=[jax.ShapeDtypeStruct(s, a.dtype) for s, a in zip(shapes, arrays)],
-        in_specs=[pl.BlockSpec(memory_space=pltpu.VMEM)] * count,
-        out_specs=[pl.BlockSpec(memory_space=pltpu.VMEM)] * count,
-        scratch_shapes=[
-            pltpu.SemaphoreType.DMA((3 * count,)),
-            pltpu.SemaphoreType.DMA((3 * count,)),
-        ],
-        compiler_params=pltpu.CompilerParams(collective_id=ident, has_side_effects=True),
-        name="line_%d" % ident,
-    )(*arrays)
+            for source, out in self.pairs:
+                self.copies.append(
+                    self.wires.send(source.at[there], out.at[z], (there, self.g))
+                )
+        for source, out in self.pairs:
+            out[z] = source[z]
+
+    def finish(self):
+        for copy in self.copies:
+            copy.wait_recv()
 
 
 def add_slots(target, source, count):
@@ -254,11 +298,12 @@
 
 
 class Fold:
-    def __init__(self, wires, parts, keep, whole, scratch, out, local_sem):
+    def __init__(self, wires, parts, whole, scratch, out, local_sem):
         self.wires, self.parts, self.whole, self.out = wires, parts, whole, out
         self.held, self.from_sib, self.cx, self.cy, self.fx, self.fy, self.fz = scratch
         self.z, self.g, self.chip, self.core = here()
-        self.load = pltpu.make_async_copy(keep, self.held, local_sem)
+        ours = parts.at[:, :, self.core] if whole else parts
+        self.load = pltpu.make_async_copy(ours, self.held, local_sem)
         self.width = self.held.shape[-1] // 2
 
     def chip_of(self, gy):
@@ -267,10 +312,11 @@
     def half(self, ref, which):
         return ref.at[:, :, pl.ds(which * self.width, self.width)]
 
-    def start(self, to_sibling):
+    def start(self):
         self.load.start()
         if self.whole:
-            self.sib = self.wires.send(to_sibling, self.from_sib, (self.z, sibling(self.g)))
+            theirs = self.parts.at[:, :, 1 - self.core]
+            self.sib = self.wires.send(theirs, self.from_sib, (self.z, sibling(self.g)))
 
     def corner(self):
         self.load.wait()
@@ -351,8 +397,8 @@
     ]
 
 
-def fold_sems(count, whole):
-    return count * ((1 if whole else 0) + 4 + 3)
+def fold_sems(whole):
+    return (1 if whole else 0) + 4 + 3
 
 
 def fold_all(flows):
@@ -366,25 +412,17 @@
 
 def scatter_kernel(count, whole, *refs):
     parts, outs = refs[:count], refs[count : 2 * count]
-    rest = list(refs[2 * count :])
-    send_sems, recv_sems, local_sems = rest[:3]
-    scratch = rest[3:]
+    send_sems, recv_sems, local_sems = refs[2 * count : 2 * count + 3]
+    scratch = refs[2 * count + 3 :]
     z, g, chip, core = here()
-    others = line_of(z, g) + [(z, along_x(g)), (z, along_y(g))]
-    if whole:
-        others.append((z, sibling(g)))
-    greet(others)
+    greet(line_of(z, g) + sides_of(z, g, whole))
     wires = Wires(send_sems, recv_sems)
-    flows = []
-    for n in range(count):
-        ours = parts[n].at[:, :, core] if whole else parts[n]
-        flows.append(
-            Fold(
-                wires, parts[n], ours, whole, scratch[7 * n : 7 * n + 7], outs[n], local_sems.at[n]
-            )
-        )
-    for n, flow in enumerate(flows):
-        flow.start(parts[n].at[:, :, 1 - core] if whole else None)
+    flows = [
+        Fold(wires, parts[n], whole, scratch[7 * n : 7 * n + 7], outs[n], local_sems.at[n])
+        for n in range(count)
+    ]
+    for flow in flows:
+        flow.start()
     fold_all(flows)
     wires.drain()
 
@@ -395,21 +433,14 @@
     scratch = []
     for _ in parts:
         scratch += fold_scratch(rows, cols, whole)
-    sems = fold_sems(count, whole)
+    wires = count * fold_sems(whole)
     return pl.pallas_call(
         partial(scatter_kernel, count, whole),
         out_shape=[jax.ShapeDtypeStruct((rows, cols), F32)] * count,
-        in_specs=[pl.BlockSpec(memory_space=HBM)] * count,
-        out_specs=[pl.BlockSpec(memory_space=pltpu.VMEM)] * count,
-        scratch_shapes=[
-            pltpu.SemaphoreType.DMA((sems,)),
-            pltpu.SemaphoreType.DMA((sems,)),
-            pltpu.SemaphoreType.DMA((count,)),
-        ]
-        + scratch,
-        compiler_params=pltpu.CompilerParams(
-            collective_id=ident, has_side_effects=True, vmem_limit_bytes=60 * 2**20
-        ),
+        in_specs=[LEFT] * count,
+        out_specs=[VMEM] * count,
+        scratch_shapes=[sems(wires), sems(wires), sems(count)] + scratch,
+        compiler_params=params(ident),
         name="scatter_%d" % ident,
     )(*parts)
 
@@ -746,188 +777,261 @@
 GROUP = 4
 
 
-def feed_kernel(
-    up_ref, down_ref, cot_ref, up_out, down_out, cot_out, send_sems, recv_sems, local_sems
-):
-    z, g, chip, core = here()
-    here_chip = 4 * z + chip
-    me = 2 * here_chip + core
-    width = up_out.shape[-1]
+def mates_of(z, chip, core):
     mates = []
     for j in range(1, 16):
-        there = (here_chip + j) % 16
+        there = (4 * z + chip + j) % 16
         mates.append((there // 4, 2 * (there % 4) + core))
-    near = (z, sibling(g))
-    greet(mates + [near])
-    wires = Wires(send_sems, recv_sems)
-
-    def piece(there):
-        return up_ref.at[:, pl.ds(pl.multiple_of(there * width, 128), width)]
-
-    kept = [
-        pltpu.make_async_copy(piece(here_chip), up_out.at[me], local_sems.at[0]),
-        pltpu.make_async_copy(down_ref, down_out.at[core], local_sems.at[1]),
-        pltpu.make_async_copy(cot_ref, cot_out.at[here_chip], local_sems.at[2]),
-    ]
-    for copy in kept:
-        copy.start()
-    flow = Spread(
-        wires, cot_ref, lambda zz, gg: cot_out.at[zz * 4 + gg // 2], columns_half, False
-    )
-    flow.first()
-    down = wires.send(down_ref, down_out.at[core], near)
-    given = [wires.send(piece(here_chip), up_out.at[me], near)]
-    moved = []
-    for j in range(1, 16):
-        moved.append(wires.send(piece((here_chip + j) % 16), up_out.at[me], mates[j - 1]))
-    flow.corner(0)
-    for k in (1, 3, 2):
-        flow.column(k)
-    for k in (1, 3, 2):
-        flow.corner(k)
-    for j in range(1, 16):
-        moved[j - 1].wait_recv()
-        origin = 2 * ((here_chip + 16 - j) % 16) + core
-        given.append(wires.send(up_out.at[origin], up_out.at[origin], near))
-    for k in (0, 1, 3, 2):
-        flow.last(k)
-    down.wait_recv()
-    for copy in given:
-        copy.wait_recv()
-    for copy in kept:
-        copy.wait()
-    wires.drain()
-
-
-def feed(w_up, w_down, cotangent):
-    rows, width = w_up.shape
-    sems = spread_sems(1, False) + 1 + 16 + 15
-    return pl.pallas_call(
-        feed_kernel,
-        out_shape=[
-            jax.ShapeDtypeStruct((32, rows, width // 16), BF16),
-            jax.ShapeDtypeStruct((2,) + w_down.shape, BF16),
-            jax.ShapeDtypeStruct((16,) + cotangent.shape, BF16),
-        ],
-        in_specs=[pl.BlockSpec(memory_space=HBM)] * 3,
-        out_specs=[pl.BlockSpec(memory_space=HBM)] * 3,
-        scratch_shapes=[
-            pltpu.SemaphoreType.DMA((sems,)),
-            pltpu.SemaphoreType.DMA((sems,)),
-            pltpu.SemaphoreType.DMA((3,)),
-        ],
-        compiler_params=pltpu.CompilerParams(collective_id=1, has_side_effects=True),
-        name="feed",
-    )(w_up, w_down, cotangent)
-
-
-def give_back_kernel(
-    up_ref,
-    down_ref,
-    up_out,
+    return mates
+
+
+class GiveBack:
+    def __init__(self, wires, up_ref, down_ref, up_out, down_out, scratch, local_sems):
+        self.wires, self.up_out, self.down_out = wires, up_out, down_out
+        self.up_held, self.up_near, self.down_near = scratch
+        self.z, self.g, self.chip, self.core = here()
+        self.up_ref, self.down_ref = up_ref, down_ref
+        self.load_up = pltpu.make_async_copy(
+            up_ref.at[:, self.core], self.up_held, local_sems.at[0]
+        )
+        self.load_down = pltpu.make_async_copy(
+            down_ref.at[self.core], down_out, local_sems.at[1]
+        )
+
+    def start(self):
+        near = (self.z, sibling(self.g))
+        self.load_up.start()
+        self.load_down.start()
+        self.up = self.wires.send(self.up_ref.at[:, 1 - self.core], self.up_near, near)
+        self.down = self.wires.send(self.down_ref.at[1 - self.core], self.down_near, near)
+
+    def columns(self):
+        self.load_up.wait()
+        self.up.wait_recv()
+        add_slots(self.up_held, self.up_near, 16)
+        here_chip = 4 * self.z + self.chip
+        self.moved = []
+        for j, mate in enumerate(mates_of(self.z, self.chip, self.core)):
+            there = (here_chip + j + 1) % 16
+            self.moved.append(
+                self.wires.send(self.up_held.at[there], self.up_out.at[here_chip], mate)
+            )
+        self.up_out[here_chip] = self.up_held[here_chip]
+
+    def rows(self):
+        self.load_down.wait()
+        self.down.wait_recv()
+        rows = self.down_out.shape[0] // 8
+
+        @pl.loop(0, 8)
+        def _(n):
+            block = pl.ds(pl.multiple_of(n * rows, 8), rows)
+            self.down_out[block] = self.down_out[block] + self.down_near[block]
+
+    def finish(self):
+        for copy in self.moved:
+            copy.wait_recv()
+
+
+def turn_kernel(
+    grad,
+    terms,
+    down_part,
+    up_grad,
+    down_grad,
+    grad_out,
+    terms_out,
     down_out,
+    up_grad_out,
+    down_grad_out,
+    send_sems,
+    recv_sems,
+    local_sems,
     up_held,
     up_near,
     down_near,
-    send_sems,
-    recv_sems,
-    local_sems,
+    *fold,
 ):
     z, g, chip, core = here()
-    here_chip = 4 * z + chip
-    mates = []
-    for j in range(1, 16):
-        there = (here_chip + j) % 16
-        mates.append((there // 4, 2 * (there % 4) + core))
-    near = (z, sibling(g))
-    greet(mates + [near])
+    greet(mates_of(z, chip, core) + [(z, sibling(g))])
     wires = Wires(send_sems, recv_sems)
-    load_up = pltpu.make_async_copy(up_ref.at[:, core], up_held, local_sems.at[0])
-    load_down = pltpu.make_async_copy(down_ref.at[core], down_out, local_sems.at[1])
-    load_up.start()
-    load_down.start()
-    up = wires.send(up_ref.at[:, 1 - core], up_near, near)
-    down = wires.send(down_ref.at[1 - core], down_near, near)
-    load_up.wait()
-    up.wait_recv()
-    add_slots(up_held, up_near, 16)
-    moved = []
-    for j in range(1, 16):
-        there = (here_chip + j) % 16
-        moved.append(wires.send(up_held.at[there], up_out.at[here_chip], mates[j - 1]))
-    up_out[here_chip] = up_held[here_chip]
-    load_down.wait()
-    down.wait_recv()
-    rows = down_out.shape[0] // 8
-
-    @pl.loop(0, 8)
-    def _(n):
-        block = pl.ds(pl.multiple_of(n * rows, 8), rows)
-        down_out[block] = down_out[block] + down_near[block]
-
-    for copy in moved:
-        copy.wait_recv()
+    lines = [
+        Line(wires, grad, lambda zz: grad_out.at[zz]),
+        Line(wires, terms, lambda zz: terms_out.at[zz]),
+    ]
+    back = GiveBack(
+        wires,
+        up_grad,
+        down_grad,
+        up_grad_out,
+        down_grad_out,
+        (up_held, up_near, down_near),
+        local_sems,
+    )
+    flow = Fold(wires, down_part, False, fold, down_out, local_sems.at[2])
+    flow.start()
+    for line in lines:
+        line.first()
+    back.start()
+    flow.corner()
+    grad_out[z] = grad[...]
+    terms_out[z] = terms[...]
+    back.columns()
+    flow.sides()
+    for step in range(3):
+        for line in lines:
+            line.take(step)
+    back.rows()
+    flow.line()
+    flow.finish()
+    back.finish()
     wires.drain()
 
 
-def give_back(up_part, down_part):
-    rows, width = up_part.shape[-2:]
-    down_shape = down_part.shape[1:]
+def turn_back(grad, terms, down_part, up_grad, down_grad):
+    rows, width = up_grad.shape[-2:]
+    down_shape = down_grad.shape[1:]
+    latent_rows, model_width = grad.shape
+    wires = 2 * LINE_SEMS + fold_sems(False) + 17
     return pl.pallas_call(
-        give_back_kernel,
+        turn_kernel,
         out_shape=[
+            jax.ShapeDtypeStruct((LINES,) + grad.shape, BF16),
+            jax.ShapeDtypeStruct((LINES,) + terms.shape, F32),
+            jax.ShapeDtypeStruct(grad.shape, F32),
             jax.ShapeDtypeStruct((16, rows, width), BF16),
             jax.ShapeDtypeStruct(down_shape, F32),
         ],
-        in_specs=[pl.BlockSpec(memory_space=HBM)] * 2,
-        out_specs=[pl.BlockSpec(memory_space=pltpu.VMEM)] * 2,
+        in_specs=[VMEM, VMEM, LEFT, LEFT, LEFT],
+        out_specs=[VMEM] * 5,
         scratch_shapes=[
+            sems(wires),
+            sems(wires),
+            sems(3),
             pltpu.VMEM((16, rows, width), BF16),
             pltpu.VMEM((16, rows, width), BF16),
             pltpu.VMEM(down_shape, F32),
-            pltpu.SemaphoreType.DMA((17,)),
-            pltpu.SemaphoreType.DMA((17,)),
-            pltpu.SemaphoreType.DMA((2,)),
+        ]
+        + fold_scratch(latent_rows, model_width, False),
+        compiler_params=params(2),
+        name="turn_back",
+    )(grad, terms, down_part, up_grad, down_grad)
+
+
+def queries_kernel(parts, weight_part, out, weight_out, send_sems, recv_sems, local_sem, *fold):
+    z, g, _, _ = here()
+    greet(line_of(z, g) + sides_of(z, g, True))
+    wires = Wires(send_sems, recv_sems)
+    exchange = Exchange(wires, [(parts, out)])
+    flow = Fold(wires, weight_part, True, fold, weight_out, local_sem)
+    flow.start()
+    exchange.first()
+    fold_all([flow])
+    exchange.finish()
+    wires.drain()
+
+
+def queries_home(parts, weight_part):
+    rows, cols = weight_part.shape[-2:]
+    wires = fold_sems(True) + 3
+    return pl.pallas_call(
+        queries_kernel,
+        out_shape=[
+            jax.ShapeDtypeStruct(parts.shape, BF16),
+            jax.ShapeDtypeStruct((rows, cols), F32),
         ],
-        compiler_params=pltpu.CompilerParams(collective_id=2, has_side_effects=True),
-        name="give_back",
-    )(up_part, down_part)
-
-
-def total_kernel(mine, out, sums, got, send_sems, recv_sems):
+        in_specs=[VMEM, LEFT],
+        out_specs=[VMEM, VMEM],
+        scratch_shapes=[sems(wires), sems(wires), pltpu.SemaphoreType.DMA]
+        + fold_scratch(rows, cols, True),
+        compiler_params=params(3),
+        name="queries_home",
+    )(parts, weight_part)
+
+
+class Total:
+    def __init__(self, wires, mine, out, sums, got):
+        self.wires, self.out, self.sums, self.got = wires, out, sums, got
+        self.z, self.g, _, _ = here()
+        self.source = mine
+        self.step = 0
+
+    def push(self):
+        sides = [sibling(self.g), along_x(self.g), along_y(self.g)]
+        if self.step < 3:
+            self.copies = [
+                self.wires.send(self.source, self.got.at[self.step], (self.z, sides[self.step]))
+            ]
+        else:
+            self.copies = [
+                self.wires.send(self.source, self.got.at[3 + k], device)
+                for k, device in enumerate(line_of(self.z, self.g))
+            ]
+
+    def pull(self):
+        for copy in self.copies:
+            copy.wait_recv()
+        if self.step < 3:
+            self.sums[self.step] = self.source[...] + self.got[self.step]
+            self.source = self.sums.at[self.step]
+            self.step += 1
+        else:
+            self.out[...] = self.source[...] + self.got[3] + self.got[4] + self.got[5]
+
+
+def ending_kernel(count, *refs):
+    parts, small, outs = refs[:count], refs[count], refs[count + 1 : 2 * count + 1]
+    small_out, send_sems, recv_sems, local_sems, small_sums, small_got = refs[
+        2 * count + 1 : 2 * count + 7
+    ]
+    scratch = refs[2 * count + 7 :]
     z, g, _, _ = here()
-    sides = [(z, sibling(g)), (z, along_x(g)), (z, along_y(g))]
-    line = line_of(z, g)
-    greet(sides + line)
+    greet(line_of(z, g) + sides_of(z, g, True))
     wires = Wires(send_sems, recv_sems)
-    source = mine
-    for n, side in enumerate(sides):
-        copy = wires.send(source, got.at[n], side)
-        copy.wait_recv()
-        sums[n] = source[...] + got[n]
-        source = sums.at[n]
-    copies = [wires.send(source, got.at[3 + k], line[k]) for k in range(3)]
-    for copy in copies:
-        copy.wait_recv()
-    out[...] = source[...] + got[3] + got[4] + got[5]
+    flows = [
+        Fold(wires, parts[n], True, scratch[7 * n : 7 * n + 7], outs[n], local_sems.at[n])
+        for n in range(count)
+    ]
+    total = Total(wires, small, small_out, small_sums, small_got)
+    total.push()
+    for flow in flows:
+        flow.start()
+    stages = ("corner", "sides", "line", "finish")
+    for tick in range(count + len(stages) - 1):
+        for n in range(len(stages)):
+            if 0 <= tick - n < count:
+                getattr(flows[tick - n], stages[n])()
+        if tick < 4:
+            total.pull()
+            if tick < 3:
+                total.push()
     wires.drain()
 
 
-def total(array):
+def ending(parts, small):
+    count = len(parts)
+    rows, cols = parts[0].shape[-2:]
+    scratch = []
+    for _ in parts:
+        scratch += fold_scratch(rows, cols, True)
+    wires = count * fold_sems(True) + 6
     return pl.pallas_call(
-        total_kernel,
-        out_shape=jax.ShapeDtypeStruct(array.shape, F32),
-        in_specs=[pl.BlockSpec(memory_space=pltpu.VMEM)],
-        out_specs=pl.BlockSpec(memory_space=pltpu.VMEM),
+        partial(ending_kernel, count),
+        out_shape=[jax.ShapeDtypeStruct((rows, cols), F32)] * count
+        + [jax.ShapeDtypeStruct(small.shape, F32)],
+        in_specs=[LEFT] * count + [VMEM],
+        out_specs=[VMEM] * (count + 1),
         scratch_shapes=[
-            pltpu.VMEM((3,) + array.shape, F32),
-            pltpu.VMEM((6,) + array.shape, F32),
-            pltpu.SemaphoreType.DMA((6,)),
-            pltpu.SemaphoreType.DMA((6,)),
-        ],
-        compiler_params=pltpu.CompilerParams(collective_id=3, has_side_effects=True),
-        name="total",
-    )(array)
+            sems(wires),
+            sems(wires),
+            sems(count),
+            pltpu.VMEM((3,) + small.shape, F32),
+            pltpu.VMEM((6,) + small.shape, F32),
+        ]
+        + scratch,
+        compiler_params=params(4),
+        name="ending",
+    )(*parts, small)
 
 
 def head_masks(rows, width, head_size):
@@ -984,80 +1088,439 @@
     return out
 
 
-def forward_kernel(
-    scale,
-    item_ref,
-    table_ref,
-    key_ref,
-    value_ref,
-    valid_ref,
-    own_query_ref,
-    own_key_ref,
-    own_value_ref,
-    weighted_ref,
-    stats_ref,
-    own_weighted_ref,
-    own_stats_ref,
-    sums,
-):
-    items, rows, width = table_ref.shape
-    frames = valid_ref.shape[0]
-    patches = valid_ref.shape[2]
-    groups = H // GROUP
-    span = width // groups
+def multiply(left, right, out, tile):
+    @pl.loop(0, right.shape[1] // tile)
+    def _(n):
+        cols = pl.ds(pl.multiple_of(n * tile, 128), tile)
+        out[:, cols] = jnp.dot(left[...], right[:, cols], preferred_element_type=F32).astype(BF16)
+
+
+def assemble(smalls, out):
+    count, rows, lanes = smalls.shape
+    shard = out.shape[1] // count
+    block = 8
+    row = lax.broadcasted_iota(jnp.int32, (block * lanes, block * shard), 0)
+    col = lax.broadcasted_iota(jnp.int32, (block * lanes, block * shard), 1)
+    lane = row % lanes
+    chosen = ((row // lanes) * shard + lane == col) & (lane < shard)
+    place = jnp.where(chosen, 1.0, 0.0).astype(BF16)
+    for n in range(count // block):
+        pieces = jnp.concatenate([smalls[n * block + d] for d in range(block)], axis=1)
+        out[:, n * block * shard : (n + 1) * block * shard] = jnp.dot(
+            pieces.astype(BF16), place, preferred_element_type=F32
+        )
+
+
+def up_places(z, chip):
+    places = []
+    for dz in range(LINES):
+        for dx, dy in ((0, 0), (1, 0), (0, 1), (1, 1)):
+            if dz or dx or dy:
+                x, y = chip % 2, chip // 2
+                there = (y + dy) % 2 * 2 + (x + dx) % 2
+                places.append(((turn(z, dz), there), (turn(z, LINES - dz) if dz else z, there)))
+    return places
+
+
+def opening_kernel(scale, *refs):
+    (
+        small_ref,
+        key_shard,
+        value_shard,
+        query_shard,
+        out_shard,
+        latents_ref,
+        up_ref,
+        down_ref,
+        cot_ref,
+        media_ref,
+        valid_ref,
+        times_ref,
+        item_ref,
+        tables_out,
+        counts_out,
+        key_weight_out,
+        value_weight_out,
+        query_weight_out,
+        out_weight_out,
+        up_out,
+        down_out,
+        cot_out,
+        normed_out,
+        keys_out,
+        values_out,
+        table_out,
+        got_weighted,
+        got_stats,
+        own_weighted,
+        own_stats,
+        send_sems,
+        recv_sems,
+        local_sems,
+        smalls,
+        key_weight,
+        value_weight,
+        query_weight,
+        line_latents,
+        line_normed,
+        normed,
+        keys,
+        values,
+        table,
+        time_rows,
+        sums,
+        weighted,
+        stats,
+    ) = refs
+    z, g, chip, core = here()
+    here_chip = 4 * z + chip
+    me = 2 * here_chip + core
+    items, rows, width = line_latents.shape
+    frames, _, patches = valid_ref.shape
+    shard = key_shard.shape[0]
+    span = width // (H // GROUP)
+    up_width = up_out.shape[-1]
+    near = (z, sibling(g))
+    places = up_places(z, chip)
+    greet([(there[0], 2 * there[1] + core) for there, _ in places] + [near])
+    wires = Wires(send_sems, recv_sems)
     masks = head_masks(rows, span, span // GROUP)
     lane = lax.broadcasted_iota(jnp.int32, (rows, 128), 1)
-    sums[...] = jnp.zeros_like(sums)
-    stats_ref[...] = jnp.zeros_like(stats_ref)
-    stats = jnp.zeros((rows, 128), F32)
-    for group in range(groups):
-        cols = pl.ds(group * span, span)
-        weighted, heads = attend(
-            own_query_ref[:, cols], own_key_ref[:, cols], own_value_ref[:, cols], None, scale, masks
+    local = []
+
+    def keep(source, target):
+        copy = pltpu.make_async_copy(source, target, local_sems.at[len(local)])
+        copy.start()
+        local.append(copy)
+        return copy
+
+    def rows_of(ref):
+        return lambda zz, gg: ref.at[pl.ds(pl.multiple_of((zz * 8 + gg) * shard, 16), shard)]
+
+    def piece(place):
+        return up_ref.at[:, pl.ds(pl.multiple_of((4 * place[0] + place[1]) * up_width, 128), up_width)]
+
+    def whole(source, slot):
+        return Spread(wires, source, slot, columns_half, True), keep(source, slot(z, g))
+
+    def small_slot(zz, gg):
+        return smalls.at[zz * 8 + gg]
+
+    small = Spread(wires, small_ref, small_slot, rows_half, True)
+    small_kept = keep(small_ref, small_slot(z, g))
+    key, key_kept = whole(key_shard, rows_of(key_weight))
+    value, value_kept = whole(value_shard, rows_of(value_weight))
+    query, query_kept = whole(query_shard, rows_of(query_weight))
+    out, out_kept = whole(out_shard, rows_of(out_weight_out))
+    cot = Spread(wires, cot_ref, lambda zz, gg: cot_out.at[zz * 4 + gg // 2], columns_half, False)
+    line = Line(wires, latents_ref, lambda zz: line_latents.at[zz])
+    exchange = Exchange(wires, [(weighted, got_weighted), (stats, got_stats)])
+    line_kept = keep(latents_ref, line_latents.at[z])
+    late = [
+        out_kept,
+        keep(cot_ref, cot_out.at[here_chip]),
+        keep(piece((z, chip)), up_out.at[me]),
+        keep(down_ref, down_out.at[core]),
+    ]
+    prompt = len(local)
+    moved, given, down = [], [], []
+    chunk = 32
+
+    def normalise(first, last):
+        @pl.loop(first, last)
+        def _(n):
+            block = pl.ds(pl.multiple_of(n * chunk, chunk), chunk)
+            frame = n // (patches // chunk)
+            row = media_ref[block].astype(F32) + time_rows[pl.ds(frame, 1)]
+            normed[block] = layer_norm(row, tables_out[8:9]).astype(BF16)
+
+    def normalise_latents():
+        gain = tables_out[9:10]
+        line_kept.wait()
+        for item in range(items):
+
+            @pl.loop(0, rows // chunk)
+            def _(n):
+                block = pl.ds(pl.multiple_of(n * chunk, chunk), chunk)
+                row = line_latents[item, block].astype(F32)
+                line_normed[item, block] = layer_norm(row, gain).astype(BF16)
+
+        normed[frames * patches :] = line_normed[z]
+
+    def tabulate():
+        small_kept.wait()
+        assemble(smalls, tables_out)
+        counts = smalls[0, 8:]
+        for n in range(1, smalls.shape[0]):
+            counts = counts + smalls[n, 8:]
+        counts_out[...] = counts
+        time_rows[...] = jnp.dot(
+            times_ref[...], tables_out[...].astype(BF16), preferred_element_type=F32
         )
-        own_weighted_ref[:, cols] = weighted
-        stats = stats + put_heads(heads, group, lane)
-    own_stats_ref[...] = stats
-
-    @pl.loop(0, frames)
-    def _(frame):
-        item = item_ref[frame]
-        block = pl.ds(pl.multiple_of(frame * patches, patches), patches)
-        valid = valid_ref[frame]
-        stats = jnp.zeros((rows, 128), F32)
-        for group in range(groups):
-            cols = pl.ds(group * span, span)
-            weighted, heads = attend(
-                table_ref[item, :, cols],
-                key_ref[block, cols],
-                value_ref[block, cols],
-                valid,
-                scale,
-                masks,
+
+    def project_keys():
+        key_kept.wait()
+        keep(key_weight, key_weight_out)
+        keep(normed, normed_out)
+        multiply(normed, key_weight, keys, span)
+        keep(keys, keys_out)
+
+    def project_values():
+        value_kept.wait()
+        keep(value_weight, value_weight_out)
+        multiply(normed, value_weight, values, span)
+        keep(values, values_out)
+
+    def project_queries():
+        query_kept.wait()
+        keep(query_weight, query_weight_out)
+
+        @pl.loop(0, width // span)
+        def _(n):
+            cols = pl.ds(pl.multiple_of(n * span, 128), span)
+            for item in range(items):
+                table[item, :, cols] = jnp.dot(
+                    line_normed[item], query_weight[:, cols], preferred_element_type=F32
+                ).astype(BF16)
+
+        keep(table, table_out)
+
+    def attend_own():
+        sums[...] = jnp.zeros_like(sums)
+        stats[...] = jnp.zeros_like(stats)
+        last = slice(frames * patches, frames * patches + rows)
+        own = jnp.zeros((rows, 128), F32)
+        for group in range(H // GROUP):
+            cols = slice(group * span, (group + 1) * span)
+            part, heads = attend(
+                table[z, :, cols], keys[last, cols], values[last, cols], None, scale, masks
             )
-            sums[item, :, cols] += weighted
-            stats = stats + put_heads(heads, group, lane)
-        stats_ref[item] += stats
-
-    weighted_ref[...] = sums[...].astype(BF16)
-
-
-def forward(item_index, table, keys, values, valid, own, scale):
-    items, rows, width = table.shape
-    vmem = pl.BlockSpec(memory_space=pltpu.VMEM)
+            own_weighted[:, cols] = part
+            own = own + put_heads(heads, group, lane)
+        own_stats[...] = own
+
+    def attend_frames(first, last):
+        @pl.loop(first, last)
+        def _(frame):
+            block = pl.ds(pl.multiple_of(frame * patches, patches), patches)
+            valid = valid_ref[frame]
+            found = jnp.zeros((rows, 128), F32)
+            for group in range(H // GROUP):
+                cols = slice(group * span, (group + 1) * span)
+                chosen = item_ref[frame, 0] * table[0, :, cols].astype(F32)
+                for item in range(1, items):
+                    chosen = chosen + item_ref[frame, item] * table[item, :, cols].astype(F32)
+                part, heads = attend(
+                    chosen.astype(BF16), keys[block, cols], values[block, cols], valid, scale, masks
+                )
+                found = found + put_heads(heads, group, lane)
+                for item in range(items):
+                    sums[item, :, cols] += item_ref[frame, item] * part
+            for item in range(items):
+                stats[item] += item_ref[frame, item] * found
+
+    def down_first():
+        down.append(wires.send(down_ref, down_out.at[core], near))
+
+    def up_first():
+        given.append(wires.send(piece((z, chip)), up_out.at[me], near))
+        for there, _ in places:
+            moved.append(
+                wires.send(piece(there), up_out.at[me], (there[0], 2 * there[1] + core))
+            )
+
+    def up_last():
+        for n, (_, origin) in enumerate(places):
+            moved[n].wait_recv()
+            held = up_out.at[2 * (4 * origin[0] + origin[1]) + core]
+            given.append(wires.send(held, held, near))
+        for copy in given:
+            copy.wait_recv()
+
+    def sums_first():
+        weighted[...] = sums[...].astype(BF16)
+        exchange.first()
+
+    key.first()
+    small.first()
+    query.first()
+    key.column(0)
+    small.corner_y(0)
+    small.column(0)
+    key.column(1)
+    down_first()
+    query.corner_x(0)
+    value.first()
+    query.column(0)
+    query.column(1)
+    key.corner_y(1)
+    key.corner_x(1)
+    value.column(0)
+    key.column(2)
+    small.corner_x(1)
+    small.corner_y(1)
+    value.corner_y(0)
+    query.corner_y(2)
+    line.first()
+    small.corner_x(0)
+    query.corner_y(0)
+    value.corner_y(1)
+    key.corner_y(0)
+    query.corner_x(1)
+    small.column(1)
+    query.corner_y(1)
+    small.column(2)
+    key.corner_x(2)
+    key.corner_x(0)
+    cot.first()
+    value.column(1)
+    value.corner_x(0)
+    key.corner_x(3)
+    value.column(2)
+    small.last(0)
+    key.last(1)
+    key.corner_y(3)
+    small.corner_y(2)
+    value.corner_x(1)
+    query.last(0)
+    query.corner_x(2)
+    small.corner_x(2)
+    key.last(0)
+    small.corner_x(3)
+    out.first()
+    small.corner_y(3)
+    query.last(1)
+    value.corner_y(3)
+    small.last(1)
+    value.corner_x(2)
+    small.last(2)
+    key.corner_y(2)
+    query.column(2)
+    small.last(3)
+    value.last(0)
+    query.last(2)
+    key.last(3)
+    small.finish()
+    line.take(0)
+    down[0].wait_recv()
+    value.last(1)
+    tabulate()
+    out.column(0)
+    query.corner_x(3)
+    query.corner_y(3)
+    value.corner_x(3)
+    value.corner_y(2)
+    line.take(1)
+    normalise(0, 8)
+    cot.column(0)
+    cot.corner_y(0)
+    line.take(2)
+    up_first()
+    out.column(1)
+    query.last(3)
+    cot.column(1)
+    out.corner_y(0)
+    normalise_latents()
+    query.finish()
+    value.last(3)
+    project_queries()
+    value.last(2)
+    key.last(2)
+    cot.corner_x(0)
+    normalise(8, 16)
+    out.column(2)
+    value.finish()
+    cot.corner_y(1)
+    project_values()
+    key.finish()
+    project_keys()
+    cot.corner_x(1)
+    attend_own()
+    attend_frames(0, frames // 2)
+    cot.corner_y(2)
+    attend_frames(frames // 2, frames)
+    sums_first()
+    out.corner_y(2)
+    out.corner_x(2)
+    cot.corner_x(2)
+    cot.column(2)
+    exchange.finish()
+    out.corner_y(3)
+    out.corner_x(1)
+    cot.corner_x(3)
+    cot.last(2)
+    cot.corner_y(3)
+    cot.last(0)
+    out.corner_y(1)
+    cot.last(1)
+    out.corner_x(3)
+    out.last(1)
+    cot.last(3)
+    out.corner_x(0)
+    out.last(2)
+    out.last(0)
+    up_last()
+    out.last(3)
+    out.finish()
+    for copy in late + local[prompt:]:
+        copy.wait()
+    wires.drain()
+
+
+def opening(scale, small, weights, latents, w_up, w_down, cotangent, media, valid, times, items):
+    rows, width = latents.shape
+    shard = weights[0].shape[0]
+    up_rows, up_width = w_up.shape
+    all_rows = media.shape[0] + rows
+    wires = 5 * spread_sems(True) + spread_sems(False) + LINE_SEMS + 31 + 1 + 6
+    square = jax.ShapeDtypeStruct((width, width), BF16)
+    table = jax.ShapeDtypeStruct((LINES, rows, width), BF16)
+    keys = jax.ShapeDtypeStruct((all_rows, width), BF16)
     return pl.pallas_call(
-        partial(forward_kernel, scale),
+        partial(opening_kernel, scale),
         out_shape=[
-            jax.ShapeDtypeStruct((items, rows, width), BF16),
-            jax.ShapeDtypeStruct((items, rows, 128), F32),
+            jax.ShapeDtypeStruct((16, width), F32),
+            jax.ShapeDtypeStruct((8, 128), F32),
+            square,
+            square,
+            square,
+            square,
+            jax.ShapeDtypeStruct((32, up_rows, up_width // 16), BF16),
+            jax.ShapeDtypeStruct((2,) + w_down.shape, BF16),
+            jax.ShapeDtypeStruct((16,) + cotangent.shape, BF16),
+            keys,
+            keys,
+            keys,
+            table,
+            table,
+            jax.ShapeDtypeStruct((LINES, rows, 128), F32),
             jax.ShapeDtypeStruct((rows, width), F32),
             jax.ShapeDtypeStruct((rows, 128), F32),
         ],
-        in_specs=[pl.BlockSpec(memory_space=pltpu.SMEM)] + [vmem] * 7,
-        out_specs=[vmem] * 4,
-        scratch_shapes=[pltpu.VMEM((items, rows, width), F32)],
-        name="attention_forward",
-    )(item_index, table, keys, values, valid, *own)
+        in_specs=[LEFT] * 9 + [VMEM] * 3 + [pl.BlockSpec(memory_space=pltpu.SMEM)],
+        out_specs=[VMEM] * 2 + [LEFT] * 11 + [VMEM] * 4,
+        scratch_shapes=[
+            sems(wires),
+            sems(wires),
+            sems(16),
+            pltpu.VMEM((32,) + small.shape, F32),
+            pltpu.VMEM((width, width), BF16),
+            pltpu.VMEM((width, width), BF16),
+            pltpu.VMEM((width, width), BF16),
+            pltpu.VMEM((LINES, rows, width), BF16),
+            pltpu.VMEM((LINES, rows, width), BF16),
+            pltpu.VMEM((all_rows, width), BF16),
+            pltpu.VMEM((all_rows, width), BF16),
+            pltpu.VMEM((all_rows, width), BF16),
+            pltpu.VMEM((LINES, rows, width), BF16),
+            pltpu.VMEM((8, width), F32),
+            pltpu.VMEM((LINES, rows, width), F32),
+            pltpu.VMEM((LINES, rows, width), BF16),
+            pltpu.VMEM((LINES, rows, 128), F32),
+        ],
+        compiler_params=params(0),
+        name="opening",
+    )(small, *weights, latents, w_up, w_down, cotangent, media, valid, times, items)
 
 
 def repel(queries, grads, keys, values, valid, shift, slope, scale, masks):
@@ -1343,54 +1806,63 @@
         axis=0,
     )
     small = jnp.pad(small, ((0, 0), (0, 128 - shard)))
-    smalls, full_key, full_value, full_query, full_out = gather(
-        [small, w_key, w_value, w_query, w_out], True, 0, small=(0,)
-    )
-    full_key, full_value, full_query, full_out = (
-        w.reshape(width, width) for w in (full_key, full_value, full_query, full_out)
-    )
-    tables = jnp.swapaxes(smalls[:, :11, :shard], 0, 1).reshape(11, width)
+    times = (time_index[:, None] == jnp.arange(16, dtype=jnp.int32)[None, :]).astype(BF16)
+    times = jnp.pad(times, ((0, 8 - frames), (0, 0)))
+    items = (item_index[:, None] == jnp.arange(LINES, dtype=jnp.int32)[None, :]).astype(F32)
+    valid_rows = valid.reshape(frames, 1, patches)
+    (
+        tables,
+        counts,
+        full_key,
+        full_value,
+        full_query,
+        full_out,
+        up_cols,
+        down_rows,
+        cot_rows,
+        normed,
+        keys,
+        values,
+        table,
+        got_weighted,
+        got_stats,
+        own_weighted,
+        own_stats,
+    ) = opening(
+        scale,
+        small,
+        (w_key, w_value, w_query, w_out),
+        latents,
+        w_up,
+        w_down,
+        cotangent,
+        media,
+        valid_rows,
+        times,
+        items,
+    )
     full_time = tables[:8].astype(BF16)
     full_media_gain, full_latent_gain, full_ffn_gain = tables[8:9], tables[9:10], tables[10:11]
-    valid_total = jnp.sum(smalls[:, 11, 0])
+    valid_total = counts[3, 0]
     coefficient = ENTROPY_WEIGHT * (valid.shape[0] * lax.axis_size(AXES)) / valid_total
-    up_cols, down_rows, cot_rows = feed(w_up, w_down, cotangent)
     up_cols = up_cols.reshape(width, -1)
     down_rows = down_rows.reshape(-1, width)
     cot_rows = cot_rows.reshape(-1, width)
-
-    time_onehot = (
-        time_index[:, None] == jnp.arange(full_time.shape[0], dtype=jnp.int32)[None, :]
-    ).astype(F32)
-    time_rows = product(time_onehot.astype(BF16), full_time)
+    time_onehot = times[:frames, :8].astype(F32)
+    time_rows = product(times[:frames, :8], full_time)
     media_in = (
         media.astype(F32).reshape(frames, patches, width) + time_rows[:, None, :]
     ).reshape(-1, width)
-    media_normed = layer_norm(media_in, full_media_gain).astype(BF16)
-    media_key = product(media_normed, full_key).astype(BF16)
-    media_value = product(media_normed, full_value).astype(BF16)
     latent_in = latents.astype(F32)
-    latent_normed = layer_norm(latent_in, full_latent_gain).astype(BF16)
-    own_query = product(latent_normed, full_query).astype(BF16)
-    own_key = product(latent_normed, full_key).astype(BF16)
-    own_value = product(latent_normed, full_value).astype(BF16)
-    valid_rows = valid.reshape(frames, 1, patches)
-    (table,) = along_line([own_query], True, 4)
-    weighted, stats, own_weighted, own_stats = forward(
-        item_index,
-        table,
-        media_key,
-        media_value,
-        valid_rows,
-        (own_query, own_key, own_value),
-        scale,
-    )
-    got_weighted, got_stats = along_line([weighted, stats], False, 5)
+    media_rows = media.shape[0]
+    media_normed, latent_normed = normed[:media_rows], normed[media_rows:]
+    media_key, own_key = keys[:media_rows], keys[media_rows:]
+    media_value, own_value = values[:media_rows], values[media_rows:]
+    own_query = lax.dynamic_index_in_dim(table, column, 0, keepdims=False)
     attention, attn_low, sums, middle, ffn_normed = settle(
         got_weighted, got_stats, own_weighted, own_stats, full_out, latents, full_ffn_gain
     )
-    (ffn_rows,) = gather([ffn_normed], False, 6)
-    ffn_rows = ffn_rows.reshape(-1, width)
+    ffn_rows = gather(ffn_normed, 5).reshape(-1, width)
     up_rows = product(ffn_rows, up_cols)
     hidden = jax.nn.gelu(up_rows, approximate=False).astype(BF16)
     hidden_grad = inner_last(cot_rows, down_rows)
@@ -1399,16 +1871,9 @@
     normed_part = inner_last(up_grad, up_cols).astype(BF16)
     down_part = product(hidden, down_rows).astype(BF16)
     shape = (LINES, PLANE, latent_rows, width)
-    ffn_normed_grad, down_sum = scatter(
-        [normed_part.reshape(shape), down_part.reshape(shape)], False, 7
-    )
-    new_latents = (middle + down_sum).astype(BF16)
+    (ffn_normed_grad,) = scatter([normed_part.reshape(shape)], False, 6)
     up_grad_part = inner_first(ffn_rows, up_grad).astype(BF16)
     down_grad_part = inner_first(hidden, cot_rows)
-    shard_up, shard_down = give_back(
-        up_grad_part.reshape(16, 2, shard, -1), down_grad_part.reshape(2, -1, width)
-    )
-    shard_up = jnp.swapaxes(shard_up, 0, 1).reshape(shard, -1).astype(F32)
     middle_grad, middle_low, grad_ffn_gain, weighted_grad, terms = unsettle(
         ffn_normed_grad,
         middle,
@@ -1419,7 +1884,15 @@
         sums,
         coefficient.reshape(1, 1),
     )
-    grad_table, terms_table = along_line([weighted_grad, terms], True, 8)
+    grad_table, terms_table, down_sum, shard_up, shard_down = turn_back(
+        weighted_grad,
+        terms,
+        down_part.reshape(shape),
+        up_grad_part.reshape(16, 2, shard, -1),
+        down_grad_part.reshape(2, -1, width),
+    )
+    new_latents = (middle + down_sum).astype(BF16)
+    shard_up = jnp.swapaxes(shard_up, 0, 1).reshape(shard, -1).astype(F32)
     query_terms, media_key_grad, media_value_grad, query_part, own_key_grad, own_value_grad = backward(
         item_index,
         table,
@@ -1431,7 +1904,9 @@
         (own_query, weighted_grad, terms, own_key, own_value),
         scale,
     )
-    (got_query,) = along_line([query_terms], False, 9)
+    slots = (LINES, PLANE, 2, shard, width)
+    out_part = inner_first(attn_low, middle_low).astype(BF16).reshape(slots)
+    got_query, shard_out = queries_home(query_terms, out_part)
     query_grad = (jnp.sum(got_query.astype(F32), axis=0) + query_part).astype(BF16)
     media_normed_grad = inner_last(media_key_grad, full_key) + inner_last(
         media_value_grad, full_value
@@ -1452,28 +1927,17 @@
     value_part = inner_first(media_normed, media_value_grad) + inner_first(
         latent_normed, own_value_grad
     )
-    out_part = inner_first(attn_low, middle_low)
     query_weight_part = inner_first(latent_normed, query_grad)
-    slots = (LINES, PLANE, 2, shard, width)
-    shard_out, shard_value, shard_key, shard_query = scatter(
+    small_part = jnp.concatenate(
+        [grad_time, grad_media_gain, grad_latent_gain, grad_ffn_gain, jnp.zeros((5, width), F32)],
+        axis=0,
+    )
+    shard_value, shard_key, shard_query, smalls_grad = ending(
         [
             part.astype(BF16).reshape(slots)
-            for part in (out_part, value_part, key_part, query_weight_part)
+            for part in (value_part, key_part, query_weight_part)
         ],
-        True,
-        10,
-    )
-    smalls_grad = total(
-        jnp.concatenate(
-            [
-                grad_time,
-                grad_media_gain,
-                grad_latent_gain,
-                grad_ffn_gain,
-                jnp.zeros((5, width), F32),
-            ],
-            axis=0,
-        )
+        small_part,
     )
     place = (column * 8 + row_index) * shard
     mine = lax.dynamic_slice(smalls_grad, (0, place), (16, shard))

time: 648 us -> 548 us (0.85)
  Pallas kernels: 519 us -> 433 us
  matrix products: 81.6 us -> 64.1 us
    pallas_call x2 -> x1, Pallas kernels: 175 us -> 40.8 us  [scatter(): pl.pallas_call(partial(scatter_kernel, count, whole), out_shape=[jax.Shap...]
    pallas_call x10 -> x5, Pallas kernels: 321 us -> 368 us  [the longest x1 141 us: opening(): pl.pallas_call(partial(opening_kernel, scale), out_shape=[jax.ShapeDtypeS...]
    dot_general x8 -> x3, matrix products: 28.4 us -> 11.1 us  [product(): return jnp.dot(left_side, right_side, preferred_element_type=jnp.float32)]
where the time goes in v2:
time: 548 us; the launch traced here: 538 us
  Pallas kernels  433 us (79%)
  matrix products  64.1 us (12%)
  local copies, waits for them, and re-layouts  24.6 us (4%)
  other arithmetic  14.3 us (3%)
    pallas_call x1, Pallas kernels, opening(): pl.pallas_call(partial(opening_kernel, scale), out_shape=[jax.ShapeDtypeS...  141 us
    pallas_call x1, Pallas kernels, ending(): pl.pallas_call(partial(ending_kernel, count), out_shape=[jax.ShapeDtypeSt...  85.6 us
    pallas_call x1, Pallas kernels, turn_back(): pl.pallas_call(turn_kernel, out_shape=[jax.ShapeDtypeStruct((LINES,) + gr...  52.9 us
    pallas_call x1, Pallas kernels, queries_home(): pl.pallas_call(queries_kernel, out_shape=[jax.ShapeDtypeStruct(parts.shap...  46.9 us
    pallas_call x1, Pallas kernels, gather(): pl.pallas_call(gather_kernel, out_shape=jax.ShapeDtypeStruct((16,) + shar...  41.5 us
    pallas_call x1, Pallas kernels, scatter(): pl.pallas_call(partial(scatter_kernel, count, whole), out_shape=[jax.Shap...  40.8 us
    dot_general x8, matrix products, inner_first(): lax.dot_general(left_side, right_side, (((0,), (0,)), ((), ())), preferre...  26.5 us
    dot_general x7, matrix products, inner_last(): lax.dot_general(left_side, right_side, (((1,), (1,)), ((), ())), preferre...  26.3 us

profile of v2, /device:TPU:0, one launch (start us, length us, event | category | flops | bytes accessed | tf_op | source)
XLA Modules:
  0.0 537.8 jit_solution(10944642106414149542)
XLA Ops:
  0.7 1.3 convert_reduce_fusion.3
  2.0 0.6 broadcast_in_dim.54
  2.6 0.2 dynamic-slice_reduce_fusion
  3.2 0.7 bitcast_convert_fusion.2
  3.9 1.1 convert_reduce_fusion.1
  4.9 1.2 fusion.43
  6.1 0.7 bitcast_convert_fusion
  6.8 0.7 iota_compare_fusion.1
  7.5 0.6 pad.9.refs_11_
  8.1 0.6 fusion.48.refs_12_
  8.7 0.7 concatenate.6
  9.5 0.6 pad.8.refs_0_
  10.1 141.5 %opening.1 = (f32[16,1536]{1,0:T(8,128)}, f32[8,128]{1,0:T(8,128)}, bf16[1536,1536]{1,0:T(8,128)(2,1)}, bf16[1536,1536]{1,0:T(8,128)(2,1)}, bf16[1536,1536]{1,0:...) custom-call(f32[16,128]{1,0:T(8,128)} %pad.8.refs_0_, ...), custom_call_target="tpu_custom_call" | custom-call | tf_op jit(solution)/shard_map/opening/pallas_call | solution.py:1479
  151.6 1.2 slice.52
  153.5 1.5 slice_reduce_fusion
  155.0 0.9 fusion.47
  155.9 4.9 settle.1
  160.8 0.4 fusion.3
  161.2 0.6 multiply_reduce_fusion.2
  161.8 1.6 dynamic-slice_bitcast_fusion.own_query_ref
  163.5 0.7 slice.55.own_key_ref
  164.2 1.2 slice.53.key_ref
  165.4 0.8 copy-done.5
  166.2 0.7 slice.56.own_value_ref
  166.9 1.3 slice.54.value_ref
  168.2 41.5 %gather.1 = bf16[16,64,1536]{2,1,0:T(8,128)(2,1)} custom-call(bf16[64,1536]{1,0:T(8,128)(2,1)} %get-tuple-element.64.shard), custom_call_target="tpu_custom_call" | custom-call | tf_op jit(solution)/shard_map/gather/pallas_call | solution.py:261
  209.7 6.6 %fusion.8 = (bf16[384,1024]{1,0:T(8,128)(2,1)S(1)}, f32[1024,384]{0,1:T(8,128)S(1)}) fusion(bf16[1024,1536]{1,0:T(8,128)(2,1)} %bitcast.154, bf16[1536,384]{1,0:T(8,128)(2,1)S(1)} %bitcast.166), kind=kOutput, calls=%fused_computation.27 | convolution fusion | flops 1233518592 | bytes 6684672 | tf_op jit(solution)/shard_map/dot_general | solution.py:456
  216.4 2.8 fusion.55.down_grad
  219.2 5.1 add_convert_fusion
  224.3 2.9 convolution_convert_fusion.4
  227.2 3.5 convolution_convert_fusion.2
  230.7 3.5 convolution_convert_fusion.3
  234.2 40.8 %scatter_6.1.normed_grad_ref = f32[64,1536]{1,0:T(8,128)} custom-call(bf16[4,4,64,1536]{3,2,1,0:T(8,128)(2,1)} %bitcast.156), custom_call_target="tpu_custom_call" | custom-call | tf_op jit(solution)/shard_map/scatter_6/pallas_call | solution.py:437
  275.0 5.6 %unsettle.1 = (f32[64,1536]{1,0:T(8,128)}, bf16[64,1536]{1,0:T(8,128)(2,1)}, f32[1,1536]{1,0:T(1,128)}, bf16[64,1536]{1,0:T(8,128)(2,1)}, f32[64,128]{1,0:T(8,128)}) custom-call(f32[64,1536]{1,0:T(8,128)} %scatter_6.1.normed_grad_ref, f32[64,1536]{1,0:T(8,128)} %get-tuple-element.63.middle_ref, f32[1,1536]{1,0:T(1,128)} %get-tuple-element.116.gain_ref, ...), custom_call_target="tpu_custom_call" | custom-call | tf_op jit(solution)/shard_map/unsettle/pallas_call | solution.py:1750
  280.6 52.9 %turn_back.1 = (bf16[4,64,1536]{2,1,0:T(8,128)(2,1)}, f32[4,64,128]{2,1,0:T(8,128)}, f32[64,1536]{1,0:T(8,128)}, bf16[16,48,384]{2,1,0:T(8,128)(2,1)}, f32[192,1536]{1,0:T(8,128)}) custom-call(bf16[64,1536]{1,0:T(8,128)(2,1)} %get-tuple-element.71.grad.own_grad_ref, f32[64,128]{1,0:T(8,128)} %get-tuple-element.72.terms.own_terms_ref, ...), custom_call_target="tpu_custom_call" | custom-call | tf_op jit(solution)/shard_map/turn_back/pallas_call | solution.py:896
  333.6 1.7 add_convert_fusion.2
  335.3 13.1 %attention_backward.1 = (bf16[4,64,1536]{2,1,0:T(8,128)(2,1)}, bf16[512,1536]{1,0:T(8,128)(2,1)}, bf16[512,1536]{1,0:T(8,128)(2,1)}, f32[64,1536]{1,0:T(8,128)},...) custom-call(s32[4]{0:T(128)} %copy-done.21, bf16[4,64,1536]{2,1,0:T(8,128)(2,1)} %get-tuple-element.74.table_ref, ...), custom_call_target="tpu_custom_call" | custom-call | tf_op jit(solution)/shard_map/attention_backward/pallas_call | solution.py:1616
  348.5 1.1 copy.38
  349.6 0.6 copy-done.23
  350.2 4.8 fusion.56
  355.1 3.3 multiply_reduce_fusion
  358.4 2.6 bitcast_reduce_fusion
  361.0 0.2 fusion.49
  361.3 3.6 convolution_convert_fusion.1
  364.9 46.9 %queries_home.1 = (bf16[4,64,1536]{2,1,0:T(8,128)(2,1)}, f32[48,1536]{1,0:T(8,128)}) custom-call(bf16[4,64,1536]{2,1,0:T(8,128)(2,1)} %get-tuple-element.84.parts, bf16[4,4,2,48,1536]{4,3,2,1,0:T(8,128)(2,1)} %bitcast.146), custom_call_target="tpu_custom_call" | custom-call | tf_op jit(solution)/shard_map/queries_home/pallas_call | solution.py:937
  411.7 1.3 convert_reduce_fusion
  413.1 4.0 fusion.57
  417.1 3.9 convolution_add_fusion.4
  421.1 1.7 fusion.42
  422.8 1.3 concatenate.7.refs_3_
  424.1 1.0 fusion.41
  425.1 4.7 convolution_convert_fusion
  429.7 2.7 fusion.30
  432.4 3.6 fusion
  436.1 2.7 fusion.28
  438.7 3.6 fusion.1
  442.4 85.6 %ending.1 = (f32[48,1536]{1,0:T(8,128)}, f32[48,1536]{1,0:T(8,128)}, f32[48,1536]{1,0:T(8,128)}, f32[16,1536]{1,0:T(8,128)}) custom-call(bf16[4,4,2,48,1536]{4,3,2,1,0:T(8,128)(2,1)} %bitcast.148, bf16[4,4,2,48,1536]{4,3,2,1,0:T(8,128)(2,1)} %bitcast.149, bf16[4,4,2,48,1536]{4,3,2,1,0:T(8,128)(2,1)} %bitcast.145, f32[16,1536]{1,0:T(8,128)} %concatenate.7.refs_3_), custom_call_target="tpu_custom_call" | custom-call | tf_op jit(solution)/shard_map/ending/pallas_call | solution.py:1018
  528.0 1.4 dynamic-slice_bitcast_fusion.1
  529.4 1.4 constant_dynamic-slice_fusion
  530.8 1.7 copy.44
  532.5 1.7 copy.45
  534.2 1.7 copy.46
  535.9 0.7 copy.47
  536.6 1.0 copy.48
  (78 shorter events, 0.7 us)
Async XLA Ops:
  0.6 2.0 copy-start
  3.2 148.4 %copy-start.21 = (s32[4]{0:T(128)}, s32[4]{0:T(128)S(1)}, u32[]{:S(2)}) copy-start(s32[4]{0:T(128)S(1)} %broadcast_clamp_fusion.item_ref) | copy-start | bytes 52
  155.9 4.9 copy-start.2
  160.8 2.7 copy-start.6
  164.2 2.0 copy-start.5
  168.2 41.5 %copy-start.25 = (bf16[32,48,384]{2,1,0:T(8,128)(2,1)S(1)}, bf16[32,48,384]{2,1,0:T(8,128)(2,1)}, u32[]{:S(2)}) copy-start(bf16[32,48,384]{2,1,0:T(8,128)(2,1)} %get-tuple-element.65) | copy-start | bytes 3538948
  209.7 6.7 %copy-start.22 = (bf16[16,64,1536]{2,1,0:T(8,128)(2,1)S(1)}, bf16[16,64,1536]{2,1,0:T(8,128)(2,1)}, u32[]{:S(2)}) copy-start(bf16[16,64,1536]{2,1,0:T(8,128)(2,1)} %get-tuple-element.66) | copy-start | bytes 9437188
  216.4 2.8 copy-start.9
  219.2 5.1 copy-start.4
  280.6 53.0 %copy-start.7 = (f32[64,1536]{1,0:T(8,128)S(1)}, f32[64,1536]{1,0:T(8,128)}, u32[]{:S(2)}) copy-start(f32[64,1536]{1,0:T(8,128)} %get-tuple-element.63.middle_ref) | copy-start | bytes 1179652
  335.3 13.1 %copy-start.14 = (bf16[16,48,384]{2,1,0:T(8,128)(2,1)S(1)}, bf16[16,48,384]{2,1,0:T(8,128)(2,1)}, u32[]{:S(2)}) copy-start(bf16[16,48,384]{2,1,0:T(8,128)(2,1)} %get-tuple-element.99) | copy-start | bytes 1769476
  348.4 1.8 copy-start.23
  348.5 6.6 %slice-start = ((s8[4718592]{0:T(1024)(128)(4,1)}), s8[4194304]{0:T(1024)(128)(4,1)S(1)}, s32[]{:S(2)}) async-start(s8[4718592]{0:T(1024)(128)(4,1)} %bitcast.150), calls=%async_computation | async-start | bytes 8388608
  350.2 4.8 slice-start.1
  350.2 4.8 copy-start.8
  358.4 2.8 copy-start.13
  358.4 2.8 copy-start.19
  364.8 48.2 %copy-start.16 = (f32[64,1536]{1,0:T(8,128)S(1)}, f32[64,1536]{1,0:T(8,128)}, u32[]{:S(2)}) copy-start(f32[64,1536]{1,0:T(8,128)} %get-tuple-element.88) | copy-start | bytes 1179652
  364.8 56.2 %slice-start.2 = ((s8[4718592]{0:T(1024)(128)(4,1)}), s8[524288]{0:T(1024)(128)(4,1)S(1)}, s32[]{:S(2)}) async-start(s8[4718592]{0:T(1024)(128)(4,1)} %bitcast.152), calls=%async_computation.2 | async-start | bytes 1048576
  413.1 4.0 copy-start.11
  413.1 8.0 %slice-start.3 = ((s8[4718592]{0:T(1024)(128)(4,1)}), s8[4194304]{0:T(1024)(128)(4,1)S(1)}, s32[]{:S(2)}) async-start(s8[4718592]{0:T(1024)(128)(4,1)} %bitcast.152), calls=%async_computation.3 | async-start | bytes 8388608
  417.1 4.0 copy-start.3
  417.1 4.0 copy-start.12
  421.1 1.7 copy-start.20
  421.1 3.0 copy-start.15
  425.1 4.7 copy-start.17
  432.4 3.7 copy-start.24
  528.0 7.9 %copy-start.18 = (f32[48,1536]{1,0:T(8,128)S(1)}, f32[48,1536]{1,0:T(8,128)}, u32[]{:S(2)}) copy-start(f32[48,1536]{1,0:T(8,128)} %get-tuple-element.148) | copy-start | bytes 884740
  528.0 8.6 %copy-start.10 = (f32[192,1536]{1,0:T(8,128)S(1)}, f32[192,1536]{1,0:T(8,128)}, u32[]{:S(2)}) copy-start(f32[192,1536]{1,0:T(8,128)} %get-tuple-element.150) | copy-start | bytes 3538948
  534.2 3.4 copy-start.1

commit v3 on v2

--- a/solution.py
+++ b/solution.py
@@ -298,73 +298,75 @@
 
 
 class Fold:
-    def __init__(self, wires, parts, whole, scratch, out, local_sem):
+    def __init__(self, wires, parts, whole, scratch, out):
         self.wires, self.parts, self.whole, self.out = wires, parts, whole, out
-        self.held, self.from_sib, self.cx, self.cy, self.fx, self.fy, self.fz = scratch
+        self.from_sib, self.cx, self.cy, self.fx, self.fy, self.fz = scratch
         self.z, self.g, self.chip, self.core = here()
-        ours = parts.at[:, :, self.core] if whole else parts
-        self.load = pltpu.make_async_copy(ours, self.held, local_sem)
-        self.width = self.held.shape[-1] // 2
-
-    def chip_of(self, gy):
-        return gy // 2
+        self.width = parts.shape[-1] // 2
+        self.sends = []
+
+    def send(self, source, target, gy):
+        copy = self.wires.send(source, target, (self.z, gy))
+        self.sends.append(copy)
+        return copy
+
+    def column(self, q):
+        return self.parts.at[:, q, self.core] if self.whole else self.parts.at[:, q]
 
     def half(self, ref, which):
         return ref.at[:, :, pl.ds(which * self.width, self.width)]
 
+    def merge(self, q):
+        if self.whole:
+            core = self.core
+
+            @pl.loop(0, LINES)
+            def _(n):
+                self.parts[n, q, core] = self.parts[n, q, core] + self.from_sib[n, q]
+
     def start(self):
-        self.load.start()
         if self.whole:
             theirs = self.parts.at[:, :, 1 - self.core]
-            self.sib = self.wires.send(theirs, self.from_sib, (self.z, sibling(self.g)))
+            self.sib = self.send(theirs, self.from_sib, sibling(self.g))
 
     def corner(self):
-        self.load.wait()
         if self.whole:
             self.sib.wait_recv()
-
-            @pl.loop(0, LINES)
-            def _(n):
-                for q in range(PLANE):
-                    self.held[n, q] = (
-                        self.held[n, q].astype(F32) + self.from_sib[n, q].astype(F32)
-                    ).astype(BF16)
-
-        far = self.held.at[:, self.chip_of(along_y(along_x(self.g)))]
-        self.to_y = self.wires.send(self.half(far, 0), self.cy, (self.z, along_y(self.g)))
-        self.to_x = self.wires.send(self.half(far, 1), self.cx, (self.z, along_x(self.g)))
-
-    def sides(self):
-        width = self.width
-        self.to_y.wait_recv()
-        near = self.chip_of(along_x(self.g))
+        q = along_y(along_x(self.g)) // 2
+        self.merge(q)
+        far = self.column(q)
+        self.to_y = self.send(self.half(far, 0), self.cy, along_y(self.g))
+        self.to_x = self.send(self.half(far, 1), self.cx, along_x(self.g))
+
+    def side(self, gy, came, corner, which, target):
+        q = gy // 2
+        self.merge(q)
+        came.wait_recv()
+        column = self.column(q)
+        cols = slice(which * self.width, (which + 1) * self.width)
 
         @pl.loop(0, LINES)
         def _(n):
-            self.held[n, near, :, :width] = (
-                self.held[n, near, :, :width].astype(F32) + self.cy[n].astype(F32)
-            ).astype(BF16)
-
-        self.along_x = self.wires.send(self.held.at[:, near], self.fx, (self.z, along_x(self.g)))
-        self.to_x.wait_recv()
-        beside = self.chip_of(along_y(self.g))
-
-        @pl.loop(0, LINES)
-        def _(n):
-            self.held[n, beside, :, width:] = (
-                self.held[n, beside, :, width:].astype(F32) + self.cx[n].astype(F32)
-            ).astype(BF16)
-
-        self.along_y = self.wires.send(self.held.at[:, beside], self.fy, (self.z, along_y(self.g)))
+            column[n, :, cols] = column[n, :, cols] + corner[n]
+
+        return self.send(column, target, gy)
+
+    def side_x(self):
+        self.by_x = self.side(along_x(self.g), self.to_y, self.cy, 0, self.fx)
+
+    def side_y(self):
+        self.by_y = self.side(along_y(self.g), self.to_x, self.cx, 1, self.fy)
 
     def line(self):
-        self.along_x.wait_recv()
-        self.along_y.wait_recv()
+        self.merge(self.chip)
+        self.by_x.wait_recv()
+        self.by_y.wait_recv()
+        column = self.column(self.chip)
         self.zs = []
         for k in (2, 1, 3):
             there = turn(self.z, k)
             self.fx[there] = (
-                self.held[there, self.chip].astype(F32)
+                column[there].astype(F32)
                 + self.fx[there].astype(F32)
                 + self.fy[there].astype(F32)
             ).astype(BF16)
@@ -372,9 +374,7 @@
                 self.wires.send(self.fx.at[there], self.fz.at[k - 1], (there, self.g))
             )
         z = self.z
-        self.out[...] = (
-            self.held[z, self.chip].astype(F32) + self.fx[z].astype(F32) + self.fy[z].astype(F32)
-        )
+        self.out[...] = column[z].astype(F32) + self.fx[z].astype(F32) + self.fy[z].astype(F32)
 
     def finish(self):
         for copy in self.zs:
@@ -383,11 +383,16 @@
             self.fz[0].astype(F32) + self.fz[1].astype(F32) + self.fz[2].astype(F32)
         )
 
+    def release(self):
+        for copy in self.sends:
+            copy.wait_send()
+        waited = [id(copy) for copy in self.sends]
+        self.wires.sent = [entry for entry in self.wires.sent if id(entry[1]) not in waited]
+
 
 def fold_scratch(rows, cols, whole):
     half = cols // 2
     return [
-        pltpu.VMEM((LINES, PLANE, rows, cols), BF16),
         pltpu.VMEM((LINES, PLANE, rows, cols) if whole else (1, 1, 16, 128), BF16),
         pltpu.VMEM((LINES, rows, half), BF16),
         pltpu.VMEM((LINES, rows, half), BF16),
@@ -397,52 +402,40 @@
     ]
 
 
+FOLD = 6
+
+
 def fold_sems(whole):
     return (1 if whole else 0) + 4 + 3
 
 
-def fold_all(flows):
-    stages = ("corner", "sides", "line", "finish")
-    for tick in range(len(flows) + len(stages) - 1):
-        for n in range(len(stages)):
-            flow = tick - n
-            if 0 <= flow < len(flows):
-                getattr(flows[flow], stages[n])()
-
-
-def scatter_kernel(count, whole, *refs):
-    parts, outs = refs[:count], refs[count : 2 * count]
-    send_sems, recv_sems, local_sems = refs[2 * count : 2 * count + 3]
-    scratch = refs[2 * count + 3 :]
-    z, g, chip, core = here()
-    greet(line_of(z, g) + sides_of(z, g, whole))
+def scatter_kernel(parts, out, send_sems, recv_sems, *scratch):
+    z, g, _, _ = here()
+    greet(line_of(z, g) + sides_of(z, g, False))
     wires = Wires(send_sems, recv_sems)
-    flows = [
-        Fold(wires, parts[n], whole, scratch[7 * n : 7 * n + 7], outs[n], local_sems.at[n])
-        for n in range(count)
-    ]
-    for flow in flows:
-        flow.start()
-    fold_all(flows)
+    flow = Fold(wires, parts, False, scratch, out)
+    flow.start()
+    flow.corner()
+    flow.side_x()
+    flow.side_y()
+    flow.line()
+    flow.finish()
     wires.drain()
 
 
-def scatter(parts, whole, ident):
-    count = len(parts)
-    rows, cols = parts[0].shape[-2:]
-    scratch = []
-    for _ in parts:
-        scratch += fold_scratch(rows, cols, whole)
-    wires = count * fold_sems(whole)
+def scatter(parts, ident):
+    rows, cols = parts.shape[-2:]
+    wires = fold_sems(False)
     return pl.pallas_call(
-        partial(scatter_kernel, count, whole),
-        out_shape=[jax.ShapeDtypeStruct((rows, cols), F32)] * count,
-        in_specs=[LEFT] * count,
-        out_specs=[VMEM] * count,
-        scratch_shapes=[sems(wires), sems(wires), sems(count)] + scratch,
-        compiler_params=params(ident),
-        name="scatter_%d" % ident,
-    )(*parts)
+        scatter_kernel,
+        out_shape=jax.ShapeDtypeStruct((rows, cols), F32),
+        in_specs=[VMEM],
+        out_specs=VMEM,
+        scratch_shapes=[sems(wires), sems(wires)] + fold_scratch(rows, cols, False),
+        compiler_params=params(6),
+        name="scatter",
+        input_output_aliases={},
+    )(parts)
 
 
 def layer_norm(row_block, gain_row):
@@ -850,6 +843,7 @@
     up_held,
     up_near,
     down_near,
+    down_held,
     *fold,
 ):
     z, g, chip, core = here()
@@ -868,16 +862,19 @@
         (up_held, up_near, down_near),
         local_sems,
     )
-    flow = Fold(wires, down_part, False, fold, down_out, local_sems.at[2])
-    flow.start()
+    flow = Fold(wires, down_held, False, fold, down_out)
+    load = pltpu.make_async_copy(down_part, down_held, local_sems.at[2])
+    load.start()
     for line in lines:
         line.first()
     back.start()
+    load.wait()
     flow.corner()
     grad_out[z] = grad[...]
     terms_out[z] = terms[...]
     back.columns()
-    flow.sides()
+    flow.side_x()
+    flow.side_y()
     for step in range(3):
         for line in lines:
             line.take(step)
@@ -911,42 +908,12 @@
             pltpu.VMEM((16, rows, width), BF16),
             pltpu.VMEM((16, rows, width), BF16),
             pltpu.VMEM(down_shape, F32),
+            pltpu.VMEM((LINES, PLANE, latent_rows, model_width), BF16),
         ]
         + fold_scratch(latent_rows, model_width, False),
         compiler_params=params(2),
         name="turn_back",
     )(grad, terms, down_part, up_grad, down_grad)
-
-
-def queries_kernel(parts, weight_part, out, weight_out, send_sems, recv_sems, local_sem, *fold):
-    z, g, _, _ = here()
-    greet(line_of(z, g) + sides_of(z, g, True))
-    wires = Wires(send_sems, recv_sems)
-    exchange = Exchange(wires, [(parts, out)])
-    flow = Fold(wires, weight_part, True, fold, weight_out, local_sem)
-    flow.start()
-    exchange.first()
-    fold_all([flow])
-    exchange.finish()
-    wires.drain()
-
-
-def queries_home(parts, weight_part):
-    rows, cols = weight_part.shape[-2:]
-    wires = fold_sems(True) + 3
-    return pl.pallas_call(
-        queries_kernel,
-        out_shape=[
-            jax.ShapeDtypeStruct(parts.shape, BF16),
-            jax.ShapeDtypeStruct((rows, cols), F32),
-        ],
-        in_specs=[VMEM, LEFT],
-        out_specs=[VMEM, VMEM],
-        scratch_shapes=[sems(wires), sems(wires), pltpu.SemaphoreType.DMA]
-        + fold_scratch(rows, cols, True),
-        compiler_params=params(3),
-        name="queries_home",
-    )(parts, weight_part)
 
 
 class Total:
@@ -977,61 +944,6 @@
             self.step += 1
         else:
             self.out[...] = self.source[...] + self.got[3] + self.got[4] + self.got[5]
-
-
-def ending_kernel(count, *refs):
-    parts, small, outs = refs[:count], refs[count], refs[count + 1 : 2 * count + 1]
-    small_out, send_sems, recv_sems, local_sems, small_sums, small_got = refs[
-        2 * count + 1 : 2 * count + 7
-    ]
-    scratch = refs[2 * count + 7 :]
-    z, g, _, _ = here()
-    greet(line_of(z, g) + sides_of(z, g, True))
-    wires = Wires(send_sems, recv_sems)
-    flows = [
-        Fold(wires, parts[n], True, scratch[7 * n : 7 * n + 7], outs[n], local_sems.at[n])
-        for n in range(count)
-    ]
-    total = Total(wires, small, small_out, small_sums, small_got)
-    total.push()
-    for flow in flows:
-        flow.start()
-    stages = ("corner", "sides", "line", "finish")
-    for tick in range(count + len(stages) - 1):
-        for n in range(len(stages)):
-            if 0 <= tick - n < count:
-                getattr(flows[tick - n], stages[n])()
-        if tick < 4:
-            total.pull()
-            if tick < 3:
-                total.push()
-    wires.drain()
-
-
-def ending(parts, small):
-    count = len(parts)
-    rows, cols = parts[0].shape[-2:]
-    scratch = []
-    for _ in parts:
-        scratch += fold_scratch(rows, cols, True)
-    wires = count * fold_sems(True) + 6
-    return pl.pallas_call(
-        partial(ending_kernel, count),
-        out_shape=[jax.ShapeDtypeStruct((rows, cols), F32)] * count
-        + [jax.ShapeDtypeStruct(small.shape, F32)],
-        in_specs=[LEFT] * count + [VMEM],
-        out_specs=[VMEM] * (count + 1),
-        scratch_shapes=[
-            sems(wires),
-            sems(wires),
-            sems(count),
-            pltpu.VMEM((3,) + small.shape, F32),
-            pltpu.VMEM((6,) + small.shape, F32),
-        ]
-        + scratch,
-        compiler_params=params(4),
-        name="ending",
-    )(*parts, small)
 
 
 def head_masks(rows, width, head_size):
@@ -1542,92 +1454,358 @@
     return jnp.concatenate([terms[:, first + h : first + h + 1] for h in range(GROUP)], axis=0)
 
 
-def backward_kernel(
-    scale,
-    item_ref,
-    table_ref,
-    grad_ref,
-    terms_ref,
-    key_ref,
-    value_ref,
-    valid_ref,
-    own_query_ref,
-    own_grad_ref,
-    own_terms_ref,
-    own_key_ref,
-    own_value_ref,
-    query_grad_ref,
-    key_grad_ref,
-    value_grad_ref,
-    own_query_grad_ref,
-    own_key_grad_ref,
-    own_value_grad_ref,
-    sums,
-):
-    items, rows, width = table_ref.shape
-    frames = valid_ref.shape[0]
-    patches = valid_ref.shape[2]
+def closing_kernel(scale, *refs):
+    (
+        table_ref,
+        grad_ref,
+        terms_ref,
+        keys_ref,
+        values_ref,
+        normed_ref,
+        valid_ref,
+        attn_ref,
+        low_ref,
+        own_grad_ref,
+        own_terms_ref,
+        key_weight_ref,
+        value_weight_ref,
+        query_weight_ref,
+        media_ref,
+        time_rows_ref,
+        tables_ref,
+        latents_ref,
+        middle_grad_ref,
+        ffn_gain_ref,
+        item_ref,
+        time_ref,
+        media_grad_out,
+        latents_grad_out,
+        small_out,
+        out_out,
+        value_out,
+        key_out,
+        query_out,
+        send_sems,
+        recv_sems,
+        local_sems,
+        table,
+        grads,
+        keys,
+        values,
+        normed,
+        key_grad,
+        value_grad,
+        weight_a,
+        weight_b,
+        sums,
+        terms_query,
+        got_query,
+        query_grad,
+        own_query_grad,
+        media_grad,
+        latent_grad,
+        small,
+        small_sums,
+        small_got,
+        part_a,
+        part_b,
+        part_c,
+        *fold,
+    ) = refs
+    z, g, _, core = here()
+    items, rows, width = table.shape
+    frames, _, patches = valid_ref.shape
+    media_rows = frames * patches
+    shard = width // 32
     groups = H // GROUP
     span = width // groups
     masks = head_masks(rows, span, span // GROUP)
-    sums[...] = jnp.zeros_like(sums)
-    own_terms = own_terms_ref[...]
-    for group in range(groups):
-        cols = pl.ds(group * span, span)
-        own_query_grad_ref[:, cols], own_key_grad_ref[:, cols], own_value_grad_ref[:, cols] = repel(
-            own_query_ref[:, cols],
-            own_grad_ref[:, cols],
-            own_key_ref[:, cols],
-            own_value_ref[:, cols],
-            None,
-            stacked_columns(own_terms, group * GROUP),
-            stacked_columns(own_terms, H + group * GROUP),
-            scale,
-            masks,
-        )
-
-    @pl.loop(0, frames)
-    def _(frame):
-        item = item_ref[frame]
-        block = pl.ds(pl.multiple_of(frame * patches, patches), patches)
-        valid = valid_ref[frame]
-        terms = terms_ref[item]
+    greet(line_of(z, g) + sides_of(z, g, True))
+    wires = Wires(send_sems, recv_sems)
+    out = Fold(wires, part_a, True, fold[:FOLD], out_out)
+    value = Fold(wires, part_b, True, fold[FOLD : 2 * FOLD], value_out)
+    key = Fold(wires, part_c, True, fold[2 * FOLD : 3 * FOLD], key_out)
+    query = Fold(wires, part_a, True, fold[3 * FOLD :], query_out)
+    total = Total(wires, small, small_out, small_sums, small_got)
+    exchange = Exchange(wires, [(terms_query, got_query)])
+    local = []
+
+    def load(source, target):
+        copy = pltpu.make_async_copy(source, target, local_sems.at[len(local)])
+        copy.start()
+        local.append(copy)
+        return copy
+
+    loads = [
+        load(table_ref, table),
+        load(grad_ref, grads),
+        load(keys_ref, keys),
+        load(values_ref, values),
+    ]
+    normed_load = load(normed_ref, normed)
+    key_load = load(key_weight_ref, weight_a)
+    value_load = load(value_weight_ref, weight_b)
+    stored = []
+
+    def weight_part(part, left, right):
+        @pl.loop(0, LINES)
+        def _(n):
+            cols = pl.ds(pl.multiple_of(n * span, 128), span)
+            block = dot_first(left[:, cols], right[...]).astype(BF16)
+            part[n] = block.reshape(PLANE, 2, shard, width)
+
+    def out_part():
+        weight_part(part_a, attn_ref, low_ref)
+        out.start()
+
+    def value_part():
+        normed_load.wait()
+        weight_part(part_b, normed, value_grad)
+        value.start()
+
+    def key_part():
+        weight_part(part_c, normed, key_grad)
+        key.start()
+
+    def repel_own():
+        for copy in loads:
+            copy.wait()
+        sums[...] = jnp.zeros_like(sums)
+        own_terms = own_terms_ref[...]
         for group in range(groups):
-            cols = pl.ds(group * span, span)
-            query_grad, key_grad_ref[block, cols], value_grad_ref[block, cols] = repel(
-                table_ref[item, :, cols],
-                grad_ref[item, :, cols],
-                key_ref[block, cols],
-                value_ref[block, cols],
-                valid,
-                stacked_columns(terms, group * GROUP),
-                stacked_columns(terms, H + group * GROUP),
+            cols = slice(group * span, (group + 1) * span)
+            (
+                own_query_grad[:, cols],
+                key_grad[media_rows:, cols],
+                value_grad[media_rows:, cols],
+            ) = repel(
+                table[z, :, cols],
+                own_grad_ref[:, cols],
+                keys[media_rows:, cols],
+                values[media_rows:, cols],
+                None,
+                stacked_columns(own_terms, group * GROUP),
+                stacked_columns(own_terms, H + group * GROUP),
                 scale,
                 masks,
             )
-            sums[item, :, cols] += query_grad
-
-    query_grad_ref[...] = sums[...].astype(BF16)
-
-
-def backward(item_index, table, grads, terms, keys, values, valid, own, scale):
-    items, rows, width = table.shape
-    vmem = pl.BlockSpec(memory_space=pltpu.VMEM)
+
+    def repel_frames(first, last):
+        @pl.loop(first, last)
+        def _(frame):
+            block = pl.ds(pl.multiple_of(frame * patches, patches), patches)
+            valid = valid_ref[frame]
+            share = [item_ref[frame, item] for item in range(items)]
+
+            def pick(ref, cols):
+                chosen = share[0] * ref[0, :, cols].astype(F32)
+                for item in range(1, items):
+                    chosen = chosen + share[item] * ref[item, :, cols].astype(F32)
+                return chosen
+
+            everything = slice(0, 128)
+            terms = pick(terms_ref, everything)
+            for group in range(groups):
+                cols = slice(group * span, (group + 1) * span)
+                query_part, key_grad[block, cols], value_grad[block, cols] = repel(
+                    pick(table, cols).astype(BF16),
+                    pick(grads, cols).astype(BF16),
+                    keys[block, cols],
+                    values[block, cols],
+                    valid,
+                    stacked_columns(terms, group * GROUP),
+                    stacked_columns(terms, H + group * GROUP),
+                    scale,
+                    masks,
+                )
+                for item in range(items):
+                    sums[item, :, cols] += share[item] * query_part
+
+    def queries_first():
+        terms_query[...] = sums[...].astype(BF16)
+        exchange.first()
+
+    def media_half(n):
+        if n == 0:
+            key_load.wait()
+            value_load.wait()
+            small[...] = jnp.zeros_like(small)
+            small[10:11] = ffn_gain_ref[...]
+        else:
+            stored[-1].wait()
+        count = media_rows // 2
+        first = n * count
+        block = slice(first, first + count)
+
+        @pl.loop(0, groups)
+        def _(t):
+            cols = pl.ds(pl.multiple_of(t * span, 128), span)
+            media_grad[:, cols] = dot_last(key_grad[block], weight_a[cols]) + dot_last(
+                value_grad[block], weight_b[cols]
+            )
+
+        gain = tables_ref[8:9]
+        chunk = 32
+        per_frame = patches // chunk
+        for f in range(count // patches):
+            frame = n * (count // patches) + f
+            moving = time_rows_ref[frame : frame + 1]
+
+            def step(t, carry):
+                gain_sum, row_sum = carry
+                here_rows = pl.ds(pl.multiple_of(f * patches + t * chunk, chunk), chunk)
+                there_rows = pl.ds(pl.multiple_of(first + f * patches + t * chunk, chunk), chunk)
+                row = media_ref[there_rows].astype(F32) + moving
+                pulled, summand = norm_pull(row, gain, media_grad[here_rows])
+                media_grad[here_rows] = pulled
+                return (
+                    gain_sum + jnp.sum(summand, axis=0, keepdims=True),
+                    row_sum + jnp.sum(pulled, axis=0, keepdims=True),
+                )
+
+            zero = jnp.zeros((1, width), F32)
+            gain_sum, row_sum = lax.fori_loop(0, per_frame, step, (zero, zero))
+            small[8:9] += gain_sum
+            for t in range(8):
+                small[t : t + 1] += time_ref[frame, t] * row_sum
+        stored.append(load(media_grad, media_grad_out.at[pl.ds(first, count)]))
+
+    def latents_side():
+        @pl.loop(0, groups)
+        def _(t):
+            cols = pl.ds(pl.multiple_of(t * span, 128), span)
+            latent_grad[:, cols] = dot_last(key_grad[media_rows:], weight_a[cols]) + dot_last(
+                value_grad[media_rows:], weight_b[cols]
+            )
+
+        stored.append(load(query_weight_ref, weight_a))
+
+    def query_part():
+        found = own_query_grad[...]
+        for item in range(items):
+            found = found + got_query[item].astype(F32)
+        query_grad[...] = found.astype(BF16)
+        out.release()
+        weight_part(part_a, normed.at[media_rows:], query_grad)
+        query.start()
+
+    def latents_end():
+        stored[-1].wait()
+
+        @pl.loop(0, groups)
+        def _(t):
+            cols = pl.ds(pl.multiple_of(t * span, 128), span)
+            latent_grad[:, cols] += dot_last(query_grad[...], weight_a[cols])
+
+        pulled, summand = norm_pull(
+            latents_ref[...].astype(F32), tables_ref[9:10], latent_grad[...]
+        )
+        latents_grad_out[...] = middle_grad_ref[...] + pulled
+        small[9:10] = jnp.sum(summand, axis=0, keepdims=True)
+        total.push()
+
+    def total_next():
+        total.pull()
+        total.push()
+
+    out_part()
+    repel_own()
+    repel_frames(0, frames // 2)
+    out.corner()
+    repel_frames(frames // 2, frames)
+    queries_first()
+    out.side_x()
+    out.side_y()
+    value_part()
+    key_part()
+    value.corner()
+    media_half(0)
+    key.corner()
+    value.side_x()
+    value.side_y()
+    out.line()
+    media_half(1)
+    key.side_x()
+    exchange.finish()
+    key.side_y()
+    latents_side()
+    query_part()
+    value.line()
+    latents_end()
+    total_next()
+    query.corner()
+    key.line()
+    total_next()
+    query.side_x()
+    value.finish()
+    query.side_y()
+    total_next()
+    out.finish()
+    query.line()
+    key.finish()
+    total.pull()
+    query.finish()
+    stored[1].wait()
+    wires.drain()
+
+
+def closing(scale, *args):
+    (table, grads, terms, keys, values, normed) = args[:6]
+    media, latents = args[14], args[17]
+    rows, width = latents.shape
+    shard = width // 32
+    wires = 4 * fold_sems(True) + 6 + 3
+    bf = [
+        table.shape,
+        table.shape,
+        keys.shape,
+        keys.shape,
+        keys.shape,
+        keys.shape,
+        keys.shape,
+        (width, width),
+        (width, width),
+    ]
+    part = pltpu.VMEM((LINES, PLANE, 2, shard, width), BF16)
+    small = (16, width)
+    scratch = [pltpu.VMEM(shape, BF16) for shape in bf] + [
+        pltpu.VMEM(table.shape, F32),
+        pltpu.VMEM(table.shape, BF16),
+        pltpu.VMEM(table.shape, BF16),
+        pltpu.VMEM((rows, width), BF16),
+        pltpu.VMEM((rows, width), F32),
+        pltpu.VMEM((media.shape[0] // 2, width), F32),
+        pltpu.VMEM((rows, width), F32),
+        pltpu.VMEM(small, F32),
+        pltpu.VMEM((3,) + small, F32),
+        pltpu.VMEM((6,) + small, F32),
+        part,
+        part,
+        part,
+    ]
+    for _ in range(4):
+        scratch += fold_scratch(shard, width, True)
+    smem = pl.BlockSpec(memory_space=pltpu.SMEM)
     return pl.pallas_call(
-        partial(backward_kernel, scale),
+        partial(closing_kernel, scale),
         out_shape=[
-            jax.ShapeDtypeStruct((items, rows, width), BF16),
-            jax.ShapeDtypeStruct(keys.shape, BF16),
-            jax.ShapeDtypeStruct(keys.shape, BF16),
-            jax.ShapeDtypeStruct((rows, width), F32),
-            jax.ShapeDtypeStruct((rows, width), BF16),
-            jax.ShapeDtypeStruct((rows, width), BF16),
-        ],
-        in_specs=[pl.BlockSpec(memory_space=pltpu.SMEM)] + [vmem] * 11,
-        out_specs=[vmem] * 6,
-        scratch_shapes=[pltpu.VMEM((items, rows, width), F32)],
-        name="attention_backward",
-    )(item_index, table, grads, terms, keys, values, valid, *own)
+            jax.ShapeDtypeStruct(media.shape, F32),
+            jax.ShapeDtypeStruct(latents.shape, F32),
+            jax.ShapeDtypeStruct(small, F32),
+        ]
+        + [jax.ShapeDtypeStruct((shard, width), F32)] * 4,
+        in_specs=[LEFT, LEFT, VMEM, LEFT, LEFT, LEFT]
+        + [VMEM] * 5
+        + [LEFT] * 3
+        + [VMEM] * 6
+        + [smem] * 2,
+        out_specs=[LEFT] + [VMEM] * 6,
+        scratch_shapes=[sems(wires), sems(wires), sems(12)] + scratch,
+        compiler_params=pltpu.CompilerParams(
+            collective_id=3, has_side_effects=True, vmem_limit_bytes=67043328
+        ),
+        name="closing",
+    )(*args)
 
 
 def settle_kernel(
@@ -1848,17 +2026,7 @@
     up_cols = up_cols.reshape(width, -1)
     down_rows = down_rows.reshape(-1, width)
     cot_rows = cot_rows.reshape(-1, width)
-    time_onehot = times[:frames, :8].astype(F32)
     time_rows = product(times[:frames, :8], full_time)
-    media_in = (
-        media.astype(F32).reshape(frames, patches, width) + time_rows[:, None, :]
-    ).reshape(-1, width)
-    latent_in = latents.astype(F32)
-    media_rows = media.shape[0]
-    media_normed, latent_normed = normed[:media_rows], normed[media_rows:]
-    media_key, own_key = keys[:media_rows], keys[media_rows:]
-    media_value, own_value = values[:media_rows], values[media_rows:]
-    own_query = lax.dynamic_index_in_dim(table, column, 0, keepdims=False)
     attention, attn_low, sums, middle, ffn_normed = settle(
         got_weighted, got_stats, own_weighted, own_stats, full_out, latents, full_ffn_gain
     )
@@ -1871,7 +2039,7 @@
     normed_part = inner_last(up_grad, up_cols).astype(BF16)
     down_part = product(hidden, down_rows).astype(BF16)
     shape = (LINES, PLANE, latent_rows, width)
-    (ffn_normed_grad,) = scatter([normed_part.reshape(shape)], False, 6)
+    ffn_normed_grad = scatter(normed_part.reshape(shape), 6)
     up_grad_part = inner_first(ffn_rows, up_grad).astype(BF16)
     down_grad_part = inner_first(hidden, cot_rows)
     middle_grad, middle_low, grad_ffn_gain, weighted_grad, terms = unsettle(
@@ -1893,51 +2061,38 @@
     )
     new_latents = (middle + down_sum).astype(BF16)
     shard_up = jnp.swapaxes(shard_up, 0, 1).reshape(shard, -1).astype(F32)
-    query_terms, media_key_grad, media_value_grad, query_part, own_key_grad, own_value_grad = backward(
-        item_index,
+    (
+        media_grad,
+        latents_grad,
+        smalls_grad,
+        shard_out,
+        shard_value,
+        shard_key,
+        shard_query,
+    ) = closing(
+        scale,
         table,
         grad_table,
         terms_table,
-        media_key,
-        media_value,
+        keys,
+        values,
+        normed,
         valid_rows,
-        (own_query, weighted_grad, terms, own_key, own_value),
-        scale,
-    )
-    slots = (LINES, PLANE, 2, shard, width)
-    out_part = inner_first(attn_low, middle_low).astype(BF16).reshape(slots)
-    got_query, shard_out = queries_home(query_terms, out_part)
-    query_grad = (jnp.sum(got_query.astype(F32), axis=0) + query_part).astype(BF16)
-    media_normed_grad = inner_last(media_key_grad, full_key) + inner_last(
-        media_value_grad, full_value
-    )
-    media_grad, media_summand = norm_pull(media_in, full_media_gain, media_normed_grad)
-    grad_media_gain = jnp.sum(media_summand, axis=0, keepdims=True)
-    frame_sums = jnp.sum(media_grad.reshape(frames, patches, width), axis=1)
-    grad_time = collect(time_onehot, frame_sums)
-    latent_normed_grad = (
-        inner_last(query_grad, full_query)
-        + inner_last(own_key_grad, full_key)
-        + inner_last(own_value_grad, full_value)
-    )
-    latent_part, latent_summand = norm_pull(latent_in, full_latent_gain, latent_normed_grad)
-    grad_latent_gain = jnp.sum(latent_summand, axis=0, keepdims=True)
-    latents_grad = middle_grad + latent_part
-    key_part = inner_first(media_normed, media_key_grad) + inner_first(latent_normed, own_key_grad)
-    value_part = inner_first(media_normed, media_value_grad) + inner_first(
-        latent_normed, own_value_grad
-    )
-    query_weight_part = inner_first(latent_normed, query_grad)
-    small_part = jnp.concatenate(
-        [grad_time, grad_media_gain, grad_latent_gain, grad_ffn_gain, jnp.zeros((5, width), F32)],
-        axis=0,
-    )
-    shard_value, shard_key, shard_query, smalls_grad = ending(
-        [
-            part.astype(BF16).reshape(slots)
-            for part in (value_part, key_part, query_weight_part)
-        ],
-        small_part,
+        attn_low,
+        middle_low,
+        weighted_grad,
+        terms,
+        full_key,
+        full_value,
+        full_query,
+        media,
+        jnp.pad(time_rows, ((0, 8 - frames), (0, 0))),
+        tables,
+        latents,
+        middle_grad,
+        grad_ffn_gain,
+        items,
+        times[:frames, :8].astype(F32),
     )
     place = (column * 8 + row_index) * shard
     mine = lax.dynamic_slice(smalls_grad, (0, place), (16, shard))

time: 548 us -> 446 us (0.81); the launches traced: 538 us -> 445 us
  matrix products: 64.1 us -> 24.5 us
  Pallas kernels: 433 us -> 395 us
  other arithmetic: 14.3 us -> 6.89 us
  local copies, waits for them, and re-layouts: 24.6 us -> 17.4 us
    pallas_call x4 -> x2, Pallas kernels: 186 us -> 149 us  [the longest x1 108 us: closing(): pl.pallas_call(partial(closing_kernel, scale), out_shape=[jax.ShapeDtypeS...]
    dot_general x8 -> x2, matrix products: 26.5 us -> 5.73 us  [inner_first(): lax.dot_general(left_side, right_side, (((0,), (0,)), ((), ())), preferre...]
    dot_general x7 -> x2, matrix products: 26.3 us -> 8.63 us  [inner_last(): lax.dot_general(left_side, right_side, (((1,), (1,)), ((), ())), preferre...]
    reduce_sum x6 -> x0, other arithmetic: 7.11 us -> none  [the longest x1 2.6 us: per_device(): frame_sums = jnp.sum(media_grad.reshape(frames, patches, width), axis=1)]
where the time goes in v3:
time: 446 us; the launch traced here: 445 us
  Pallas kernels  395 us (89%)
  matrix products  24.5 us (5%)
  local copies, waits for them, and re-layouts  17.4 us (4%)
  other arithmetic  6.89 us (2%)
    pallas_call x1, Pallas kernels, opening(): pl.pallas_call(partial(opening_kernel, scale), out_shape=[jax.ShapeDtypeS...  142 us
    pallas_call x1, Pallas kernels, closing(): pl.pallas_call(partial(closing_kernel, scale), out_shape=[jax.ShapeDtypeS...  108 us
    pallas_call x1, Pallas kernels, turn_back(): pl.pallas_call(turn_kernel, out_shape=[jax.ShapeDtypeStruct((LINES,) + gr...  52.9 us
    pallas_call x1, Pallas kernels, gather(): pl.pallas_call(gather_kernel, out_shape=jax.ShapeDtypeStruct((16,) + shar...  41.5 us
    pallas_call x1, Pallas kernels, scatter(): pl.pallas_call(scatter_kernel, out_shape=jax.ShapeDtypeStruct((rows, cols...  40.6 us
    dot_general x3, matrix products, product(): return jnp.dot(left_side, right_side, preferred_element_type=jnp.float32)  10.1 us

profile of v3, /device:TPU:0, one launch (start us, length us, event | category | flops | bytes accessed | tf_op | source)
XLA Modules:
  0.0 445.1 jit_solution(16892985971586473580)
XLA Ops:
  0.6 0.9 dynamic-slice_reduce_fusion
  1.5 0.2 reduce-window.8
  1.7 0.2 convert_reduce_fusion
  1.9 0.7 fusion.25.refs_12_.refs_20_
  2.6 0.7 bitcast_convert_fusion
  3.2 1.3 convert_reduce_fusion.1
  4.5 0.6 broadcast_in_dim.36
  5.2 0.7 bitcast_convert_fusion.2
  5.8 0.7 concatenate.3
  6.5 0.6 pad.12.refs_0_
  7.1 0.7 iota_compare_fusion.1
  7.9 0.6 pad.13.refs_11_
  8.5 141.6 %opening.1 = (f32[16,1536]{1,0:T(8,128)}, f32[8,128]{1,0:T(8,128)}, bf16[1536,1536]{1,0:T(8,128)(2,1)}, bf16[1536,1536]{1,0:T(8,128)(2,1)}, bf16[1536,1536]{1,0:...) custom-call(f32[16,128]{1,0:T(8,128)} %pad.12.refs_0_, ...), custom_call_target="tpu_custom_call" | custom-call | tf_op jit(solution)/shard_map/opening/pallas_call | solution.py:1391
  150.0 1.4 slice.27.gain_ref
  151.4 4.8 %settle.1 = (f32[64,1536]{1,0:T(8,128)}, bf16[64,1536]{1,0:T(8,128)(2,1)}, f32[64,128]{1,0:T(8,128)}, f32[64,1536]{1,0:T(8,128)}, bf16[64,1536]{1,0:T(8,128)(2,1)}) custom-call(bf16[4,64,1536]{2,1,0:T(8,128)(2,1)} %get-tuple-element.52.weighted_ref, f32[4,64,128]{2,1,0:T(8,128)} %get-tuple-element.53.stats_ref, ...), custom_call_target="tpu_custom_call" | custom-call | tf_op jit(solution)/shard_map/settle/pallas_call | solution.py:1850
  156.2 0.0 copy-start.13
  156.2 41.5 %gather.1 = bf16[16,64,1536]{2,1,0:T(8,128)(2,1)} custom-call(bf16[64,1536]{1,0:T(8,128)(2,1)} %get-tuple-element.59.shard), custom_call_target="tpu_custom_call" | custom-call | tf_op jit(solution)/shard_map/gather/pallas_call | solution.py:261
  197.7 0.0 copy-done.13
  197.7 0.0 copy-start.12
  197.7 6.4 %fusion.3 = (bf16[384,1024]{1,0:T(8,128)(2,1)S(1)}, f32[1024,384]{0,1:T(8,128)S(1)}) fusion(bf16[1024,1536]{1,0:T(8,128)(2,1)} %bitcast.103, bf16[1536,384]{1,0:T(8,128)(2,1)S(1)} %bitcast.115), kind=kOutput, calls=%fused_computation.8 | convolution fusion | flops 1233518592 | bytes 6684672 | tf_op jit(solution)/shard_map/dot_general | solution.py:449
  204.1 0.0 copy-done.12
  204.1 0.0 copy-start.3
  204.1 2.9 fusion.30.down_grad
  207.0 0.0 copy-done.3
  207.0 0.0 copy-start.1
  207.0 5.1 %add_convert_fusion = (bf16[1024,384]{0,1:T(8,128)(2,1)S(1)}, f32[1024,384]{0,1:T(8,128)S(1)}) fusion(f32[1024,384]{0,1:T(8,128)S(1)} %get-tuple-element.99, bf16[1024,1536]{1,0:T(8,128)(2,1)S(1)} %bitcast.114, bf16[384,1536]{1,0:T(8,128)(2,1)S(1)} %bitcast.106), kind=kOutput, calls=%fused_computation.27 | convolution fusion | flops 1236271104 | bytes 8257536 | tf_op jit(solution)/shard_map/dot_general | solution.py:459
  212.1 0.0 copy-done.1
  212.1 2.9 convolution_convert_fusion.2
  215.0 3.6 convolution_convert_fusion
  218.6 3.5 convolution_convert_fusion.1
  222.1 40.6 %scatter.1.normed_grad_ref = f32[64,1536]{1,0:T(8,128)} custom-call(bf16[4,4,64,1536]{3,2,1,0:T(8,128)(2,1)} %bitcast.105), custom_call_target="tpu_custom_call" | custom-call | tf_op jit(solution)/shard_map/scatter/pallas_call | solution.py:429
  262.7 1.2 slice.28
  264.6 5.6 %unsettle.1 = (f32[64,1536]{1,0:T(8,128)}, bf16[64,1536]{1,0:T(8,128)(2,1)}, f32[1,1536]{1,0:T(1,128)}, bf16[64,1536]{1,0:T(8,128)(2,1)}, f32[64,128]{1,0:T(8,128)}) custom-call(f32[64,1536]{1,0:T(8,128)} %scatter.1.normed_grad_ref, f32[64,1536]{1,0:T(8,128)} %get-tuple-element.58.middle_ref, f32[1,1536]{1,0:T(1,128)} %slice.27.gain_ref, ...), custom_call_target="tpu_custom_call" | custom-call | tf_op jit(solution)/shard_map/unsettle/pallas_call | solution.py:1928
  270.2 0.0 copy-start.11
  270.2 52.9 %turn_back.1 = (bf16[4,64,1536]{2,1,0:T(8,128)(2,1)}, f32[4,64,128]{2,1,0:T(8,128)}, f32[64,1536]{1,0:T(8,128)}, bf16[16,48,384]{2,1,0:T(8,128)(2,1)}, f32[192,1536]{1,0:T(8,128)}) custom-call(bf16[64,1536]{1,0:T(8,128)(2,1)} %get-tuple-element.66.grad.refs_9_, f32[64,128]{1,0:T(8,128)} %get-tuple-element.67.terms.refs_10_, ...), custom_call_target="tpu_custom_call" | custom-call | tf_op jit(solution)/shard_map/turn_back/pallas_call | solution.py:893
  323.1 0.0 copy-done.11
  323.1 0.1 fusion.24
  323.3 0.6 pad.14.refs_15_
  323.9 0.6 slice_convert_fusion.2.refs_21_
  324.5 107.9 %closing.1 = (f32[512,1536]{1,0:T(8,128)}, f32[64,1536]{1,0:T(8,128)}, f32[16,1536]{1,0:T(8,128)}, f32[48,1536]{1,0:T(8,128)}, f32[48,1536]{1,0:T(8,128)}, /*index=5*/f32[48,1536]{1,0:T(8,128)}, f32[48,1536]{1,0:T(8,128)}) custom-call(bf16[4,64,1536]{2,1,0:T(8,128)(2,1)} %get-tuple-element.69.refs_0_, bf16[4,64,1536]{2,1,0:T(8,128)(2,1)} %get-tuple-element.70.refs_1_, ...), custom_call_target="tpu_custom_call" | custom-call | tf_op jit(solution)/shard_map/closing/pallas_call | solution.py:1789
  432.4 1.4 constant_dynamic-slice_fusion
  433.8 1.4 dynamic-slice_bitcast_fusion
  435.2 0.0 copy-start.2
  435.2 1.2 convert_bitcast_fusion
  436.4 0.0 copy-start
  436.4 1.1 copy.38
  437.5 0.0 copy-done.2
  437.5 0.0 copy-done.6
  437.5 0.7 add_convert_fusion.1
  438.2 0.6 copy-done
  438.8 0.0 copy-start.5
  438.8 1.7 copy.46
  440.5 0.0 copy-done.5
  440.5 0.7 copy.47
  441.2 0.0 copy-done.10
  441.2 0.7 copy.48
  441.9 0.0 copy-done.9
  441.9 0.7 copy.49
  442.6 0.0 copy-done.8
  442.7 0.7 copy.50
  443.4 0.0 copy-done.7
  443.4 0.7 copy.51
  444.1 0.0 copy-done.4
  444.1 1.0 copy.52
  (9 shorter events, 0.0 us)
Async XLA Ops:
  156.2 41.5 %copy-start.13 = (bf16[32,48,384]{2,1,0:T(8,128)(2,1)S(1)}, bf16[32,48,384]{2,1,0:T(8,128)(2,1)}, u32[]{:S(2)}) copy-start(bf16[32,48,384]{2,1,0:T(8,128)(2,1)} %get-tuple-element.60) | copy-start | bytes 3538948
  197.7 6.4 %copy-start.12 = (bf16[16,64,1536]{2,1,0:T(8,128)(2,1)S(1)}, bf16[16,64,1536]{2,1,0:T(8,128)(2,1)}, u32[]{:S(2)}) copy-start(bf16[16,64,1536]{2,1,0:T(8,128)(2,1)} %get-tuple-element.61) | copy-start | bytes 9437188
  204.1 2.9 copy-start.3
  207.0 5.1 %copy-start.1 = (bf16[16,64,1536]{2,1,0:T(8,128)(2,1)S(1)}, bf16[16,64,1536]{2,1,0:T(8,128)(2,1)}, u32[]{:S(2)}) copy-start(bf16[16,64,1536]{2,1,0:T(8,128)(2,1)} %gather.1) | copy-start | bytes 9437188
  270.2 52.9 %copy-start.11 = (f32[16,1536]{1,0:T(8,128)S(1)}, f32[16,1536]{1,0:T(8,128)}, u32[]{:S(2)}) copy-start(f32[16,1536]{1,0:T(8,128)} %get-tuple-element.57.refs_16_) | copy-start | bytes 294916
  435.2 2.3 copy-start.2
  435.2 2.3 copy-start.6
  436.4 2.4 copy-start
  438.8 1.7 copy-start.5
  438.8 2.4 copy-start.10
  438.8 3.1 copy-start.9
  440.5 2.2 copy-start.8
  440.5 2.9 copy-start.7
  440.5 3.6 copy-start.4

commit v4 on v3

--- a/solution.py
+++ b/solution.py
@@ -244,29 +244,6 @@
 
 VMEM = pl.BlockSpec(memory_space=pltpu.VMEM)
 LEFT = pl.BlockSpec(memory_space=HBM)
-
-
-def gather_kernel(shard, out, send_sems, recv_sems, local_sem):
-    z, g, chip, core = here()
-    greet(line_of(z, g) + sides_of(z, g, False))
-    wires = Wires(send_sems, recv_sems)
-    copy = pltpu.make_async_copy(shard, out.at[4 * z + chip], local_sem)
-    copy.start()
-    spread_all([Spread(wires, shard, lambda zz, gg: out.at[zz * 4 + gg // 2], columns_half, False)])
-    copy.wait()
-    wires.drain()
-
-
-def gather(shard, ident):
-    return pl.pallas_call(
-        gather_kernel,
-        out_shape=jax.ShapeDtypeStruct((16,) + shard.shape, shard.dtype),
-        in_specs=[LEFT],
-        out_specs=LEFT,
-        scratch_shapes=[sems(spread_sems(False)), sems(spread_sems(False)), pltpu.SemaphoreType.DMA],
-        compiler_params=params(ident),
-        name="gather",
-    )(shard)
 
 
 class Exchange:
@@ -409,33 +386,79 @@
     return (1 if whole else 0) + 4 + 3
 
 
-def scatter_kernel(parts, out, send_sems, recv_sems, *scratch):
-    z, g, _, _ = here()
-    greet(line_of(z, g) + sides_of(z, g, False))
-    wires = Wires(send_sems, recv_sems)
-    flow = Fold(wires, parts, False, scratch, out)
-    flow.start()
-    flow.corner()
-    flow.side_x()
-    flow.side_y()
-    flow.line()
-    flow.finish()
-    wires.drain()
-
-
-def scatter(parts, ident):
-    rows, cols = parts.shape[-2:]
-    wires = fold_sems(False)
-    return pl.pallas_call(
-        scatter_kernel,
-        out_shape=jax.ShapeDtypeStruct((rows, cols), F32),
-        in_specs=[VMEM],
-        out_specs=VMEM,
-        scratch_shapes=[sems(wires), sems(wires)] + fold_scratch(rows, cols, False),
-        compiler_params=params(6),
-        name="scatter",
-        input_output_aliases={},
-    )(parts)
+class FoldSteps:
+    def __init__(self, wires, parts, scratch, out):
+        self.wires, self.parts, self.out = wires, parts, out
+        _, self.cx, self.cy, self.fx, self.fy, self.fz = scratch
+        self.z, self.g, self.chip, _ = here()
+        self.width = parts.shape[-1] // 2
+        self.base = wires.reserve(LINES)
+        low, high = (3 - self.z) // 3, self.z // 3
+        back = (0, 1 + 2 * low, 3 - low - high, 2 - low + high)
+        self.back = back
+        self.zs = [turn(self.z, LINES - k) if n else self.z for n, k in enumerate(back)]
+        self.to_x, self.to_y, self.by_x, self.by_y = {}, {}, {}, {}
+
+    def half(self, n, q, which):
+        return self.parts.at[self.zs[n], q, :, pl.ds(which * self.width, self.width)]
+
+    def corner(self, n):
+        far = along_y(along_x(self.g)) // 2
+        place = self.zs[n]
+        self.to_y[n] = self.wires.send(
+            self.half(n, far, 0), self.cy.at[place], (self.z, along_y(self.g))
+        )
+        self.to_x[n] = self.wires.send(
+            self.half(n, far, 1), self.cx.at[place], (self.z, along_x(self.g))
+        )
+
+    def side(self, n, gy, came, corner, which, target):
+        came.wait_recv()
+        q, place = gy // 2, self.zs[n]
+        cols = slice(which * self.width, (which + 1) * self.width)
+        self.parts[place, q, :, cols] = self.parts[place, q, :, cols] + corner[place]
+        return self.wires.send(self.parts.at[place, q], target.at[place], (self.z, gy))
+
+    def side_x(self, n):
+        self.by_x[n] = self.side(n, along_x(self.g), self.to_y[n], self.cy, 0, self.fx)
+
+    def side_y(self, n):
+        self.by_y[n] = self.side(n, along_y(self.g), self.to_x[n], self.cx, 1, self.fy)
+
+    def line(self, n):
+        self.by_x[n].wait_recv()
+        self.by_y[n].wait_recv()
+        place = self.zs[n]
+        found = (
+            self.parts[place, self.chip].astype(F32)
+            + self.fx[place].astype(F32)
+            + self.fy[place].astype(F32)
+        )
+        if n == 0:
+            self.out[...] = found
+            return
+        self.fx[place] = found.astype(BF16)
+        k = LINES - self.back[n]
+        copy = self.wires.copy(
+            self.fx.at[place],
+            self.fz.at[k - 1],
+            (place, self.g),
+            self.base + k,
+            self.base + k,
+        )
+        copy.start()
+        self.wires.sent.append((None, copy))
+
+    def finish(self):
+        for k in (1, 2, 3):
+            held = self.fz.at[k - 1]
+            self.wires.copy(held, held, (self.z, self.g), 0, self.base + k).wait_recv()
+        self.out[...] += (
+            self.fz[0].astype(F32) + self.fz[1].astype(F32) + self.fz[2].astype(F32)
+        )
+
+
+STEP_SEMS = 16 + LINES
 
 
 def layer_norm(row_block, gain_row):
@@ -779,141 +802,60 @@
 
 
 class GiveBack:
-    def __init__(self, wires, up_ref, down_ref, up_out, down_out, scratch, local_sems):
-        self.wires, self.up_out, self.down_out = wires, up_out, down_out
-        self.up_held, self.up_near, self.down_near = scratch
+    def __init__(self, wires, up_part, down_part, scratch, up_out, down_out):
+        self.wires, self.up_part, self.down_part = wires, up_part, down_part
+        self.up_out, self.down_out = up_out, down_out
+        self.up_near, self.down_near, self.up_got = scratch
         self.z, self.g, self.chip, self.core = here()
-        self.up_ref, self.down_ref = up_ref, down_ref
-        self.load_up = pltpu.make_async_copy(
-            up_ref.at[:, self.core], self.up_held, local_sems.at[0]
-        )
-        self.load_down = pltpu.make_async_copy(
-            down_ref.at[self.core], down_out, local_sems.at[1]
-        )
-
-    def start(self):
+        self.places = up_places(self.z, self.chip)
+
+    def first(self):
         near = (self.z, sibling(self.g))
-        self.load_up.start()
-        self.load_down.start()
-        self.up = self.wires.send(self.up_ref.at[:, 1 - self.core], self.up_near, near)
-        self.down = self.wires.send(self.down_ref.at[1 - self.core], self.down_near, near)
+        theirs = 1 - self.core
+        self.up = self.wires.send(self.up_part.at[:, :, theirs], self.up_near, near)
+        self.down = self.wires.send(self.down_part.at[theirs], self.down_near, near)
 
     def columns(self):
-        self.load_up.wait()
         self.up.wait_recv()
-        add_slots(self.up_held, self.up_near, 16)
-        here_chip = 4 * self.z + self.chip
+        core = self.core
+
+        @pl.loop(0, LINES)
+        def _(n):
+            for q in range(PLANE):
+                self.up_part[n, q, core] = self.up_part[n, q, core] + self.up_near[n, q]
+
         self.moved = []
-        for j, mate in enumerate(mates_of(self.z, self.chip, self.core)):
-            there = (here_chip + j + 1) % 16
+        for there, _ in self.places:
             self.moved.append(
-                self.wires.send(self.up_held.at[there], self.up_out.at[here_chip], mate)
+                self.wires.send(
+                    self.up_part.at[there[0], there[1], core],
+                    self.up_got.at[self.z, self.chip],
+                    (there[0], 2 * there[1] + core),
+                )
             )
-        self.up_out[here_chip] = self.up_held[here_chip]
+        self.up_got[self.z, self.chip] = self.up_part[self.z, self.chip, core]
 
     def rows(self):
-        self.load_down.wait()
         self.down.wait_recv()
         rows = self.down_out.shape[0] // 8
+        core = self.core
 
         @pl.loop(0, 8)
         def _(n):
             block = pl.ds(pl.multiple_of(n * rows, 8), rows)
-            self.down_out[block] = self.down_out[block] + self.down_near[block]
+            self.down_out[block] = self.down_part[core, block] + self.down_near[block]
 
     def finish(self):
         for copy in self.moved:
             copy.wait_recv()
-
-
-def turn_kernel(
-    grad,
-    terms,
-    down_part,
-    up_grad,
-    down_grad,
-    grad_out,
-    terms_out,
-    down_out,
-    up_grad_out,
-    down_grad_out,
-    send_sems,
-    recv_sems,
-    local_sems,
-    up_held,
-    up_near,
-    down_near,
-    down_held,
-    *fold,
-):
-    z, g, chip, core = here()
-    greet(mates_of(z, chip, core) + [(z, sibling(g))])
-    wires = Wires(send_sems, recv_sems)
-    lines = [
-        Line(wires, grad, lambda zz: grad_out.at[zz]),
-        Line(wires, terms, lambda zz: terms_out.at[zz]),
-    ]
-    back = GiveBack(
-        wires,
-        up_grad,
-        down_grad,
-        up_grad_out,
-        down_grad_out,
-        (up_held, up_near, down_near),
-        local_sems,
-    )
-    flow = Fold(wires, down_held, False, fold, down_out)
-    load = pltpu.make_async_copy(down_part, down_held, local_sems.at[2])
-    load.start()
-    for line in lines:
-        line.first()
-    back.start()
-    load.wait()
-    flow.corner()
-    grad_out[z] = grad[...]
-    terms_out[z] = terms[...]
-    back.columns()
-    flow.side_x()
-    flow.side_y()
-    for step in range(3):
-        for line in lines:
-            line.take(step)
-    back.rows()
-    flow.line()
-    flow.finish()
-    back.finish()
-    wires.drain()
-
-
-def turn_back(grad, terms, down_part, up_grad, down_grad):
-    rows, width = up_grad.shape[-2:]
-    down_shape = down_grad.shape[1:]
-    latent_rows, model_width = grad.shape
-    wires = 2 * LINE_SEMS + fold_sems(False) + 17
-    return pl.pallas_call(
-        turn_kernel,
-        out_shape=[
-            jax.ShapeDtypeStruct((LINES,) + grad.shape, BF16),
-            jax.ShapeDtypeStruct((LINES,) + terms.shape, F32),
-            jax.ShapeDtypeStruct(grad.shape, F32),
-            jax.ShapeDtypeStruct((16, rows, width), BF16),
-            jax.ShapeDtypeStruct(down_shape, F32),
-        ],
-        in_specs=[VMEM, VMEM, LEFT, LEFT, LEFT],
-        out_specs=[VMEM] * 5,
-        scratch_shapes=[
-            sems(wires),
-            sems(wires),
-            sems(3),
-            pltpu.VMEM((16, rows, width), BF16),
-            pltpu.VMEM((16, rows, width), BF16),
-            pltpu.VMEM(down_shape, F32),
-            pltpu.VMEM((LINES, PLANE, latent_rows, model_width), BF16),
-        ]
-        + fold_scratch(latent_rows, model_width, False),
-        compiler_params=params(2),
-        name="turn_back",
-    )(grad, terms, down_part, up_grad, down_grad)
+        width = self.up_got.shape[-1]
+        for n in range(LINES):
+            for q in range(PLANE):
+                first = (n * PLANE + q) * width
+                self.up_out[:, first : first + width] = self.up_got[n, q].astype(F32)
+
+
+GIVE_SEMS = 17
 
 
 class Total:
@@ -1821,6 +1763,7 @@
     sums_ref,
     middle_ref,
     normed_ref,
+    ready,
 ):
     rows, width = latents_ref.shape
     span = width // (H // GROUP)
@@ -1837,29 +1780,12 @@
         attention = weighted / spread_heads(stats, group * GROUP, masks)
         attention_ref[:, cols] = attention
         attn_ref[:, cols] = attention.astype(BF16)
+    ready()
     middle = latents_ref[...].astype(F32) + jnp.dot(
         attn_ref[...], out_ref[...], preferred_element_type=F32
     )
     middle_ref[...] = middle
     normed_ref[...] = layer_norm(middle, gain_ref[...]).astype(BF16)
-
-
-def settle(weighted, stats, own_weighted, own_stats, w_out, latents, gain):
-    vmem = pl.BlockSpec(memory_space=pltpu.VMEM)
-    shape = latents.shape
-    return pl.pallas_call(
-        settle_kernel,
-        out_shape=[
-            jax.ShapeDtypeStruct(shape, F32),
-            jax.ShapeDtypeStruct(shape, BF16),
-            jax.ShapeDtypeStruct(own_stats.shape, F32),
-            jax.ShapeDtypeStruct(shape, F32),
-            jax.ShapeDtypeStruct(shape, BF16),
-        ],
-        in_specs=[vmem] * 7,
-        out_specs=[vmem] * 5,
-        name="settle",
-    )(weighted, stats, own_weighted, own_stats, w_out, latents, gain)
 
 
 def norm_pull(rows, gain, grad):
@@ -1922,23 +1848,325 @@
     terms_ref[...] = terms
 
 
-def unsettle(normed_grad, middle, gain, cotangent, w_out, attention, stats, coef):
-    vmem = pl.BlockSpec(memory_space=pltpu.VMEM)
-    shape = middle.shape
+def gelu_parts(rows):
+    below = 0.5 * (1.0 + lax.erf(rows * (0.5**0.5)))
+    density = jnp.exp(-0.5 * rows * rows) * ((0.5 / jnp.pi) ** 0.5)
+    return rows * below, below + rows * density
+
+
+def middle_kernel(*refs):
+    (
+        weighted_ref,
+        stats_ref,
+        own_weighted_ref,
+        own_stats_ref,
+        out_weight_ref,
+        up_ref,
+        down_ref,
+        cot_rows_ref,
+        latents_ref,
+        gain_ref,
+        cot_ref,
+        coef_ref,
+        attn_out,
+        low_out,
+        middle_grad_out,
+        gain_grad_out,
+        weighted_grad_out,
+        terms_out,
+        grad_table_out,
+        terms_table_out,
+        new_latents_out,
+        up_grad_out,
+        down_grad_out,
+        send_sems,
+        recv_sems,
+        local_sems,
+        out_weight,
+        up_cols,
+        down_rows,
+        cot_rows,
+        ffn_rows,
+        attention,
+        sums,
+        middle,
+        normed,
+        hidden_grad,
+        up_grad,
+        hidden,
+        normed_part,
+        down_part,
+        up_grad_part,
+        down_grad_part,
+        up_near,
+        down_near,
+        up_got,
+        normed_grad,
+        down_sum,
+        attn_grad,
+        *fold,
+    ) = refs
+    z, g, chip, core = here()
+    rows, width = latents_ref.shape
+    span = up_cols.shape[1]
+    shard = width // 32
+    block_rows = PLANE * rows
+    near = (z, sibling(g))
+    greet([(there[0], 2 * there[1] + core) for there, _ in up_places(z, chip)] + [near])
+    wires = Wires(send_sems, recv_sems)
+    gather = Spread(
+        wires, normed, lambda zz, gg: ffn_rows.at[zz, gg // 2], columns_half, False
+    )
+    back = FoldSteps(wires, normed_part, fold[:FOLD], normed_grad)
+    down = Fold(wires, down_part, False, fold[FOLD:], down_sum)
+    give = GiveBack(
+        wires,
+        up_grad_part,
+        down_grad_part,
+        (up_near, down_near, up_got),
+        up_grad_out,
+        down_grad_out,
+    )
+    grad_line = Line(wires, weighted_grad_out, lambda zz: grad_table_out.at[zz])
+    terms_line = Line(wires, terms_out, lambda zz: terms_table_out.at[zz])
+    loads = [
+        pltpu.make_async_copy(source, target, local_sems.at[n])
+        for n, (source, target) in enumerate(
+            (
+                (out_weight_ref, out_weight),
+                (down_ref, down_rows),
+                (cot_rows_ref, cot_rows),
+                (up_ref, up_cols),
+            )
+        )
+    ]
+    for load in loads:
+        load.start()
+
+    def settle():
+        settle_kernel(
+            weighted_ref,
+            stats_ref,
+            own_weighted_ref,
+            own_stats_ref,
+            out_weight,
+            latents_ref,
+            gain_ref,
+            attention,
+            attn_out,
+            sums,
+            middle,
+            normed,
+            loads[0].wait,
+        )
+        ffn_rows[z, chip] = normed[...]
+
+    def hidden_back():
+        loads[1].wait()
+        loads[2].wait()
+        loads[3].wait()
+
+        @pl.loop(0, LINES)
+        def _(n):
+            block = cot_rows[n].reshape(block_rows, width)
+            hidden_grad[n] = dot_last(block, down_rows[...])
+
+    def group(n):
+        place = gather.zs[n]
+        block = ffn_rows[place].reshape(block_rows, width)
+        value, slope = gelu_parts(jnp.dot(block, up_cols[...], preferred_element_type=F32))
+        hidden[place] = value.astype(BF16)
+        grad = (hidden_grad[place] * slope).astype(BF16)
+        up_grad[place] = grad
+        part = dot_last(grad, up_cols[...]).astype(BF16)
+        normed_part[place] = part.reshape(PLANE, rows, width)
+
+    def down_product():
+        @pl.loop(0, LINES)
+        def _(n):
+            part = jnp.dot(hidden[n], down_rows[...], preferred_element_type=F32)
+            down_part[n] = part.astype(BF16).reshape(PLANE, rows, width)
+
+    def up_gradient():
+        grads = up_grad[...].reshape(LINES * block_rows, span)
+
+        @pl.loop(0, LINES)
+        def _(n):
+            cols = pl.ds(pl.multiple_of(n * span, 128), span)
+            block = ffn_rows[:, :, :, cols].reshape(LINES * block_rows, span)
+            part = dot_first(block, grads).astype(BF16)
+            up_grad_part[n] = part.reshape(PLANE, 2, shard, span)
+
+    def down_gradient():
+        rows_up = hidden[...].reshape(LINES * block_rows, span)
+
+        @pl.loop(0, width // span)
+        def _(n):
+            cols = pl.ds(pl.multiple_of(n * span, 128), span)
+            block = cot_rows[:, :, :, cols].reshape(LINES * block_rows, span)
+            part = dot_first(rows_up, block)
+            down_grad_part[:, :, cols] = part.reshape(2, span // 2, span)
+
+    def unsettle():
+        unsettle_kernel(
+            normed_grad,
+            middle,
+            gain_ref,
+            cot_ref,
+            out_weight,
+            attention,
+            sums,
+            coef_ref,
+            middle_grad_out,
+            low_out,
+            gain_grad_out,
+            weighted_grad_out,
+            terms_out,
+            attn_grad,
+        )
+        grad_table_out[z] = weighted_grad_out[...]
+        terms_table_out[z] = terms_out[...]
+
+    def new_rows():
+        new_latents_out[...] = (middle[...] + down_sum[...]).astype(BF16)
+
+    settle()
+    gather.first()
+    gather.column(0)
+    gather.column(1)
+    gather.corner_y(1)
+    gather.corner_y(0)
+    gather.corner_x(1)
+    hidden_back()
+    gather.corner_x(0)
+    gather.corner_x(2)
+    gather.corner_y(2)
+    gather.column(2)
+    gather.last(1)
+    gather.last(0)
+    group(0)
+    back.corner(0)
+    gather.last(2)
+    group(1)
+    gather.corner_x(3)
+    gather.corner_y(3)
+    group(2)
+    back.corner(2)
+    back.corner(1)
+    gather.last(3)
+    back.side_y(2)
+    back.side_x(2)
+    group(3)
+    back.corner(3)
+    back.side_y(1)
+    back.side_x(1)
+    down_gradient()
+    back.line(2)
+    back.side_x(3)
+    back.side_x(0)
+    back.side_y(3)
+    back.side_y(0)
+    back.line(1)
+    down_product()
+    down.start()
+    back.line(3)
+    down.corner()
+    up_gradient()
+    give.first()
+    give.columns()
+    back.line(0)
+    back.finish()
+    down.side_x()
+    down.side_y()
+    unsettle()
+    terms_line.first()
+    grad_line.first()
+    terms_line.take(0)
+    grad_line.take(0)
+    down.line()
+    give.rows()
+    give.finish()
+    terms_line.take(1)
+    grad_line.take(1)
+    grad_line.take(2)
+    terms_line.take(2)
+    down.finish()
+    new_rows()
+    wires.drain()
+
+
+def middle_part(
+    weighted, stats, own_weighted, own_stats, w_out, up_cols, down_rows, cot_rows, latents, gain, cot, coef
+):
+    rows, width = latents.shape
+    span = up_cols.shape[1]
+    shard = width // 32
+    plane = (LINES, PLANE, rows, width)
+    block = (LINES, PLANE * rows, span)
+    wires = spread_sems(False) + STEP_SEMS + fold_sems(False) + GIVE_SEMS + 2 * LINE_SEMS
+    own = (rows, width)
+    terms = own_stats.shape
+    bf = [
+        w_out.shape,
+        up_cols.shape,
+        down_rows.shape,
+        plane,
+        plane,
+    ]
+    scratch = [pltpu.VMEM(shape, BF16) for shape in bf] + [
+        pltpu.VMEM(own, F32),
+        pltpu.VMEM(terms, F32),
+        pltpu.VMEM(own, F32),
+        pltpu.VMEM(own, BF16),
+        pltpu.VMEM(block, F32),
+        pltpu.VMEM(block, BF16),
+        pltpu.VMEM(block, BF16),
+        pltpu.VMEM(plane, BF16),
+        pltpu.VMEM(plane, BF16),
+        pltpu.VMEM((LINES, PLANE, 2, shard, span), BF16),
+        pltpu.VMEM((2, span // 2, width), F32),
+        pltpu.VMEM((LINES, PLANE, shard, span), BF16),
+        pltpu.VMEM((span // 2, width), F32),
+        pltpu.VMEM((LINES, PLANE, shard, span), BF16),
+        pltpu.VMEM(own, F32),
+        pltpu.VMEM(own, F32),
+        pltpu.VMEM(own, F32),
+    ]
+    scratch += fold_scratch(rows, width, False) * 2
     return pl.pallas_call(
-        unsettle_kernel,
+        middle_kernel,
         out_shape=[
-            jax.ShapeDtypeStruct(shape, F32),
-            jax.ShapeDtypeStruct(shape, BF16),
-            jax.ShapeDtypeStruct((1, shape[1]), F32),
-            jax.ShapeDtypeStruct(shape, BF16),
-            jax.ShapeDtypeStruct(stats.shape, F32),
+            jax.ShapeDtypeStruct(own, BF16),
+            jax.ShapeDtypeStruct(own, BF16),
+            jax.ShapeDtypeStruct(own, F32),
+            jax.ShapeDtypeStruct((1, width), F32),
+            jax.ShapeDtypeStruct(own, BF16),
+            jax.ShapeDtypeStruct(terms, F32),
+            jax.ShapeDtypeStruct((LINES,) + own, BF16),
+            jax.ShapeDtypeStruct((LINES,) + terms, F32),
+            jax.ShapeDtypeStruct(own, BF16),
+            jax.ShapeDtypeStruct((shard, span * 16), F32),
+            jax.ShapeDtypeStruct((span // 2, width), F32),
         ],
-        in_specs=[vmem] * 7 + [pl.BlockSpec(memory_space=pltpu.SMEM)],
-        out_specs=[vmem] * 5,
-        scratch_shapes=[pltpu.VMEM(shape, F32)],
-        name="unsettle",
-    )(normed_grad, middle, gain, cotangent, w_out, attention, stats, coef)
+        in_specs=[VMEM] * 4 + [LEFT] * 4 + [VMEM] * 3 + [pl.BlockSpec(memory_space=pltpu.SMEM)],
+        out_specs=[VMEM] * 11,
+        scratch_shapes=[sems(wires), sems(wires), sems(4)] + scratch,
+        compiler_params=params(1),
+        name="middle",
+    )(
+        weighted,
+        stats,
+        own_weighted,
+        own_stats,
+        w_out,
+        up_cols,
+        down_rows,
+        cot_rows.reshape(plane),
+        latents,
+        gain,
+        cot,
+        coef,
+    )
 
 
 def per_device(
@@ -2027,40 +2255,32 @@
     down_rows = down_rows.reshape(-1, width)
     cot_rows = cot_rows.reshape(-1, width)
     time_rows = product(times[:frames, :8], full_time)
-    attention, attn_low, sums, middle, ffn_normed = settle(
-        got_weighted, got_stats, own_weighted, own_stats, full_out, latents, full_ffn_gain
-    )
-    ffn_rows = gather(ffn_normed, 5).reshape(-1, width)
-    up_rows = product(ffn_rows, up_cols)
-    hidden = jax.nn.gelu(up_rows, approximate=False).astype(BF16)
-    hidden_grad = inner_last(cot_rows, down_rows)
-    gelu_pull = jax.vjp(partial(jax.nn.gelu, approximate=False), up_rows)[1]
-    up_grad = gelu_pull(hidden_grad)[0].astype(BF16)
-    normed_part = inner_last(up_grad, up_cols).astype(BF16)
-    down_part = product(hidden, down_rows).astype(BF16)
-    shape = (LINES, PLANE, latent_rows, width)
-    ffn_normed_grad = scatter(normed_part.reshape(shape), 6)
-    up_grad_part = inner_first(ffn_rows, up_grad).astype(BF16)
-    down_grad_part = inner_first(hidden, cot_rows)
-    middle_grad, middle_low, grad_ffn_gain, weighted_grad, terms = unsettle(
-        ffn_normed_grad,
-        middle,
+    (
+        attn_low,
+        middle_low,
+        middle_grad,
+        grad_ffn_gain,
+        weighted_grad,
+        terms,
+        grad_table,
+        terms_table,
+        new_latents,
+        shard_up,
+        shard_down,
+    ) = middle_part(
+        got_weighted,
+        got_stats,
+        own_weighted,
+        own_stats,
+        full_out,
+        up_cols,
+        down_rows,
+        cot_rows,
+        latents,
         full_ffn_gain,
         cotangent,
-        full_out,
-        attention,
-        sums,
         coefficient.reshape(1, 1),
     )
-    grad_table, terms_table, down_sum, shard_up, shard_down = turn_back(
-        weighted_grad,
-        terms,
-        down_part.reshape(shape),
-        up_grad_part.reshape(16, 2, shard, -1),
-        down_grad_part.reshape(2, -1, width),
-    )
-    new_latents = (middle + down_sum).astype(BF16)
-    shard_up = jnp.swapaxes(shard_up, 0, 1).reshape(shard, -1).astype(F32)
     (
         media_grad,
         latents_grad,

time: 446 us -> 396 us (0.89)
  Pallas kernels: 395 us -> 368 us
  matrix products: 24.5 us -> 0.12 us
    pallas_call x5 -> x1, Pallas kernels: 145 us -> 121 us  [middle_part(): pl.pallas_call(middle_kernel, out_shape=[jax.ShapeDtypeStruct(own, BF16),...]
    dot_general x4 -> x0, matrix products: 14.4 us -> none  [the longest x2 8.63 us: inner_last(): lax.dot_general(left_side, right_side, (((1,), (1,)), ((), ())), preferre...]
    dot_general x3 -> x1, matrix products: 10.1 us -> 0.12 us  [product(): return jnp.dot(left_side, right_side, preferred_element_type=jnp.float32)]
    unnamed x35 -> x25, local copies, waits for them, and re-layouts: 6.91 us -> 11.1 us
where the time goes in v4:
time: 396 us; the launch traced here: 395 us
  Pallas kernels  368 us (93%)
  local copies, waits for them, and re-layouts  20.5 us (5%)
  other arithmetic  4.96 us (1%)
    pallas_call x1, Pallas kernels, opening(): pl.pallas_call(partial(opening_kernel, scale), out_shape=[jax.ShapeDtypeS...  141 us
    pallas_call x1, Pallas kernels, middle_part(): pl.pallas_call(middle_kernel, out_shape=[jax.ShapeDtypeStruct(own, BF16),...  121 us
    pallas_call x1, Pallas kernels, closing(): pl.pallas_call(partial(closing_kernel, scale), out_shape=[jax.ShapeDtypeS...  105 us
    unnamed x25, local copies, waits for them, and re-layouts  11.1 us

profile of v4, /device:TPU:0, one launch (start us, length us, event | category | flops | bytes accessed | tf_op | source)
XLA Modules:
  0.0 395.2 jit_solution(6200609651912935096)
XLA Ops:
  0.6 0.9 dynamic-slice_reduce_fusion
  1.5 0.2 reduce-window.8
  1.7 0.2 convert_reduce_fusion
  1.9 0.7 fusion.1.refs_12_.refs_20_
  2.5 0.7 bitcast_convert_fusion
  3.2 1.3 convert_reduce_fusion.1
  4.5 0.6 broadcast_in_dim.36
  5.2 0.7 bitcast_convert_fusion.2
  5.8 0.7 concatenate.3
  6.5 0.6 pad.12.refs_0_
  7.1 0.7 iota_compare_fusion.1
  7.9 0.6 pad.13.refs_11_
  8.4 141.5 %opening.1 = (f32[16,1536]{1,0:T(8,128)}, f32[8,128]{1,0:T(8,128)}, bf16[1536,1536]{1,0:T(8,128)(2,1)}, bf16[1536,1536]{1,0:T(8,128)(2,1)}, bf16[1536,1536]{1,0:...) custom-call(f32[16,128]{1,0:T(8,128)} %pad.12.refs_0_, ...), custom_call_target="tpu_custom_call" | custom-call | tf_op jit(solution)/shard_map/opening/pallas_call | solution.py:1333
  150.0 1.4 slice.27.refs_9_
  151.4 1.2 slice.28
  153.2 0.0 copy-start.7
  153.2 121.4 %middle.1 = (bf16[64,1536]{1,0:T(8,128)(2,1)}, bf16[64,1536]{1,0:T(8,128)(2,1)}, f32[64,1536]{1,0:T(8,128)}, f32[1,1536]{1,0:T(1,128)}, bf16[64,1536]{1,0:T(8,12...) custom-call(bf16[4,64,1536]{2,1,0:T(8,128)(2,1)} %get-tuple-element., ...), custom_call_target="tpu_custom_call" | custom-call | tf_op jit(solution)/shard_map/middle/pallas_call | solution.py:2136
  274.6 0.0 copy-done.7
  274.6 0.1 fusion
  274.8 0.6 pad.14.refs_15_
  275.4 0.6 slice_convert_fusion.2.refs_21_
  276.0 105.3 %closing.1 = (f32[512,1536]{1,0:T(8,128)}, f32[64,1536]{1,0:T(8,128)}, f32[16,1536]{1,0:T(8,128)}, f32[48,1536]{1,0:T(8,128)}, f32[48,1536]{1,0:T(8,128)}, /*index=5*/f32[48,1536]{1,0:T(8,128)}, f32[48,1536]{1,0:T(8,128)}) custom-call(bf16[4,64,1536]{2,1,0:T(8,128)(2,1)} %get-tuple-element.59.refs_0_, bf16[4,64,1536]{2,1,0:T(8,128)(2,1)} %get-tuple-element.60.refs_1_, ...), custom_call_target="tpu_custom_call" | custom-call | tf_op jit(solution)/shard_map/closing/pallas_call | solution.py:1731
  381.3 1.4 constant_dynamic-slice_fusion
  382.7 1.4 dynamic-slice_bitcast_fusion
  384.1 1.6 copy.38
  385.7 0.0 copy-start.2
  385.7 0.0 copy-start.6
  385.7 0.0 copy-start.5
  385.7 3.8 copy.39
  389.5 0.0 copy-done.2
  389.5 0.0 copy-start.4
  389.6 0.0 copy-start.3
  389.6 0.0 copy-start.1
  389.6 0.7 copy.40
  390.3 0.0 copy-done.6
  390.3 0.7 copy.41
  391.0 0.0 copy-done.5
  391.0 0.7 copy.42
  391.7 0.0 copy-done.4
  391.7 0.0 copy-start
  391.7 0.7 copy.43
  392.5 0.0 copy-done.3
  392.5 0.7 copy.44
  393.2 0.0 copy-done.1
  393.2 1.0 copy.45
  394.2 0.0 copy-done
  394.2 1.0 copy.46
  (3 shorter events, 0.0 us)
Async XLA Ops:
  153.2 121.4 %copy-start.7 = (f32[16,1536]{1,0:T(8,128)S(1)}, f32[16,1536]{1,0:T(8,128)}, u32[]{:S(2)}) copy-start(f32[16,1536]{1,0:T(8,128)} %get-tuple-element.56.refs_16_) | copy-start | bytes 294916
  385.7 3.8 copy-start.2
  385.7 4.6 %copy-start.6 = (f32[48,1536]{1,0:T(8,128)S(1)}, f32[48,1536]{1,0:T(8,128)}, u32[]{:S(2)}) copy-start(f32[48,1536]{1,0:T(8,128)} %get-tuple-element.110) | copy-start | bytes 884740
  385.7 5.3 %copy-start.5 = (f32[48,1536]{1,0:T(8,128)S(1)}, f32[48,1536]{1,0:T(8,128)}, u32[]{:S(2)}) copy-start(f32[48,1536]{1,0:T(8,128)} %get-tuple-element.111) | copy-start | bytes 884740
  389.5 2.2 copy-start.4
  389.6 2.9 copy-start.3
  389.6 3.6 copy-start.1
  391.7 2.5 copy-start
